TPU v7x, 32 devices: a whole 2x2x4 slice. The times are simulated.
32 devices in a mesh: dp: 16 (over z, y, x), tensor: 2 (over core).
Axes of the slice: x: 2, y: 2, z: 4, core: 2. Of those that a mesh axis runs over, the one named last changes fastest.
Arguments:
- tokens: bfloat16 [4, 16, 2048, 1024], P(None, 'dp', None, 'tensor'), may hold values from -40 to 40
- routed: int32 [4, 16, 256], P(None, 'dp'), may hold values from 0 to 2047, as said below
- w_query: bfloat16 [1024, 1024], P('dp', 'tensor'), may hold values from -0.1875 to 0.1875
- w_key: bfloat16 [1024, 1024], P('dp', 'tensor'), may hold values from -0.1875 to 0.1875
- w_value: bfloat16 [1024, 1024], P('dp', 'tensor'), may hold values from -0.1875 to 0.1875
- w_out: bfloat16 [1024, 1024], P('tensor', 'dp'), may hold values from -1 to 1
- w_up: bfloat16 [1024, 4096], P('dp', 'tensor'), may hold values from -0.1875 to 0.1875
- w_down: bfloat16 [4096, 1024], P('tensor', 'dp'), may hold values from -0.09375 to 0.09375
- w_route: bfloat16 [1024], P('dp'), may hold values from -0.09375 to 0.09375
- gain_attn: bfloat16 [1024], P('dp'), may hold values from 0.099609375 to 1.8984375
- gain_mlp: bfloat16 [1024], P('dp'), may hold values from 0.099609375 to 1.8984375
- cotangent: bfloat16 [4, 16, 2048, 1024], P(None, 'dp', None, 'tensor'), may hold values from -6 to 6
Outputs:
- output: bfloat16 [4, 16, 2048, 1024], P(None, 'dp', None, 'tensor')
- input_grad: bfloat16 [4, 16, 2048, 1024], P(None, 'dp', None, 'tensor')
- grad_query: float32 [1024, 1024], P('dp', 'tensor')
- grad_key: float32 [1024, 1024], P('dp', 'tensor')
- grad_value: float32 [1024, 1024], P('dp', 'tensor')
- grad_out: float32 [1024, 1024], P('tensor', 'dp')
- grad_up: float32 [1024, 4096], P('dp', 'tensor')
- grad_down: float32 [4096, 1024], P('tensor', 'dp')
- grad_route: float32 [1024], P('dp')
- grad_gain_attn: float32 [1024], P('dp')
- grad_gain_mlp: float32 [1024], P('dp')
Inputs may be any that keep to these rules, and one draw needn't show every extreme that they name: Each row of routed holds 256 different positions of its sequence in rising order.
All inputs are finite; a program needn't handle non-finite values.
Results may differ from a plain program's by a relative error of at most 0.02.
Values may be sent and summed in bfloat16 or wider, within the bound.
A program may use at most 192 MiB of HBM per device.

v0:
```python
import jax
import jax.numpy as jnp
from jax import lax
from jax.sharding import PartitionSpec as P

HD = 64


eps_norm = 1e-05


def rms_norm(values, gain):
    return values * lax.rsqrt(jnp.mean(values * values, -1, keepdims=True) + eps_norm) * gain


def dense(left, right):
    return jnp.dot(left, right, preferred_element_type=jnp.float32)


def shards(
    tokens,
    routed,
    w_query,
    w_key,
    w_value,
    w_out,
    w_up,
    w_down,
    w_route,
    gain_attn,
    gain_mlp,
    cotangent,
):
    half_width = tokens.shape[3]
    capacity = routed.shape[2]
    offset = lax.axis_index("tensor") * half_width
    width = half_width * lax.axis_size("tensor")
    score_scale = HD ** (-0.5)
    causal = lax.broadcasted_iota(jnp.int32, (capacity, capacity), 0) >= lax.broadcasted_iota(
        jnp.int32, (capacity, capacity), 1
    )

    def sequence_step(gradients, weight_rows, weight_cols, tok_seq, chosen, cot_seq):
        full_query, full_key, full_value, full_up, full_route, full_gain1, full_gain2 = weight_rows
        full_out, full_down = weight_cols
        g_query, g_key, g_value, g_up, g_route, g_gain1, g_gain2, g_out, g_down = gradients
        route_f32 = full_route.astype(jnp.float32)
        gain1_f32 = full_gain1.astype(jnp.float32)
        gain2_f32 = full_gain2.astype(jnp.float32)
        rows_half = jnp.take(tok_seq, chosen, axis=0)
        cot_half = jnp.take(cot_seq, chosen, axis=0)
        routed_rows, cot_rows = (
            lax.all_gather(rows_half, "tensor", axis=1, tiled=True),
            lax.all_gather(cot_half, "tensor", axis=1, tiled=True),
        )
        rows_f32 = routed_rows.astype(jnp.float32)
        rows_half_f32 = rows_half.astype(jnp.float32)
        cot_half_f32 = cot_half.astype(jnp.float32)
        route_logit = dense(routed_rows, full_route)
        route_gate = jax.nn.sigmoid(route_logit)
        normed = rms_norm(rows_f32, gain1_f32).astype(jnp.bfloat16)
        queries = dense(normed, full_query).astype(jnp.bfloat16).reshape(capacity, -1, HD)
        key_rows = dense(normed, full_key).astype(jnp.bfloat16).reshape(capacity, -1, HD)
        value_rows = dense(normed, full_value).astype(jnp.bfloat16).reshape(capacity, -1, HD)
        scores = (
            jnp.einsum("qhd,khd->hqk", queries, key_rows, preferred_element_type=jnp.float32)
            * score_scale
        )
        scores = jnp.where(causal[None], scores, -1e30)
        log_total = jax.nn.logsumexp(scores, axis=-1, keepdims=True)
        probs_low = jnp.exp(scores - log_total).astype(jnp.bfloat16)
        mixed_heads = jnp.einsum(
            "hqk,khd->qhd", probs_low, value_rows, preferred_element_type=jnp.float32
        )
        mixed_heads = mixed_heads.astype(jnp.bfloat16).reshape(capacity, -1)
        attended = lax.psum(dense(mixed_heads, full_out).astype(jnp.bfloat16), "tensor").astype(
            jnp.float32
        )
        hidden = rows_f32 + attended
        normed2 = rms_norm(hidden, gain2_f32).astype(jnp.bfloat16)
        up_proj = dense(normed2, full_up)
        activated = jax.nn.gelu(up_proj).astype(jnp.bfloat16)
        down_out = lax.psum(dense(activated, full_down).astype(jnp.bfloat16), "tensor").astype(
            jnp.float32
        )
        branch = attended + down_out
        branch_half = lax.dynamic_slice_in_dim(branch, offset, half_width, 1)
        d_logit = (
            jnp.sum(cot_rows.astype(jnp.float32) * branch, -1) * route_gate * (1.0 - route_gate)
        )
        new_rows = (rows_half_f32 + route_gate[:, None] * branch_half).astype(jnp.bfloat16)
        out_seq = tok_seq.at[chosen].set(new_rows)
        cot_f32 = cot_rows.astype(jnp.float32)
        d_branch = route_gate[:, None] * cot_f32
        d_down = d_branch.astype(jnp.bfloat16)
        up_again = dense(lax.optimization_barrier(normed2), full_up)
        act_again = jax.nn.gelu(up_again).astype(jnp.bfloat16)
        g_down = g_down + dense(act_again.T, d_down)
        d_act = dense(d_down, full_down.T)
        gelu_value, gelu_back = jax.vjp(jax.nn.gelu, up_again)
        d_upper = gelu_back(d_act)[0].astype(jnp.bfloat16)
        g_up = g_up + dense(normed2.T, d_upper)
        d_normed2 = lax.psum(dense(d_upper, full_up.T).astype(jnp.bfloat16), "tensor").astype(
            jnp.float32
        )
        norm2_value, norm2_back = jax.vjp(rms_norm, hidden, gain2_f32)
        d_hidden, d_gain2 = norm2_back(d_normed2)
        g_gain2 = g_gain2 + d_gain2
        d_attended = (d_branch + d_hidden).astype(jnp.bfloat16)
        g_out = g_out + dense(mixed_heads.T, d_attended)
        d_mixed = dense(d_attended, full_out.T).astype(jnp.bfloat16).reshape(capacity, -1, HD)
        scores_again = (
            jnp.einsum("qhd,khd->hqk", queries, key_rows, preferred_element_type=jnp.float32)
            * score_scale
        )
        scores_again = jnp.where(causal[None], scores_again, -1e30)
        attn_probs = jnp.exp(scores_again - log_total)
        probs_again = attn_probs.astype(jnp.bfloat16)
        d_values = jnp.einsum(
            "hqk,qhd->khd", probs_again, d_mixed, preferred_element_type=jnp.float32
        )
        d_values = d_values.astype(jnp.bfloat16).reshape(capacity, -1)
        d_probs = jnp.einsum(
            "qhd,khd->hqk", d_mixed, value_rows, preferred_element_type=jnp.float32
        )
        d_scores = attn_probs * (d_probs - jnp.sum(d_probs * attn_probs, -1, keepdims=True))
        d_scores = d_scores.astype(jnp.bfloat16)
        d_queries = (
            jnp.einsum("hqk,khd->qhd", d_scores, key_rows, preferred_element_type=jnp.float32)
            * score_scale
        )
        d_queries = d_queries.astype(jnp.bfloat16).reshape(capacity, -1)
        d_keys = (
            jnp.einsum("hqk,qhd->khd", d_scores, queries, preferred_element_type=jnp.float32)
            * score_scale
        )
        d_keys = d_keys.astype(jnp.bfloat16).reshape(capacity, -1)
        g_query = g_query + dense(normed.T, d_queries)
        g_key = g_key + dense(normed.T, d_keys)
        g_value = g_value + dense(normed.T, d_values)
        partial_normed = (
            dense(d_queries, full_query.T)
            + dense(d_keys, full_key.T)
            + dense(d_values, full_value.T)
        )
        d_hidden_half = lax.dynamic_slice_in_dim(d_hidden, offset, half_width, 1)
        route_half = lax.dynamic_slice_in_dim(route_f32, offset, half_width, 0)
        d_normed = lax.psum(partial_normed.astype(jnp.bfloat16), "tensor").astype(jnp.float32)
        norm1_value, norm1_back = jax.vjp(rms_norm, rows_f32, gain1_f32)
        d_rows_norm, d_gain1 = norm1_back(d_normed)
        g_gain1 = g_gain1 + d_gain1
        d_norm_half = lax.dynamic_slice_in_dim(d_rows_norm, offset, half_width, 1)
        g_route = g_route + jnp.dot(
            rows_f32.T, d_logit, precision=lax.Precision.HIGHEST, preferred_element_type=jnp.float32
        )
        d_half = d_hidden_half + d_norm_half + d_logit[:, None] * route_half[None, :]
        grad_rows_new = (cot_half_f32 + d_half).astype(jnp.bfloat16)
        grad_seq = cot_seq.at[chosen].set(grad_rows_new)
        new_gradients = (g_query, g_key, g_value, g_up, g_route, g_gain1, g_gain2, g_out, g_down)
        return (new_gradients, out_seq, grad_seq)

    def micro_step(gradients, micro_inputs):
        tok_micro, routed_micro, cot_micro = micro_inputs
        weight_rows = (
            lax.all_gather(w_query, "dp", axis=0, tiled=True),
            lax.all_gather(w_key, "dp", axis=0, tiled=True),
            lax.all_gather(w_value, "dp", axis=0, tiled=True),
            lax.all_gather(w_up, "dp", axis=0, tiled=True),
            lax.all_gather(w_route, "dp", axis=0, tiled=True),
            lax.all_gather(gain_attn, "dp", axis=0, tiled=True),
            lax.all_gather(gain_mlp, "dp", axis=0, tiled=True),
        )
        weight_cols = (
            lax.all_gather(w_out, "dp", axis=1, tiled=True),
            lax.all_gather(w_down, "dp", axis=1, tiled=True),
        )

        def sequence_scan(carried, seq_inputs):
            tok_seq, chosen, cot_seq = seq_inputs
            updated, out_seq, grad_seq = sequence_step(
                carried, weight_rows, weight_cols, tok_seq, chosen, cot_seq
            )
            return (updated, (out_seq, grad_seq))

        gradients, seq_results = lax.scan(
            sequence_scan, gradients, (tok_micro, routed_micro, cot_micro)
        )
        return (gradients, seq_results)

    zero_grads = (
        jnp.zeros((width, w_query.shape[1]), jnp.float32),
        jnp.zeros((width, w_key.shape[1]), jnp.float32),
        jnp.zeros((width, w_value.shape[1]), jnp.float32),
        jnp.zeros((width, w_up.shape[1]), jnp.float32),
        jnp.zeros((width,), jnp.float32),
        jnp.zeros((width,), jnp.float32),
        jnp.zeros((width,), jnp.float32),
        jnp.zeros((w_out.shape[0], width), jnp.float32),
        jnp.zeros((w_down.shape[0], width), jnp.float32),
    )
    totals, results = lax.scan(micro_step, zero_grads, (tokens, routed, cotangent))
    output, input_grad = results
    g_query, g_key, g_value, g_up, g_route, g_gain1, g_gain2, g_out, g_down = totals
    grad_query, grad_key, grad_value, grad_up, grad_route, grad_gain_attn, grad_gain_mlp = (
        lax.psum_scatter(g_query, "dp", scatter_dimension=0, tiled=True),
        lax.psum_scatter(g_key, "dp", scatter_dimension=0, tiled=True),
        lax.psum_scatter(g_value, "dp", scatter_dimension=0, tiled=True),
        lax.psum_scatter(g_up, "dp", scatter_dimension=0, tiled=True),
        lax.psum_scatter(g_route, "dp", scatter_dimension=0, tiled=True),
        lax.psum_scatter(g_gain1, "dp", scatter_dimension=0, tiled=True),
        lax.psum_scatter(g_gain2, "dp", scatter_dimension=0, tiled=True),
    )
    grad_out, grad_down = (
        lax.psum_scatter(g_out, "dp", scatter_dimension=1, tiled=True),
        lax.psum_scatter(g_down, "dp", scatter_dimension=1, tiled=True),
    )
    return (
        output,
        input_grad,
        grad_query,
        grad_key,
        grad_value,
        grad_out,
        grad_up,
        grad_down,
        grad_route,
        grad_gain_attn,
        grad_gain_mlp,
    )


def solution(mesh):
    placed = (
        P(None, "dp", None, "tensor"),
        P(None, "dp", None),
        P("dp", "tensor"),
        P("dp", "tensor"),
        P("dp", "tensor"),
        P("tensor", "dp"),
        P("dp", "tensor"),
        P("tensor", "dp"),
        P("dp"),
        P("dp"),
        P("dp"),
        P(None, "dp", None, "tensor"),
    )
    return jax.shard_map(
        shards,
        mesh=mesh,
        in_specs=placed,
        out_specs=(
            P(None, "dp", None, "tensor"),
            P(None, "dp", None, "tensor"),
            P("dp", "tensor"),
            P("dp", "tensor"),
            P("dp", "tensor"),
            P("tensor", "dp"),
            P("dp", "tensor"),
            P("tensor", "dp"),
            P("dp"),
            P("dp"),
            P("dp"),
        ),
        check_vma=False,
    )
```

profile of v0, /device:TPU:0, one launch (start us, length us, event | category | flops | bytes accessed | tf_op | source)
XLA Modules:
  0.0 2644.5 jit_solution(17404735948335513344)
XLA Ops:
  8.1 1941.5 %while.33 = (s32[]{:T(128)}, f32[1024,512]{1,0:T(8,128)}, f32[1024,512]{1,0:T(8,128)}, f32[1024,512]{1,0:T(8,128)}, f32[1024,2048]{1,0:T(8,128)}, /*index=5*/f32...) while((s32[]{:T(128)}, f32[1024,512]{1,0:T(8,128)}, ...), condition=%wide.region_17.19_spmd.clone, body=%wide.region_0.18_spmd.clone.sunk | while | flops 11211988992 | bytes 388675808 | solution.py:201
  25.8 44.1 %all-reduce.14 = (bf16[1024]{0:T(1024)(128)(2,1)S(1)}, bf16[1024]{0:T(1024)(128)(2,1)S(1)}, bf16[1024]{0:T(1024)(128)(2,1)S(1)}) all-reduce(bf16[1024]{0:T(1024)(128)(2,1)S(1)} %dynamic-update-slice.9, bf16[1024]{0:T(1024)(128)(2,1)S(1)} %dynamic-update-slice.10, ...), channel_id=1, replica_groups=mesh['dp'=16,'tensor'=2] {'dp'}, use_global_device_ids=true, to_apply=%add.1 | all-reduce | flops 3072 | bytes 12288 | tf_op jit(solution)/shard_map/while
  71.8 55.2 %all-gather.7.cloned.1.call-done = bf16[1024,512]{1,0:T(8,128)(2,1)} async-done(((bf16[64,512]{1,0:T(8,128)(2,1)}), bf16[1024,512]{1,0:T(8,128)(2,1)}) %all-gather.7.cloned.1.call-update) | async-done | bytes 1048592 | tf_op jit(solution)/shard_map/while/body/eval_jaxpr/all_gather | solution.py:166
  128.9 55.0 %all-gather.11.cloned.1.call-done = bf16[1024,512]{1,0:T(8,128)(2,1)} async-done(((bf16[64,512]{1,0:T(8,128)(2,1)}), bf16[1024,512]{1,0:T(8,128)(2,1)}) %all-gather.11.cloned.1.call-update) | async-done | bytes 1048592 | tf_op jit(solution)/shard_map/while/body/eval_jaxpr/all_gather | solution.py:167
  187.1 53.5 %all-gather.13.cloned.1.call-done = bf16[512,1024]{0,1:T(8,128)(2,1)} async-done(((bf16[512,64]{0,1:T(8,128)(2,1)}), bf16[512,1024]{0,1:T(8,128)(2,1)}) %all-gather.13.cloned.1.call-update) | async-done | bytes 1048592 | tf_op jit(solution)/shard_map/while/body/eval_jaxpr/all_gather | solution.py:174
  248.3 12.6 all-reduce.20.cloned.1.call-done
  264.3 77.0 %all-gather.15.cloned.1.call-done = bf16[1024,2048]{1,0:T(8,128)(2,1)} async-done(((bf16[64,2048]{1,0:T(8,128)(2,1)}), bf16[1024,2048]{1,0:T(8,128)(2,1)}) %all-gather.15.cloned.1.call-update) | async-done | bytes 4194320 | tf_op jit(solution)/shard_map/while/body/eval_jaxpr/all_gather | solution.py:168
  346.1 73.0 %all-gather.17.cloned.1.call-done = bf16[2048,1024]{0,1:T(8,128)(2,1)} async-done(((bf16[2048,64]{0,1:T(8,128)(2,1)}), bf16[2048,1024]{0,1:T(8,128)(2,1)}) %all-gather.17.cloned.1.call-update) | async-done | bytes 4194320 | tf_op jit(solution)/shard_map/while/body/eval_jaxpr/all_gather | solution.py:175
  479.8 7.4 all-reduce.24.cloned.1.call-done
  512.2 42.7 %all-reduce.14 = (bf16[1024]{0:T(1024)(128)(2,1)S(1)}, bf16[1024]{0:T(1024)(128)(2,1)S(1)}, bf16[1024]{0:T(1024)(128)(2,1)S(1)}) all-reduce(bf16[1024]{0:T(1024)(128)(2,1)S(1)} %dynamic-update-slice.9, bf16[1024]{0:T(1024)(128)(2,1)S(1)} %dynamic-update-slice.10, ...), channel_id=1, replica_groups=mesh['dp'=16,'tensor'=2] {'dp'}, use_global_device_ids=true, to_apply=%add.1 | all-reduce | flops 3072 | bytes 12288 | tf_op jit(solution)/shard_map/while
  556.8 54.9 %all-gather.7.cloned.1.call-done = bf16[1024,512]{1,0:T(8,128)(2,1)} async-done(((bf16[64,512]{1,0:T(8,128)(2,1)}), bf16[1024,512]{1,0:T(8,128)(2,1)}) %all-gather.7.cloned.1.call-update) | async-done | bytes 1048592 | tf_op jit(solution)/shard_map/while/body/eval_jaxpr/all_gather | solution.py:166
  613.6 54.9 %all-gather.11.cloned.1.call-done = bf16[1024,512]{1,0:T(8,128)(2,1)} async-done(((bf16[64,512]{1,0:T(8,128)(2,1)}), bf16[1024,512]{1,0:T(8,128)(2,1)}) %all-gather.11.cloned.1.call-update) | async-done | bytes 1048592 | tf_op jit(solution)/shard_map/while/body/eval_jaxpr/all_gather | solution.py:167
  671.6 53.7 %all-gather.13.cloned.1.call-done = bf16[512,1024]{0,1:T(8,128)(2,1)} async-done(((bf16[512,64]{0,1:T(8,128)(2,1)}), bf16[512,1024]{0,1:T(8,128)(2,1)}) %all-gather.13.cloned.1.call-update) | async-done | bytes 1048592 | tf_op jit(solution)/shard_map/while/body/eval_jaxpr/all_gather | solution.py:174
  732.9 12.8 all-reduce.20.cloned.1.call-done
  749.0 76.9 %all-gather.15.cloned.1.call-done = bf16[1024,2048]{1,0:T(8,128)(2,1)} async-done(((bf16[64,2048]{1,0:T(8,128)(2,1)}), bf16[1024,2048]{1,0:T(8,128)(2,1)}) %all-gather.15.cloned.1.call-update) | async-done | bytes 4194320 | tf_op jit(solution)/shard_map/while/body/eval_jaxpr/all_gather | solution.py:168
  830.8 72.8 %all-gather.17.cloned.1.call-done = bf16[2048,1024]{0,1:T(8,128)(2,1)} async-done(((bf16[2048,64]{0,1:T(8,128)(2,1)}), bf16[2048,1024]{0,1:T(8,128)(2,1)}) %all-gather.17.cloned.1.call-update) | async-done | bytes 4194320 | tf_op jit(solution)/shard_map/while/body/eval_jaxpr/all_gather | solution.py:175
  903.6 7.0 convolution_convert_fusion.24
  919.2 8.6 select_add_fusion.21
  927.7 8.6 select_add_fusion.26
  964.3 7.4 all-reduce.24.cloned.1.call-done
  996.9 42.8 %all-reduce.14 = (bf16[1024]{0:T(1024)(128)(2,1)S(1)}, bf16[1024]{0:T(1024)(128)(2,1)S(1)}, bf16[1024]{0:T(1024)(128)(2,1)S(1)}) all-reduce(bf16[1024]{0:T(1024)(128)(2,1)S(1)} %dynamic-update-slice.9, bf16[1024]{0:T(1024)(128)(2,1)S(1)} %dynamic-update-slice.10, ...), channel_id=1, replica_groups=mesh['dp'=16,'tensor'=2] {'dp'}, use_global_device_ids=true, to_apply=%add.1 | all-reduce | flops 3072 | bytes 12288 | tf_op jit(solution)/shard_map/while
  1041.6 54.8 %all-gather.7.cloned.1.call-done = bf16[1024,512]{1,0:T(8,128)(2,1)} async-done(((bf16[64,512]{1,0:T(8,128)(2,1)}), bf16[1024,512]{1,0:T(8,128)(2,1)}) %all-gather.7.cloned.1.call-update) | async-done | bytes 1048592 | tf_op jit(solution)/shard_map/while/body/eval_jaxpr/all_gather | solution.py:166
  1098.3 55.0 %all-gather.11.cloned.1.call-done = bf16[1024,512]{1,0:T(8,128)(2,1)} async-done(((bf16[64,512]{1,0:T(8,128)(2,1)}), bf16[1024,512]{1,0:T(8,128)(2,1)}) %all-gather.11.cloned.1.call-update) | async-done | bytes 1048592 | tf_op jit(solution)/shard_map/while/body/eval_jaxpr/all_gather | solution.py:167
  1156.5 53.7 %all-gather.13.cloned.1.call-done = bf16[512,1024]{0,1:T(8,128)(2,1)} async-done(((bf16[512,64]{0,1:T(8,128)(2,1)}), bf16[512,1024]{0,1:T(8,128)(2,1)}) %all-gather.13.cloned.1.call-update) | async-done | bytes 1048592 | tf_op jit(solution)/shard_map/while/body/eval_jaxpr/all_gather | solution.py:174
  1217.9 12.8 all-reduce.20.cloned.1.call-done
  1234.0 77.0 %all-gather.15.cloned.1.call-done = bf16[1024,2048]{1,0:T(8,128)(2,1)} async-done(((bf16[64,2048]{1,0:T(8,128)(2,1)}), bf16[1024,2048]{1,0:T(8,128)(2,1)}) %all-gather.15.cloned.1.call-update) | async-done | bytes 4194320 | tf_op jit(solution)/shard_map/while/body/eval_jaxpr/all_gather | solution.py:168
  1315.8 73.0 %all-gather.17.cloned.1.call-done = bf16[2048,1024]{0,1:T(8,128)(2,1)} async-done(((bf16[2048,64]{0,1:T(8,128)(2,1)}), bf16[2048,1024]{0,1:T(8,128)(2,1)}) %all-gather.17.cloned.1.call-update) | async-done | bytes 4194320 | tf_op jit(solution)/shard_map/while/body/eval_jaxpr/all_gather | solution.py:175
  1404.3 8.6 select_add_fusion.21
  1412.9 8.6 select_add_fusion.26
  1449.4 7.4 all-reduce.24.cloned.1.call-done
  1482.0 42.8 %all-reduce.14 = (bf16[1024]{0:T(1024)(128)(2,1)S(1)}, bf16[1024]{0:T(1024)(128)(2,1)S(1)}, bf16[1024]{0:T(1024)(128)(2,1)S(1)}) all-reduce(bf16[1024]{0:T(1024)(128)(2,1)S(1)} %dynamic-update-slice.9, bf16[1024]{0:T(1024)(128)(2,1)S(1)} %dynamic-update-slice.10, ...), channel_id=1, replica_groups=mesh['dp'=16,'tensor'=2] {'dp'}, use_global_device_ids=true, to_apply=%add.1 | all-reduce | flops 3072 | bytes 12288 | tf_op jit(solution)/shard_map/while
  1526.8 54.9 %all-gather.7.cloned.1.call-done = bf16[1024,512]{1,0:T(8,128)(2,1)} async-done(((bf16[64,512]{1,0:T(8,128)(2,1)}), bf16[1024,512]{1,0:T(8,128)(2,1)}) %all-gather.7.cloned.1.call-update) | async-done | bytes 1048592 | tf_op jit(solution)/shard_map/while/body/eval_jaxpr/all_gather | solution.py:166
  1583.6 54.8 %all-gather.11.cloned.1.call-done = bf16[1024,512]{1,0:T(8,128)(2,1)} async-done(((bf16[64,512]{1,0:T(8,128)(2,1)}), bf16[1024,512]{1,0:T(8,128)(2,1)}) %all-gather.11.cloned.1.call-update) | async-done | bytes 1048592 | tf_op jit(solution)/shard_map/while/body/eval_jaxpr/all_gather | solution.py:167
  1641.6 53.7 %all-gather.13.cloned.1.call-done = bf16[512,1024]{0,1:T(8,128)(2,1)} async-done(((bf16[512,64]{0,1:T(8,128)(2,1)}), bf16[512,1024]{0,1:T(8,128)(2,1)}) %all-gather.13.cloned.1.call-update) | async-done | bytes 1048592 | tf_op jit(solution)/shard_map/while/body/eval_jaxpr/all_gather | solution.py:174
  1703.0 12.8 all-reduce.20.cloned.1.call-done
  1719.1 76.9 %all-gather.15.cloned.1.call-done = bf16[1024,2048]{1,0:T(8,128)(2,1)} async-done(((bf16[64,2048]{1,0:T(8,128)(2,1)}), bf16[1024,2048]{1,0:T(8,128)(2,1)}) %all-gather.15.cloned.1.call-update) | async-done | bytes 4194320 | tf_op jit(solution)/shard_map/while/body/eval_jaxpr/all_gather | solution.py:168
  1801.0 73.0 %all-gather.17.cloned.1.call-done = bf16[2048,1024]{0,1:T(8,128)(2,1)} async-done(((bf16[2048,64]{0,1:T(8,128)(2,1)}), bf16[2048,1024]{0,1:T(8,128)(2,1)}) %all-gather.17.cloned.1.call-update) | async-done | bytes 4194320 | tf_op jit(solution)/shard_map/while/body/eval_jaxpr/all_gather | solution.py:175
  1874.0 7.0 convolution_convert_fusion.24
  1889.5 8.6 select_add_fusion.21
  1898.1 8.6 select_add_fusion.26
  1934.6 7.4 all-reduce.24.cloned.1.call-done
  1954.5 9.2 copy.56
  1965.7 77.2 %all-reduce.11 = (f32[1024]{0:T(1024)S(1)}, f32[1024]{0:T(1024)S(1)}, f32[1024]{0:T(1024)S(1)}) all-reduce(f32[1024]{0:T(1024)S(1)} %get-tuple-element.429, f32[1024]{0:T(1024)S(1)} %get-tuple-element.430, f32[1024]{0:T(1024)S(1)} %get-tuple-element.431), channel_id=8, replica_groups=mesh['dp'=16,'tensor'=2] {'dp'}, use_global_device_ids=true, to_apply=%region_24.26.clone | all-reduce | flops 3072 | bytes 24576
  2044.7 70.6 %reduce-scatter.11.cloned.1.call-done = f32[64,512]{1,0:T(8,128)} async-done(((f32[1024,512]{1,0:T(8,128)}), f32[64,512]{1,0:T(8,128)}) %reduce-scatter.11.cloned.1.call-update) | async-done | bytes 131088 | tf_op jit(solution)/shard_map/reduce_scatter | solution.py:207
  2115.3 80.4 %reduce-scatter.7.cloned.1.call-done = f32[64,512]{1,0:T(8,128)} async-done(((f32[1024,512]{1,0:T(8,128)}), f32[64,512]{1,0:T(8,128)}) %reduce-scatter.7.cloned.1.call-update) | async-done | bytes 131088 | tf_op jit(solution)/shard_map/reduce_scatter | solution.py:205
  2195.7 80.5 %reduce-scatter.9.cloned.1.call-done = f32[64,512]{1,0:T(8,128)} async-done(((f32[1024,512]{1,0:T(8,128)}), f32[64,512]{1,0:T(8,128)}) %reduce-scatter.9.cloned.1.call-update) | async-done | bytes 131088 | tf_op jit(solution)/shard_map/reduce_scatter | solution.py:206
  2276.2 178.1 %reduce-scatter.17.cloned.1.call-done = f32[2048,64]{0,1:T(8,128)} async-done(((f32[2048,1024]{0,1:T(8,128)}), f32[2048,64]{0,1:T(8,128)}) %reduce-scatter.17.cloned.1.call-update) | async-done | bytes 524304 | tf_op jit(solution)/shard_map/reduce_scatter | solution.py:215
  2454.3 183.1 %reduce-scatter.15.cloned.1.call-done = f32[64,2048]{1,0:T(8,128)} async-done(((f32[1024,2048]{1,0:T(8,128)}), f32[64,2048]{1,0:T(8,128)}) %reduce-scatter.15.cloned.1.call-update) | async-done | bytes 524304 | tf_op jit(solution)/shard_map/reduce_scatter | solution.py:208
  (735 shorter events, 371.3 us)
Async XLA Ops:
  8.1 61.8 %all-gather.9.cloned.1.call-start = ((), (), s32[]{:S(2)}) async-start(), calls=%async_computation.13 | async-start | bytes 1114112 | tf_op jit(solution)/shard_map/while/body/eval_jaxpr/all_gather | solution.py:165
  8.9 118.1 %all-gather.7.cloned.1.call-start = ((), (), s32[]{:S(2)}) async-start(), calls=%async_computation.12 | async-start | bytes 1114112 | tf_op jit(solution)/shard_map/while/body/eval_jaxpr/all_gather | solution.py:166
  9.6 174.3 %all-gather.11.cloned.1.call-start = ((), (), s32[]{:S(2)}) async-start(), calls=%async_computation.14 | async-start | bytes 1114112 | tf_op jit(solution)/shard_map/while/body/eval_jaxpr/all_gather | solution.py:167
  10.4 230.3 %all-gather.13.cloned.1.call-start = ((), (), s32[]{:S(2)}) async-start(), calls=%async_computation.15 | async-start | bytes 1114112 | tf_op jit(solution)/shard_map/while/body/eval_jaxpr/all_gather | solution.py:174
  10.9 250.0 %all-reduce.20.cloned.1.call-start = ((), (), s32[]{:S(2)}) async-start(), calls=%async_computation.16 | async-start | bytes 1048576 | tf_op jit(solution)/shard_map/while/body/eval_jaxpr/while/body/eval_jaxpr/psum | solution.py:76
  71.8 113.9 %copy-start.26 = (bf16[256,512]{0,1:T(8,128)(2,1)}, bf16[256,512]{0,1:T(8,128)(2,1)S(1)}, u32[]{:S(2)}) copy-start(bf16[256,512]{0,1:T(8,128)(2,1)S(1)} %copy.66) | copy-start | bytes 786436 | tf_op jit(solution)/shard_map/while
  128.9 57.4 %copy-start.28 = (bf16[256,512]{0,1:T(8,128)(2,1)}, bf16[256,512]{0,1:T(8,128)(2,1)S(1)}, u32[]{:S(2)}) copy-start(bf16[256,512]{0,1:T(8,128)(2,1)S(1)} %copy.65) | copy-start | bytes 786436 | tf_op jit(solution)/shard_map/while
  243.1 98.1 %all-gather.15.cloned.1.call-start = ((), (), s32[]{:S(2)}) async-start(), calls=%async_computation.17 | async-start | bytes 4456448 | tf_op jit(solution)/shard_map/while/body/eval_jaxpr/all_gather | solution.py:168
  243.7 175.4 %all-gather.17.cloned.1.call-start = ((), (), s32[]{:S(2)}) async-start(), calls=%async_computation.18 | async-start | bytes 4456448 | tf_op jit(solution)/shard_map/while/body/eval_jaxpr/all_gather | solution.py:175
  244.5 208.5 %all-reduce.22.cloned.1.call-start = ((), (), s32[]{:S(2)}) async-start(), calls=%async_computation.19 | async-start | bytes 2097152 | tf_op jit(solution)/shard_map/while/body/eval_jaxpr/while/body/eval_jaxpr/psum | solution.py:103
  434.6 52.6 %all-reduce.24.cloned.1.call-start = ((), (), s32[]{:S(2)}) async-start(), calls=%async_computation.20 | async-start | bytes 1048576 | tf_op jit(solution)/shard_map/while/body/eval_jaxpr/while/body/eval_jaxpr/psum | solution.py:148
  494.7 60.2 %all-gather.9.cloned.1.call-start = ((), (), s32[]{:S(2)}) async-start(), calls=%async_computation.13 | async-start | bytes 1114112 | tf_op jit(solution)/shard_map/while/body/eval_jaxpr/all_gather | solution.py:165
  495.3 116.4 %all-gather.7.cloned.1.call-start = ((), (), s32[]{:S(2)}) async-start(), calls=%async_computation.12 | async-start | bytes 1114112 | tf_op jit(solution)/shard_map/while/body/eval_jaxpr/all_gather | solution.py:166
  496.0 172.4 %all-gather.11.cloned.1.call-start = ((), (), s32[]{:S(2)}) async-start(), calls=%async_computation.14 | async-start | bytes 1114112 | tf_op jit(solution)/shard_map/while/body/eval_jaxpr/all_gather | solution.py:167
  496.6 228.7 %all-gather.13.cloned.1.call-start = ((), (), s32[]{:S(2)}) async-start(), calls=%async_computation.15 | async-start | bytes 1114112 | tf_op jit(solution)/shard_map/while/body/eval_jaxpr/all_gather | solution.py:174
  497.4 248.3 %all-reduce.20.cloned.1.call-start = ((), (), s32[]{:S(2)}) async-start(), calls=%async_computation.16 | async-start | bytes 1048576 | tf_op jit(solution)/shard_map/while/body/eval_jaxpr/while/body/eval_jaxpr/psum | solution.py:76
  556.8 113.5 %copy-start.26 = (bf16[256,512]{0,1:T(8,128)(2,1)}, bf16[256,512]{0,1:T(8,128)(2,1)S(1)}, u32[]{:S(2)}) copy-start(bf16[256,512]{0,1:T(8,128)(2,1)S(1)} %copy.66) | copy-start | bytes 786436 | tf_op jit(solution)/shard_map/while
  727.8 98.1 %all-gather.15.cloned.1.call-start = ((), (), s32[]{:S(2)}) async-start(), calls=%async_computation.17 | async-start | bytes 4456448 | tf_op jit(solution)/shard_map/while/body/eval_jaxpr/all_gather | solution.py:168
  728.4 175.2 %all-gather.17.cloned.1.call-start = ((), (), s32[]{:S(2)}) async-start(), calls=%async_computation.18 | async-start | bytes 4456448 | tf_op jit(solution)/shard_map/while/body/eval_jaxpr/all_gather | solution.py:175
  729.0 208.5 %all-reduce.22.cloned.1.call-start = ((), (), s32[]{:S(2)}) async-start(), calls=%async_computation.19 | async-start | bytes 2097152 | tf_op jit(solution)/shard_map/while/body/eval_jaxpr/while/body/eval_jaxpr/psum | solution.py:103
  919.1 52.6 %all-reduce.24.cloned.1.call-start = ((), (), s32[]{:S(2)}) async-start(), calls=%async_computation.20 | async-start | bytes 1048576 | tf_op jit(solution)/shard_map/while/body/eval_jaxpr/while/body/eval_jaxpr/psum | solution.py:148
  979.3 60.5 %all-gather.9.cloned.1.call-start = ((), (), s32[]{:S(2)}) async-start(), calls=%async_computation.13 | async-start | bytes 1114112 | tf_op jit(solution)/shard_map/while/body/eval_jaxpr/all_gather | solution.py:165
  980.0 116.4 %all-gather.7.cloned.1.call-start = ((), (), s32[]{:S(2)}) async-start(), calls=%async_computation.12 | async-start | bytes 1114112 | tf_op jit(solution)/shard_map/while/body/eval_jaxpr/all_gather | solution.py:166
  980.6 172.7 %all-gather.11.cloned.1.call-start = ((), (), s32[]{:S(2)}) async-start(), calls=%async_computation.14 | async-start | bytes 1114112 | tf_op jit(solution)/shard_map/while/body/eval_jaxpr/all_gather | solution.py:167
  981.3 228.8 %all-gather.13.cloned.1.call-start = ((), (), s32[]{:S(2)}) async-start(), calls=%async_computation.15 | async-start | bytes 1114112 | tf_op jit(solution)/shard_map/while/body/eval_jaxpr/all_gather | solution.py:174
  982.1 248.6 %all-reduce.20.cloned.1.call-start = ((), (), s32[]{:S(2)}) async-start(), calls=%async_computation.16 | async-start | bytes 1048576 | tf_op jit(solution)/shard_map/while/body/eval_jaxpr/while/body/eval_jaxpr/psum | solution.py:76
  1041.6 113.5 %copy-start.26 = (bf16[256,512]{0,1:T(8,128)(2,1)}, bf16[256,512]{0,1:T(8,128)(2,1)S(1)}, u32[]{:S(2)}) copy-start(bf16[256,512]{0,1:T(8,128)(2,1)S(1)} %copy.66) | copy-start | bytes 786436 | tf_op jit(solution)/shard_map/while
  1098.3 57.4 %copy-start.28 = (bf16[256,512]{0,1:T(8,128)(2,1)}, bf16[256,512]{0,1:T(8,128)(2,1)S(1)}, u32[]{:S(2)}) copy-start(bf16[256,512]{0,1:T(8,128)(2,1)S(1)} %copy.65) | copy-start | bytes 786436 | tf_op jit(solution)/shard_map/while
  1212.7 98.3 %all-gather.15.cloned.1.call-start = ((), (), s32[]{:S(2)}) async-start(), calls=%async_computation.17 | async-start | bytes 4456448 | tf_op jit(solution)/shard_map/while/body/eval_jaxpr/all_gather | solution.py:168
  1213.3 175.5 %all-gather.17.cloned.1.call-start = ((), (), s32[]{:S(2)}) async-start(), calls=%async_computation.18 | async-start | bytes 4456448 | tf_op jit(solution)/shard_map/while/body/eval_jaxpr/all_gather | solution.py:175
  1214.0 208.7 %all-reduce.22.cloned.1.call-start = ((), (), s32[]{:S(2)}) async-start(), calls=%async_computation.19 | async-start | bytes 2097152 | tf_op jit(solution)/shard_map/while/body/eval_jaxpr/while/body/eval_jaxpr/psum | solution.py:103
  1404.2 52.6 %all-reduce.24.cloned.1.call-start = ((), (), s32[]{:S(2)}) async-start(), calls=%async_computation.20 | async-start | bytes 1048576 | tf_op jit(solution)/shard_map/while/body/eval_jaxpr/while/body/eval_jaxpr/psum | solution.py:148
  1464.4 60.5 %all-gather.9.cloned.1.call-start = ((), (), s32[]{:S(2)}) async-start(), calls=%async_computation.13 | async-start | bytes 1114112 | tf_op jit(solution)/shard_map/while/body/eval_jaxpr/all_gather | solution.py:165
  1465.1 116.6 %all-gather.7.cloned.1.call-start = ((), (), s32[]{:S(2)}) async-start(), calls=%async_computation.12 | async-start | bytes 1114112 | tf_op jit(solution)/shard_map/while/body/eval_jaxpr/all_gather | solution.py:166
  1465.9 172.6 %all-gather.11.cloned.1.call-start = ((), (), s32[]{:S(2)}) async-start(), calls=%async_computation.14 | async-start | bytes 1114112 | tf_op jit(solution)/shard_map/while/body/eval_jaxpr/all_gather | solution.py:167
  1466.5 228.9 %all-gather.13.cloned.1.call-start = ((), (), s32[]{:S(2)}) async-start(), calls=%async_computation.15 | async-start | bytes 1114112 | tf_op jit(solution)/shard_map/while/body/eval_jaxpr/all_gather | solution.py:174
  1467.2 248.6 %all-reduce.20.cloned.1.call-start = ((), (), s32[]{:S(2)}) async-start(), calls=%async_computation.16 | async-start | bytes 1048576 | tf_op jit(solution)/shard_map/while/body/eval_jaxpr/while/body/eval_jaxpr/psum | solution.py:76
  1526.8 113.5 %copy-start.26 = (bf16[256,512]{0,1:T(8,128)(2,1)}, bf16[256,512]{0,1:T(8,128)(2,1)S(1)}, u32[]{:S(2)}) copy-start(bf16[256,512]{0,1:T(8,128)(2,1)S(1)} %copy.66) | copy-start | bytes 786436 | tf_op jit(solution)/shard_map/while
  1697.9 98.2 %all-gather.15.cloned.1.call-start = ((), (), s32[]{:S(2)}) async-start(), calls=%async_computation.17 | async-start | bytes 4456448 | tf_op jit(solution)/shard_map/while/body/eval_jaxpr/all_gather | solution.py:168
  1698.4 175.5 %all-gather.17.cloned.1.call-start = ((), (), s32[]{:S(2)}) async-start(), calls=%async_computation.18 | async-start | bytes 4456448 | tf_op jit(solution)/shard_map/while/body/eval_jaxpr/all_gather | solution.py:175
  1699.2 208.7 %all-reduce.22.cloned.1.call-start = ((), (), s32[]{:S(2)}) async-start(), calls=%async_computation.19 | async-start | bytes 2097152 | tf_op jit(solution)/shard_map/while/body/eval_jaxpr/while/body/eval_jaxpr/psum | solution.py:103
  1889.4 52.6 %all-reduce.24.cloned.1.call-start = ((), (), s32[]{:S(2)}) async-start(), calls=%async_computation.20 | async-start | bytes 1048576 | tf_op jit(solution)/shard_map/while/body/eval_jaxpr/while/body/eval_jaxpr/psum | solution.py:148
  1949.6 95.1 %reduce-scatter.13.cloned.1.call-start = ((), (), s32[]{:S(2)}) async-start(), calls=%async_computation.9 | async-start | bytes 2228224 | tf_op jit(solution)/shard_map/reduce_scatter | solution.py:214
  1952.5 162.7 %reduce-scatter.11.cloned.1.call-start = ((), (), s32[]{:S(2)}) async-start(), calls=%async_computation.8 | async-start | bytes 2228224 | tf_op jit(solution)/shard_map/reduce_scatter | solution.py:207
  1953.1 242.5 %reduce-scatter.7.cloned.1.call-start = ((), (), s32[]{:S(2)}) async-start(), calls=%async_computation.6 | async-start | bytes 2228224 | tf_op jit(solution)/shard_map/reduce_scatter | solution.py:205
  1953.7 322.5 %reduce-scatter.9.cloned.1.call-start = ((), (), s32[]{:S(2)}) async-start(), calls=%async_computation.7 | async-start | bytes 2228224 | tf_op jit(solution)/shard_map/reduce_scatter | solution.py:206
  1954.4 499.9 %reduce-scatter.17.cloned.1.call-start = ((), (), s32[]{:S(2)}) async-start(), calls=%async_computation.11 | async-start | bytes 8912896 | tf_op jit(solution)/shard_map/reduce_scatter | solution.py:215
  1963.7 673.7 %reduce-scatter.15.cloned.1.call-start = ((), (), s32[]{:S(2)}) async-start(), calls=%async_computation.10 | async-start | bytes 8912896 | tf_op jit(solution)/shard_map/reduce_scatter | solution.py:208
  (159 other events, 614.6 us)
Sparse Core Ops, SparseCore 0:
  11.7 58.1 all-gather.8
  72.7 54.2 all-gather.6
  129.8 54.0 all-gather.10
  186.5 54.0 all-gather.12
  243.4 17.5 all-reduce.19
  263.9 77.2 all-gather.14
  344.4 74.6 all-gather.16
  434.7 18.2 all-reduce.21
  467.2 19.8 all-reduce.23
  498.0 56.6 all-gather.8
  557.4 54.2 all-gather.6
  614.3 54.0 all-gather.10
  671.2 54.0 all-gather.12
  728.1 17.5 all-reduce.19
  748.6 77.2 all-gather.14
  828.9 74.6 all-gather.16
  919.2 18.2 all-reduce.21
  951.7 19.9 all-reduce.23
  982.8 56.6 all-gather.8
  1042.1 54.2 all-gather.6
  1099.2 54.0 all-gather.10
  1156.0 54.0 all-gather.12
  1213.1 17.5 all-reduce.19
  1233.6 77.2 all-gather.14
  1314.1 74.6 all-gather.16
  1404.4 18.2 all-reduce.21
  1436.9 19.8 all-reduce.23
  1468.0 56.6 all-gather.8
  1527.4 54.2 all-gather.6
  1584.3 54.0 all-gather.10
  1641.2 54.0 all-gather.12
  1698.2 17.5 all-reduce.19
  1718.8 77.2 all-gather.14
  1799.2 74.6 all-gather.16
  1889.5 18.2 all-reduce.21
  1922.0 19.9 all-reduce.23
Sparse Core Ops, SparseCore 1:
  1952.9 81.5 reduce-scatter.12
  2037.2 78.0 reduce-scatter.10
  2118.0 77.6 reduce-scatter.6
  2198.5 77.6 reduce-scatter.8
  2279.1 175.2 reduce-scatter.16
  2457.2 180.1 reduce-scatter.14
where the time goes:
time: 2650 us; the launch traced here: 2640 us
  waiting for transfers between devices  1950 us (74%)
  blocking collectives  268 us (10%)
  matrix products  212 us (8%)
  local copies, waits for them, and re-layouts  102 us (4%)
  other arithmetic  83.7 us (3%)
    all_gather x4, waiting for transfers between devices, micro_step(): lax.all_gather(w_up, 'dp', axis=0, tiled=True)  308 us
    all_gather x4, waiting for transfers between devices, micro_step(): lax.all_gather(w_down, 'dp', axis=1, tiled=True)  292 us
    all_gather x4, waiting for transfers between devices, micro_step(): lax.all_gather(w_key, 'dp', axis=0, tiled=True)  220 us
    all_gather x4, waiting for transfers between devices, micro_step(): lax.all_gather(w_value, 'dp', axis=0, tiled=True)  220 us
    all_gather x4, waiting for transfers between devices, micro_step(): lax.all_gather(w_out, 'dp', axis=1, tiled=True)  215 us
    dot_general x76, matrix products, dense(): return jnp.dot(left, right, preferred_element_type=jnp.float32)  200 us
    reduce_scatter x1, waiting for transfers between devices, shards(): lax.psum_scatter(g_up, 'dp', scatter_dimension=0, tiled=True)  183 us
    reduce_scatter x1, waiting for transfers between devices, shards(): lax.psum_scatter(g_down, 'dp', scatter_dimension=1, tiled=True)  178 us
  transfers between devices with their start and end apart: 42, of which 37 were waited for; matrix products, arithmetic and copies ran while one was open for 8% of the time, Pallas kernels for 0%

commit v1 on v0

v1 whole, which is shorter than its diff:
```python
import jax
import jax.numpy as jnp
from jax import lax
from jax.sharding import PartitionSpec as P

HD = 64
eps_norm = 1e-05


def dense(left, right):
    return jnp.dot(left, right, preferred_element_type=jnp.float32)


def dense_t(left, right):
    return lax.dot_general(
        left, right, (((1,), (1,)), ((), ())), preferred_element_type=jnp.float32
    )


def dense_g(left, right):
    return lax.dot_general(
        left, right, (((0,), (0,)), ((), ())), preferred_element_type=jnp.float32
    )


def rms_back(values, inv, gain, grad):
    grad_gain = jnp.sum(grad * values * inv, 0)
    scaled = grad * gain
    dot = jnp.mean(scaled * values, -1, keepdims=True)
    return inv * scaled - values * (inv * inv * inv) * dot, grad_gain


def shards(
    tokens,
    routed,
    w_query,
    w_key,
    w_value,
    w_out,
    w_up,
    w_down,
    w_route,
    gain_attn,
    gain_mlp,
    cotangent,
):
    micro, seqs, length, half_width = tokens.shape
    capacity = routed.shape[2]
    batch = micro * seqs
    total = batch * capacity
    cols = w_query.shape[1]
    hidden_cols = w_up.shape[1]
    width = half_width * lax.axis_size("tensor")
    offset = lax.axis_index("tensor") * half_width
    scale = HD ** (-0.5)
    swap = [(0, 1), (1, 0)]

    vec = jnp.stack([w_route, gain_attn, gain_mlp], 1)
    vec = jnp.pad(vec, ((0, 0), (0, 125)))
    packed = jnp.concatenate([w_query, w_key, w_value, w_up, w_out.T, w_down.T, vec], 1)
    gathered = lax.all_gather(packed, "dp", axis=0, tiled=True)
    b1, b2, b3 = cols, 2 * cols, 3 * cols
    b4 = b3 + hidden_cols
    b5 = b4 + w_out.shape[0]
    b6 = b5 + w_down.shape[0]
    fq = gathered[:, :b1]
    fk = gathered[:, b1:b2]
    fv = gathered[:, b2:b3]
    fup = gathered[:, b3:b4]
    foutT = gathered[:, b4:b5]
    fdownT = gathered[:, b5:b6]
    route = gathered[:, b6]
    route_f32 = route.astype(jnp.float32)
    gain1 = gathered[:, b6 + 1].astype(jnp.float32)
    gain2 = gathered[:, b6 + 2].astype(jnp.float32)

    tok = tokens.reshape(batch, length, half_width)
    cot = cotangent.reshape(batch, length, half_width)
    chosen = routed.reshape(batch, capacity)
    rows_half = jnp.take_along_axis(tok, chosen[:, :, None], axis=1).reshape(total, half_width)
    cot_half = jnp.take_along_axis(cot, chosen[:, :, None], axis=1).reshape(total, half_width)
    rows = lax.all_gather(rows_half, "tensor", axis=1, tiled=True)
    cot_rows = lax.all_gather(cot_half, "tensor", axis=1, tiled=True)

    rows_f = rows.astype(jnp.float32)
    cot_f = cot_rows.astype(jnp.float32)
    gate = jax.nn.sigmoid(dense(rows, route))
    inv1 = lax.rsqrt(jnp.mean(rows_f * rows_f, -1, keepdims=True) + eps_norm)
    normed = (rows_f * inv1 * gain1).astype(jnp.bfloat16)
    heads = cols // HD

    def split(x):
        return x.astype(jnp.bfloat16).reshape(batch, capacity, heads, HD).transpose(0, 2, 1, 3)

    def join(x):
        return x.transpose(0, 2, 1, 3).reshape(total, cols)

    q = split(dense(normed, fq))
    k = split(dense(normed, fk))
    v = split(dense(normed, fv))
    causal = lax.broadcasted_iota(jnp.int32, (capacity, capacity), 0) >= lax.broadcasted_iota(
        jnp.int32, (capacity, capacity), 1
    )
    scores = jnp.einsum("bhqd,bhkd->bhqk", q, k, preferred_element_type=jnp.float32) * scale
    scores = jnp.where(causal, scores, -1e30)
    peak = jnp.max(scores, -1, keepdims=True)
    expd = jnp.exp(scores - peak)
    probs = expd / jnp.sum(expd, -1, keepdims=True)
    probs_low = probs.astype(jnp.bfloat16)
    mixed = jnp.einsum("bhqk,bhkd->bhqd", probs_low, v, preferred_element_type=jnp.float32)
    mixed = join(mixed.astype(jnp.bfloat16))

    def pair_sum(x):
        low = x.astype(jnp.bfloat16)
        other = lax.ppermute(low, "tensor", swap)
        return low.astype(jnp.float32) + other.astype(jnp.float32)

    attended = pair_sum(dense_t(mixed, foutT))
    hidden = rows_f + attended
    inv2 = lax.rsqrt(jnp.mean(hidden * hidden, -1, keepdims=True) + eps_norm)
    normed2 = (hidden * inv2 * gain2).astype(jnp.bfloat16)
    up = dense(normed2, fup)
    act32, gelu_back = jax.vjp(jax.nn.gelu, up)
    act = act32.astype(jnp.bfloat16)
    down = pair_sum(dense_t(act, fdownT))
    branch = attended + down
    d_logit = jnp.sum(cot_f * branch, -1) * gate * (1.0 - gate)
    branch_half = lax.dynamic_slice_in_dim(branch, offset, half_width, 1)
    new_rows = (rows_half.astype(jnp.float32) + gate[:, None] * branch_half).astype(jnp.bfloat16)

    d_branch = gate[:, None] * cot_f
    d_down = d_branch.astype(jnp.bfloat16)
    g_downT = dense_g(d_down, act)
    d_act = dense(d_down, fdownT)
    d_upper = gelu_back(d_act)[0].astype(jnp.bfloat16)
    g_up = dense_g(normed2, d_upper)
    d_normed2 = pair_sum(dense_t(d_upper, fup))
    d_hidden, g_gain2 = rms_back(hidden, inv2, gain2, d_normed2)
    d_attended = (d_branch + d_hidden).astype(jnp.bfloat16)
    g_outT = dense_g(d_attended, mixed)
    d_mixed = split(dense(d_attended, foutT))
    d_values = jnp.einsum("bhqk,bhqd->bhkd", probs_low, d_mixed, preferred_element_type=jnp.float32)
    d_values = join(d_values.astype(jnp.bfloat16))
    d_probs = jnp.einsum("bhqd,bhkd->bhqk", d_mixed, v, preferred_element_type=jnp.float32)
    d_scores = probs * (d_probs - jnp.sum(d_probs * probs, -1, keepdims=True))
    d_scores = d_scores.astype(jnp.bfloat16)
    d_q = jnp.einsum("bhqk,bhkd->bhqd", d_scores, k, preferred_element_type=jnp.float32) * scale
    d_k = jnp.einsum("bhqk,bhqd->bhkd", d_scores, q, preferred_element_type=jnp.float32) * scale
    d_q = join(d_q.astype(jnp.bfloat16))
    d_k = join(d_k.astype(jnp.bfloat16))
    g_q = dense_g(normed, d_q)
    g_k = dense_g(normed, d_k)
    g_v = dense_g(normed, d_values)
    d_normed = pair_sum(dense_t(d_q, fq) + dense_t(d_k, fk) + dense_t(d_values, fv))
    d_rows, g_gain1 = rms_back(rows_f, inv1, gain1, d_normed)
    g_route = jnp.sum(rows_f * d_logit[:, None], 0)
    d_half = (
        lax.dynamic_slice_in_dim(d_hidden + d_rows, offset, half_width, 1)
        + d_logit[:, None] * lax.dynamic_slice_in_dim(route_f32, offset, half_width, 0)[None, :]
    )
    grad_rows = (cot_half.astype(jnp.float32) + d_half).astype(jnp.bfloat16)

    seq_ids = lax.broadcasted_iota(jnp.int32, (batch, capacity), 0)
    output = tok.at[seq_ids, chosen].set(
        new_rows.reshape(batch, capacity, half_width), unique_indices=True
    )
    input_grad = cot.at[seq_ids, chosen].set(
        grad_rows.reshape(batch, capacity, half_width), unique_indices=True
    )

    g_vec = jnp.pad(jnp.stack([g_route, g_gain1, g_gain2], 1), ((0, 0), (0, 125)))
    grads = jnp.concatenate(
        [x.astype(jnp.bfloat16) for x in (g_q, g_k, g_v, g_up, g_outT, g_downT, g_vec)], 1
    )
    own = lax.psum_scatter(grads, "dp", scatter_dimension=0, tiled=True).astype(jnp.float32)
    return (
        output.reshape(tokens.shape),
        input_grad.reshape(tokens.shape),
        own[:, :b1],
        own[:, b1:b2],
        own[:, b2:b3],
        own[:, b4:b5].T,
        own[:, b3:b4],
        own[:, b5:b6].T,
        own[:, b6],
        own[:, b6 + 1],
        own[:, b6 + 2],
    )


def solution(mesh):
    rows = P("dp", "tensor")
    columns = P("tensor", "dp")
    vector = P("dp")
    stored = P(None, "dp", None, "tensor")
    return jax.shard_map(
        shards,
        mesh=mesh,
        in_specs=(
            stored,
            P(None, "dp", None),
            rows,
            rows,
            rows,
            columns,
            rows,
            columns,
            vector,
            vector,
            vector,
            stored,
        ),
        out_specs=(
            stored,
            stored,
            rows,
            rows,
            rows,
            columns,
            rows,
            columns,
            vector,
            vector,
            vector,
        ),
        check_vma=False,
    )
```

time: 2650 us -> 701 us (0.26)
  waiting for transfers between devices: 1950 us -> 401 us
  blocking collectives: 268 us -> 0 us
  matrix products: 212 us -> 106 us
  other arithmetic: 83.7 us -> 35.1 us
  local copies, waits for them, and re-layouts: 102 us -> 133 us
    all_gather x24 -> x3, waiting for transfers between devices: 1250 us -> 168 us  [the longest x1 156 us: shards(): gathered = lax.all_gather(packed, 'dp', axis=0, tiled=True)]
    reduce_scatter x6 -> x1, waiting for transfers between devices: 593 us -> 230 us  [shards(): lax.psum_scatter(grads, 'dp', scatter_dimension=0, tiled=True)]
    while x4 -> x0, blocking collectives: 172 us -> none
    dot_general x76 -> x7, matrix products: 200 us -> 36.8 us  [dense(): return jnp.dot(left, right, preferred_element_type=jnp.float32)]
    psum x12 -> x0, waiting for transfers between devices: 90.9 us -> none  [the longest x4 50.9 us: sequence_step(): lax.psum(dense(mixed_heads, full_out).astype(jnp.bfloat16), 'tensor')]
    unnamed x1 -> x0, blocking collectives: 77.2 us -> none
    unnamed x6 -> x102, local copies, waits for them, and re-layouts: 2.34 us -> 63.8 us
    dot_general x28 -> x18, matrix products: 12.2 us -> 69.5 us  [the longest x6 29.7 us: dense_t(): lax.dot_general(left, right, (((1,), (1,)), ((), ())), preferred_element_...]
  transfers between devices with their start and end apart: 42 -> 8, of which waited for: 37 -> 5; matrix products, arithmetic and copies ran while one was open for 8% -> 15% of each run, Pallas kernels for 0% -> 0%
where the time goes in v1:
time: 701 us; the launch traced here: 692 us
  waiting for transfers between devices  401 us (57%)
  local copies, waits for them, and re-layouts  133 us (19%)
  matrix products  106 us (15%)
  other arithmetic  35.1 us (5%)
  between operations  14.7 us (2%)
    reduce_scatter x1, waiting for transfers between devices, shards(): lax.psum_scatter(grads, 'dp', scatter_dimension=0, tiled=True)  230 us
    all_gather x1, waiting for transfers between devices, shards(): gathered = lax.all_gather(packed, 'dp', axis=0, tiled=True)  156 us
    unnamed x102, local copies, waits for them, and re-layouts  63.8 us
    dot_general x7, matrix products, dense(): return jnp.dot(left, right, preferred_element_type=jnp.float32)  36.8 us
    dot_general x6, matrix products, dense_t(): lax.dot_general(left, right, (((1,), (1,)), ((), ())), preferred_element_...  29.7 us
    dot_general x6, matrix products, dense_g(): lax.dot_general(left, right, (((0,), (0,)), ((), ())), preferred_element_...  27.3 us
    gather x2, local copies, waits for them, and re-layouts, shards(): jnp.take_along_axis(cot, chosen[:, :, None], axis=1)  20.9 us
    gather x2, local copies, waits for them, and re-layouts, shards(): jnp.take_along_axis(tok, chosen[:, :, None], axis=1)  14.9 us
  transfers between devices with their start and end apart: 8, of which 5 were waited for; matrix products, arithmetic and copies ran while one was open for 15% of the time, Pallas kernels for 0%

profile of v1, /device:TPU:0, one launch (start us, length us, event | category | flops | bytes accessed | tf_op | source)
XLA Modules:
  0.0 692.0 jit_solution(9246433559412853809)
XLA Ops:
  7.2 7.3 %copy.172 = bf16[4,1,2048,512]{3,2,1,0:T(8,128)(2,1)} copy(bf16[4,1,2048,512]{3,2,1,0:T(8,128)(2,1)} %param.14) | data formatting | bytes 16777216
  14.5 7.3 %copy.173 = bf16[4,1,2048,512]{3,2,1,0:T(8,128)(2,1)} copy(bf16[4,1,2048,512]{3,2,1,0:T(8,128)(2,1)} %param.25) | data formatting | bytes 16777216
  21.9 14.2 %gather_fusion = bf16[1024,512]{1,0:T(8,128)(2,1)S(1)} fusion(bf16[4,2048,512]{2,1,0:T(8,128)(2,1)} %bitcast.104, s32[1024]{0:T(1024)S(1)} %bitcast.99), kind=kCustom, calls=%fused_computation.clone | custom fusion | bytes 2105344 | tf_op jit(solution)/shard_map/jit(take_along_axis)/gather | solution.py:80
  36.9 19.3 %gather_fusion.1 = bf16[1024,512]{1,0:T(8,128)(2,1)} fusion(bf16[4,2048,512]{2,1,0:T(8,128)(2,1)} %bitcast.101, s32[1024]{0:T(1024)S(1)} %bitcast.100), kind=kCustom, calls=%fused_computation.1.clone | custom fusion | bytes 2105344 | tf_op jit(solution)/shard_map/jit(take_along_axis)/gather | solution.py:81
  57.9 1.9 broadcast_select_fusion.1
  62.7 11.9 %all-gather.4.cloned.1.call-done = bf16[1024,1024]{0,1:T(8,128)(2,1)} async-done(((bf16[1024,512]{0,1:T(8,128)(2,1)}), bf16[1024,1024]{0,1:T(8,128)(2,1)}) %all-gather.4.cloned.1.call-update) | async-done | bytes 2097168 | tf_op jit(solution)/shard_map/all_gather | solution.py:82
  74.5 2.1 fusion.13
  77.2 155.7 %all-gather.6.cloned.1.call-done = bf16[1024,6272]{1,0:T(8,128)(2,1)} async-done(((bf16[64,6272]{1,0:T(8,128)(2,1)}), bf16[1024,6272]{1,0:T(8,128)(2,1)}) %all-gather.6.cloned.1.call-update) | async-done | bytes 12845072 | tf_op jit(solution)/shard_map/all_gather | solution.py:61
  234.4 4.3 convolution_convert_fusion.6
  241.9 2.6 convolution_convert_fusion.7
  247.7 3.6 convolution_convert_fusion.8
  251.3 2.3 copy.82
  253.6 2.6 reshape.173
  256.2 2.5 fusion.83
  258.8 2.3 fusion.97
  261.9 2.4 copy-done.6
  265.4 4.2 convolution_convert_fusion
  274.1 4.1 multiply_reduce_fusion.3
  278.2 2.0 copy-done.1
  280.2 9.2 %fusion.33 = f32[1024,2048]{1,0:T(8,128)} fusion(bf16[1024,6272]{1,0:T(8,128)(2,1)} %all-gather.6.cloned.1.call-done, f32[1024,1024]{0,1:T(8,128)S(1)} %get-tuple-element.50, f32[1024]{0:T(1024)S(1)} %get-tuple-element.34, f32[1024]{0:T(1024)S(1)} %get-tuple-element.61), kind=kOutput, calls=%fused_computation.63 | convolution fusion | flops 4298113024 | bytes 16785408 | tf_op jit(solution)/shard_map/dot_general | solution.py:11
  289.4 13.2 %fusion.7 = bf16[1024,2048]{1,0:T(8,128)(2,1)S(1)} fusion(f32[1024,2048]{1,0:T(8,128)} %fusion.33, bf16[1024,6272]{1,0:T(8,128)(2,1)} %all-gather.6.cloned.1.call-done, bf16[1024,1024]{0,1:T(8,128)(2,1)} %all-gather.8.cloned.1.call-done, f32[1024]{0:T(1024)S(1)} %add_divide_fusion), kind=kOutput, calls=%fused_computation.13 | convolution fusion | flops 4340056064 | bytes 18878464 | tf_op jit(solution)/shard_map/dot_general | solution.py:11
  302.6 1.9 copy-done.35
  304.5 7.3 %fusion.44 = bf16[1024,1024]{0,1:T(8,128)(2,1)S(1)} fusion(bf16[1024,2048]{1,0:T(8,128)(2,1)S(1)} %fusion.7, bf16[1024,6272]{1,0:T(8,128)(2,1)} %all-gather.6.cloned.1.call-done), kind=kOutput, calls=%fused_computation.80 | convolution fusion | flops 4296015872 | bytes 10485760 | tf_op jit(solution)/shard_map/dot_general | solution.py:15
  312.1 9.4 %fusion.47 = bf16[1024,1024]{0,1:T(8,128)(2,1)S(1)} fusion(bf16[1024,6272]{1,0:T(8,128)(2,1)} %all-gather.6.cloned.1.call-done, f32[1024,2048]{1,0:T(8,128)} %fusion.33), kind=kOutput, calls=%fused_computation.81 | convolution fusion | flops 4314890240 | bytes 14680064 | tf_op jit(solution)/shard_map/dot_general | solution.py:15
  323.4 2.4 collective-permute-done.1
  325.8 8.0 %fusion.11 = (bf16[1024,1024]{0,1:T(8,128)(2,1)S(1)}, f32[1024,1024]{0,1:T(8,128)}, f32[1024]{0:T(1024)S(1)}, f32[1024,1024]{0,1:T(8,128)}) fusion(bf16[1024,1024]{0,1:T(8,128)(2,1)S(1)} %copy-done.10, f32[1024]{0:T(1024)S(1)} %add_divide_fusion, f32[1024]{0:T(1024)S(1)} %broadcast_multiply_fusion.1, f32[1024,1024]{0,1:T(8,128)S(1)} %copy-done.2, ...), kind=kLoop, calls=%fused_computation.30 | loop fusion | flops 22019072 | bytes 29384704 | tf_op jit(solution)/shard_map/convert_element_type | solution.py:139
  335.1 3.5 convolution_convert_fusion.5
  338.6 2.3 copy.93
  340.9 2.6 reshape.181
  343.5 5.7 multiply_reduce_fusion
  359.1 2.5 fusion.70
  361.6 2.5 fusion.67
  364.1 3.8 add_convert_fusion
  368.3 2.4 convolution_convert_fusion.4
  370.8 2.3 copy.111
  373.1 2.3 constant_dynamic-update-slice_fusion.7
  375.4 3.6 convolution_convert_fusion.3
  379.0 2.6 copy.112
  381.6 2.3 convolution_convert_fusion.2
  385.5 2.5 constant_dynamic-update-slice_fusion.6
  389.2 10.1 %convert_dynamic-update-slice_fusion.1 = bf16[1024,6272]{1,0:T(8,128)(2,1)} fusion(bf16[1024,6272]{1,0:T(8,128)(2,1)} %constant_dynamic-update-slice_fusion.5, bf16[1024,2048]{1,0:T(8,128)(2,1)} %copy-done.35, f32[1024,1024]{0,1:T(8,128)} %copy-done.1, f32[1024]{0:T(1024)S(1)} %get-tuple-element.34, f32[1024]{0:T(1024)S(1)} %get-tuple-element.61), kind=kOutput, calls=%fused_computation.41 | convolution fusion | flops 4300210176 | bytes 12591104 | tf_op jit(solution)/shard_map/dot_general | solution.py:21
  399.4 2.4 fusion.58
  401.7 6.4 convert_dynamic-update-slice_fusion
  408.1 5.1 fusion.17
  417.7 4.2 fusion.37
  423.2 13.5 %scatter_fusion = bf16[8192,512]{1,0:T(8,128)(2,1)} fusion(bf16[8192,512]{1,0:T(8,128)(2,1)} %bitcast.105, s32[1024]{0:T(1024)S(1)} %bitcast.137, bf16[1024,512]{1,0:T(8,128)(2,1)S(1)} %copy.90), kind=kCustom, calls=%fused_computation.2 | custom fusion | bytes 3149824
  436.8 13.5 %scatter_fusion.1 = bf16[8192,512]{1,0:T(8,128)(2,1)} fusion(bf16[8192,512]{1,0:T(8,128)(2,1)} %bitcast.102, s32[1024]{0:T(1024)S(1)} %bitcast.138, bf16[1024,512]{1,0:T(8,128)(2,1)S(1)} %copy.108), kind=kCustom, calls=%fused_computation.3 | custom fusion | bytes 3149824
  450.3 229.6 %reduce-scatter.2.cloned.1.call-done = bf16[64,6272]{1,0:T(8,128)(2,1)} async-done(((bf16[1024,6272]{1,0:T(8,128)(2,1)}), bf16[64,6272]{1,0:T(8,128)(2,1)}) %reduce-scatter.2.cloned.1.call-update) | async-done | bytes 802832 | tf_op jit(solution)/shard_map/reduce_scatter | solution.py:175
  (162 shorter events, 47.4 us)
Async XLA Ops:
  7.2 67.4 %all-gather.4.cloned.1.call-start = ((), (), s32[]{:S(2)}) async-start(), calls=%async_computation.1 | async-start | bytes 3145728 | tf_op jit(solution)/shard_map/all_gather | solution.py:82
  14.5 7.3 %copy-start.29 = (s32[4,1,256]{2,1,0:T(1,128)S(1)}, s32[4,1,256]{2,1,0:T(1,128)}, u32[]{:S(2)}) copy-start(s32[4,1,256]{2,1,0:T(1,128)} %param.15) | copy-start | bytes 12292
  21.9 14.3 %copy-start.22 = (s32[4,256,1]{1,2,0:T(1,128)}, s32[4,256,1]{1,2,0:T(1,128)S(1)}, u32[]{:S(2)}) copy-start(s32[4,256,1]{1,2,0:T(1,128)S(1)} %get-tuple-element.52) | copy-start | bytes 12292
  57.8 3.3 copy-start.30
  57.8 3.3 copy-start.31
  57.9 3.3 copy-start.32
  57.9 3.5 copy-start.24
  57.9 3.5 copy-start.25
  57.9 3.5 copy-start.26
  57.9 3.5 copy-start.20
  57.9 3.5 copy-start.27
  57.9 3.5 copy-start.21
  61.1 171.8 %all-gather.6.cloned.1.call-start = ((), (), s32[]{:S(2)}) async-start(), calls=%async_computation.2 | async-start | bytes 13647872 | tf_op jit(solution)/shard_map/all_gather | solution.py:61
  61.5 0.9 copy-start.19
  62.4 227.0 %all-gather.8.cloned.1.call-start = ((), (), s32[]{:S(2)}) async-start(), calls=%async_computation.3 | async-start | bytes 3145728 | tf_op jit(solution)/shard_map/all_gather | solution.py:83
  238.7 3.2 copy-start
  258.8 2.3 copy-start.16
  261.0 3.3 copy-start.6
  265.3 4.2 copy-start.14
  265.4 4.2 copy-start.8
  269.6 4.5 collective-permute-start
  270.9 409.0 %reduce-scatter.2.cloned.1.call-start = ((), (), s32[]{:S(2)}) async-start(), calls=%async_computation.4 | async-start | bytes 13647872 | tf_op jit(solution)/shard_map/reduce_scatter | solution.py:175
  278.2 2.0 copy-start.1
  302.6 1.9 copy-start.35
  311.9 10.1 %copy-start.2 = (f32[1024,1024]{0,1:T(8,128)S(1)}, f32[1024,1024]{0,1:T(8,128)}, u32[]{:S(2)}) copy-start(f32[1024,1024]{0,1:T(8,128)} %copy-done.1) | copy-start | bytes 12582916
  311.9 10.1 %collective-permute-start.2 = (bf16[1024,1024]{0,1:T(8,128)(2,1)S(1)}, bf16[1024,1024]{0,1:T(8,128)(2,1)S(1)}, u32[]{:S(2)}, u32[]{:S(2)}) collective-permute-start(bf16[1024,1024]{0,1:T(8,128)(2,1)S(1)} %fusion.44), channel_id=1, source_target_pairs={{0,1},{1,0},{2,3},{3,2},{4,5},{5,4},{6,7},{7,6},{8,9},{9,8},{10,11... | collective-permute-start | bytes 6291464 | tf_op jit(solution)/shard_map/ppermute | solution.py:115
  321.4 4.4 copy-start.10
  321.4 4.4 collective-permute-start.1
  333.8 1.3 copy-start.12
  343.5 5.7 slice-start
  343.5 6.5 slice-start.1
  352.0 1.2 copy-start.7
  353.2 1.4 copy-start.18
  358.1 3.5 copy-start.17
  368.0 40.2 %collective-permute-start.3 = (bf16[1024,1024]{0,1:T(8,128)(2,1)}, bf16[1024,1024]{0,1:T(8,128)(2,1)}, u32[]{:S(2)}, u32[]{:S(2)}) collective-permute-start(bf16[1024,1024]{0,1:T(8,128)(2,1)} %add_convert_fusion), channel_id=1, source_target_pairs={{0,1},{1,0},{2,3},{3,2},{4,5},{5,4},{6,7},{7,6},{8,9},{9,8},{10,11... | collective-permute-start | bytes 6291464 | tf_op jit(solution)/shard_map/ppermute | solution.py:115
  385.5 16.3 %slice-start.2 = ((s8[8388608]{0:T(1024)(128)(4,1)}), s8[4194304]{0:T(1024)(128)(4,1)S(1)}, s32[]{:S(2)}) async-start(s8[8388608]{0:T(1024)(128)(4,1)} %bitcast.145), calls=%async_computation.7 | async-start | bytes 8388608
  389.2 10.2 %copy-start.13 = (bf16[1024,1024]{0,1:T(8,128)(2,1)S(1)}, bf16[1024,1024]{0,1:T(8,128)(2,1)}, u32[]{:S(2)}) copy-start(bf16[1024,1024]{0,1:T(8,128)(2,1)} %copy-done.12) | copy-start | bytes 6291460
  389.2 10.2 %copy-start.15 = (bf16[64,8,4,256]{3,1,2,0:T(8,128)(2,1)S(1)}, bf16[64,8,4,256]{3,1,2,0:T(8,128)(2,1)}, u32[]{:S(2)}) copy-start(bf16[64,8,4,256]{3,1,2,0:T(8,128)(2,1)} %copy-done.14) | copy-start | bytes 3145732
  389.2 12.6 %slice-start.3 = ((s8[8388608]{0:T(1024)(128)(4,1)}), s8[4194304]{0:T(1024)(128)(4,1)S(1)}, s32[]{:S(2)}) async-start(s8[8388608]{0:T(1024)(128)(4,1)} %bitcast.145), calls=%async_computation.8 | async-start | bytes 8388608
  399.3 2.4 copy-start.11
  414.3 0.7 copy-start.23
  414.3 0.7 copy-start.33
  414.3 0.8 copy-start.34
  414.3 1.4 copy-start.4
  414.3 1.4 copy-start.28
  415.2 2.3 copy-start.3
  415.2 2.5 copy-start.5
  679.9 4.6 copy-start.9
Sparse Core Ops, SparseCore 0:
  61.2 13.2 all-gather.3
  77.2 155.6 all-gather.5
  271.0 8.9 all-gather.7
  414.4 265.4 reduce-scatter.1

commit v2 on v1

--- a/solution.py
+++ b/solution.py
@@ -2,6 +2,287 @@
 import jax.numpy as jnp
 from jax import lax
 from jax.sharding import PartitionSpec as P
+from jax.experimental import pallas as pl
+from jax.experimental.pallas import tpu as pltpu
+
+MESH = pl.DeviceIdType.MESH
+NB = 48
+PATTERN = "XYZXYXYZ"
+LAGS = (0, 3, 6, 9, 12, 15)
+
+class Place:
+    def __init__(self):
+        me = lax.axis_index("dp")
+        self.x = me % 2
+        self.y = (me // 2) % 2
+        self.z = me // 4
+        self.nx = me + 1 - 2 * self.x
+        self.ny = me + 2 - 4 * self.y
+        self.up = me + 4
+        self.dn = me - 4
+
+def barrier(p, core=False):
+    bar = pltpu.get_barrier_semaphore()
+    def sig(d):
+        pl.semaphore_signal(bar, inc=1, device_id=d, device_id_type=MESH)
+    sig({"dp": p.nx}); sig({"dp": p.ny})
+    if core: sig({"tensor": 1 - lax.axis_index("tensor")})
+    @pl.when(p.z < 3)
+    def _(): sig({"dp": p.up})
+    @pl.when(p.z > 0)
+    def _(): sig({"dp": p.dn})
+    inner = jnp.logical_and(p.z > 0, p.z < 3)
+    base = 3 if core else 2
+    @pl.when(inner)
+    def _(): pl.semaphore_wait(bar, base + 2)
+    @pl.when(jnp.logical_not(inner))
+    def _(): pl.semaphore_wait(bar, base + 1)
+
+def both(a, b): return jnp.logical_and(a, b)
+
+class Gather:
+    def __init__(self, p, W, ss, rs):
+        self.p, self.W, self.ss, self.rs = p, W, ss, rs
+    def copy(self, ref, b, k, dev):
+        return pltpu.make_async_remote_copy(ref, ref, self.ss.at[b, k], self.rs.at[b, k], device_id={"dp": dev}, device_id_type=MESH)
+    def zref(self, b, c, zz):
+        p = self.p
+        zz = jnp.clip(zz, 0, 3)
+        return self.W.at[b, zz] if c == "Z" else self.W.at[b, zz, p.y, p.x]
+    def zsend(self, b, c, hop, act):
+        p = self.p
+        @pl.when(both(p.z - hop + 1 >= 0, p.z < 3))
+        def _(): act(self.copy(self.zref(b, c, p.z - hop + 1), b, hop - 1, jnp.minimum(p.up, 15)))
+        @pl.when(both(p.z + hop - 1 <= 3, p.z > 0))
+        def _(): act(self.copy(self.zref(b, c, p.z + hop - 1), b, 2 + hop, jnp.maximum(p.dn, 0)))
+    def zrecv(self, b, c, hop):
+        p = self.p
+        @pl.when(p.z - hop >= 0)
+        def _(): self.copy(self.zref(b, c, p.z - hop), b, hop - 1, p.nx).wait_recv()
+        @pl.when(p.z + hop <= 3)
+        def _(): self.copy(self.zref(b, c, p.z + hop), b, 2 + hop, p.nx).wait_recv()
+    def stage(self, b, c, j):
+        p, W = self.p, self.W
+        x, y, z = p.x, p.y, p.z
+        if c == "X":
+            seq = ["z1", "z2", "z3", ("y", W.at[b, :, y, x], W.at[b, :, 1 - y, x]), ("x", W.at[b, :, :, x], W.at[b, :, :, 1 - x])]
+        elif c == "Y":
+            seq = ["z1", "z2", "z3", ("x", W.at[b, :, y, x], W.at[b, :, y, 1 - x]), ("y", W.at[b, :, y], W.at[b, :, 1 - y])]
+        else:
+            seq = [("x", W.at[b, z, y, x], W.at[b, z, y, 1 - x]), ("y", W.at[b, z, y], W.at[b, z, 1 - y]), "z1", "z2", "z3"]
+        return seq[j]
+    def send(self, b, c, j, act=lambda d: d.start()):
+        st = self.stage(b, c, j)
+        if isinstance(st, str): self.zsend(b, c, int(st[1]), act)
+        else:
+            kind, dev = (6, self.p.ny) if st[0] == "y" else (7, self.p.nx)
+            act(self.copy(st[1], b, kind, dev))
+    def recv(self, b, c, j):
+        st = self.stage(b, c, j)
+        if isinstance(st, str): self.zrecv(b, c, int(st[1]))
+        else:
+            kind, dev = (6, self.p.ny) if st[0] == "y" else (7, self.p.nx)
+            self.copy(st[2], b, kind, dev).wait_recv()
+    def step(self, s, pos, static=None):
+        for j in (5, 4, 3, 2, 1, 0):
+            if static is not None and not (0 <= static - LAGS[j] < NB): continue
+            b = s - LAGS[j]
+            c = PATTERN[(pos - LAGS[j]) % 8]
+            if j > 0: self.recv(b, c, j - 1)
+            if j < 5: self.send(b, c, j)
+    def drain(self):
+        def body(r, _):
+            for pos in range(8):
+                for j in range(5):
+                    self.send(r * 8 + pos, PATTERN[pos], j, act=lambda d: d.wait_send())
+            return 0
+        lax.fori_loop(0, NB // 8, body, 0)
+
+class Scatter:
+    def __init__(self, p, G, out, L8, L4, LZ, P4, P2, P1, ss, rs):
+        self.p, self.G, self.out, self.ss, self.rs = p, G, out, ss, rs
+        self.L8, self.L4, self.LZ, self.P4, self.P2, self.P1 = L8, L4, LZ, P4, P2, P1
+    def slot(self, b, bp):
+        r = b // 8
+        c = PATTERN[bp]
+        if c == "Z": return r * 2 + {2: 0, 7: 1}[bp]
+        return r * 6 + {0: 0, 1: 1, 3: 2, 4: 3, 5: 4, 6: 5}[bp]
+    def copy(self, src, dst, b, k, dev):
+        return pltpu.make_async_remote_copy(src, dst, self.ss.at[b, k], self.rs.at[b, k], device_id={"dp": dev}, device_id_type=MESH)
+    def gz(self, b, c, t):
+        t = jnp.clip(t, 0, 3)
+        return self.G.at[b, t] if c == "Z" else self.G.at[b, t, self.p.y, self.p.x]
+    def lz(self, b, bp, k):
+        i = self.slot(b, bp)
+        return self.P4.at[i, k] if PATTERN[bp] == "Z" else self.LZ.at[i, k]
+    def add(self, ref, land):
+        ref[...] = (ref[...].astype(jnp.float32) + land[...].astype(jnp.float32)).astype(ref.dtype)
+    def zsend(self, b, bp, hop, act):
+        p, c = self.p, PATTERN[bp]
+        @pl.when(both(p.z + hop <= 3, p.z < 3))
+        def _(): act(self.copy(self.gz(b, c, p.z + hop), self.lz(b, bp, hop - 1), b, hop - 1, jnp.minimum(p.up, 15)))
+        @pl.when(both(p.z - hop >= 0, p.z > 0))
+        def _(): act(self.copy(self.gz(b, c, p.z - hop), self.lz(b, bp, 2 + hop), b, 2 + hop, jnp.maximum(p.dn, 0)))
+    def zrecv(self, b, bp, hop, final):
+        p, c = self.p, PATTERN[bp]
+        def take(k, t):
+            land = self.lz(b, bp, k)
+            self.copy(land, land, b, k, p.nx).wait_recv()
+            if not final: self.add(self.gz(b, c, t), land)
+        lo = both(p.z >= 1, p.z - 1 + hop <= 3)
+        hi = both(p.z <= 2, p.z + 1 - hop >= 0)
+        if not final:
+            @pl.when(lo)
+            def _(): take(hop - 1, p.z - 1 + hop)
+            @pl.when(hi)
+            def _(): take(2 + hop, p.z + 1 - hop)
+        else:
+            own = self.G.at[b, p.z, p.y, p.x]
+            a, d = self.lz(b, bp, 0), self.lz(b, bp, 3)
+            f32 = jnp.float32
+            @pl.when(p.z == 0)
+            def _():
+                take(3, p.z)
+                self.out[b] = own[...].astype(f32) + d[...].astype(f32)
+            @pl.when(p.z == 3)
+            def _():
+                take(0, p.z)
+                self.out[b] = own[...].astype(f32) + a[...].astype(f32)
+            @pl.when(both(p.z > 0, p.z < 3))
+            def _():
+                take(0, p.z); take(3, p.z)
+                self.out[b] = own[...].astype(f32) + a[...].astype(f32) + d[...].astype(f32)
+    def stage(self, b, bp, j):
+        p, G = self.p, self.G
+        x, y, z = p.x, p.y, p.z
+        c = PATTERN[bp]; i = self.slot(b, bp)
+        if c == "X":
+            return [("x", G.at[b, :, :, 1 - x], self.L8.at[i], G.at[b, :, :, x]), ("y", G.at[b, :, 1 - y, x], self.L4.at[i], G.at[b, :, y, x]), "z3", "z2", "z1"][j]
+        if c == "Y":
+            return [("y", G.at[b, :, 1 - y], self.L8.at[i], G.at[b, :, y]), ("x", G.at[b, :, y, 1 - x], self.L4.at[i], G.at[b, :, y, x]), "z3", "z2", "z1"][j]
+        return ["z3", "z2", "z1", ("y", G.at[b, z, 1 - y], self.P2.at[i], G.at[b, z, y]), ("x", G.at[b, z, y, 1 - x], self.P1.at[i], G.at[b, z, y, x])][j]
+    def send(self, b, bp, j, act=lambda d: d.start()):
+        st = self.stage(b, bp, j)
+        if isinstance(st, str): self.zsend(b, bp, int(st[1]), act)
+        else:
+            kind, dev = (6, self.p.ny) if st[0] == "y" else (7, self.p.nx)
+            act(self.copy(st[1], st[2], b, kind, dev))
+    def recv(self, b, bp, j):
+        st = self.stage(b, bp, j)
+        if isinstance(st, str): self.zrecv(b, bp, int(st[1]), PATTERN[bp] != "Z" and j == 4)
+        else:
+            kind, dev = (6, self.p.ny) if st[0] == "y" else (7, self.p.nx)
+            self.copy(st[2], st[2], b, kind, dev).wait_recv()
+            if j == 4: self.out[b] = st[3][...].astype(jnp.float32) + st[2][...].astype(jnp.float32)
+            else: self.add(st[3], st[2])
+    def step(self, s, pos, static=None, nb=NB):
+        live = [j for j in (5, 4, 3, 2, 1, 0) if static is None or 0 <= static - LAGS[j] < nb]
+        for j in live:
+            if j > 0: self.recv(s - LAGS[j], (pos - LAGS[j]) % 8, j - 1)
+        for j in live:
+            if j < 5: self.send(s - LAGS[j], (pos - LAGS[j]) % 8, j)
+    def drain(self):
+        def body(r, _):
+            for pos in range(8):
+                for j in range(5):
+                    self.send(r * 8 + pos, pos, j, act=lambda d: d.wait_send())
+            return 0
+        lax.fori_loop(0, NB // 8, body, 0)
+    @staticmethod
+    def scratch():
+        bf = jnp.bfloat16
+        nx, nz = NB // 8 * 6, NB // 8 * 2
+        return [pltpu.VMEM((nx, 4, 2, 64, 128), bf), pltpu.VMEM((nx, 4, 64, 128), bf), pltpu.VMEM((nx, 6, 64, 128), bf),
+                pltpu.VMEM((nz, 6, 2, 2, 64, 128), bf), pltpu.VMEM((nz, 2, 64, 128), bf), pltpu.VMEM((nz, 64, 128), bf),
+                pltpu.SemaphoreType.DMA((NB, 8)), pltpu.SemaphoreType.DMA((NB, 8))]
+
+
+def run_steps(steps):
+    for s in range(16):
+        steps.step(s, s % 8, static=s)
+
+    def body(r, _):
+        for pos in range(8):
+            steps.step(r * 8 + pos, pos)
+        return 0
+
+    lax.fori_loop(2, NB // 8, body, 0)
+    for s in range(NB, NB + LAGS[5] + 1):
+        steps.step(s, s % 8, static=s)
+    steps.drain()
+
+
+def gather_kernel(w_ref, o_ref, W, ss, rs, ls):
+    p = Place()
+    first = pltpu.make_async_copy(w_ref, W.at[:, p.z, p.y, p.x], ls.at[0])
+    first.start()
+    barrier(p)
+    first.wait()
+    run_steps(Gather(p, W, ss, rs))
+    last = pltpu.make_async_copy(W, o_ref, ls.at[0])
+    last.start()
+    last.wait()
+
+
+def scatter_kernel(g_ref, o_ref, G, ls, *rest):
+    p = Place()
+    first = pltpu.make_async_copy(g_ref, G, ls.at[0])
+    first.start()
+    barrier(p)
+    first.wait()
+    run_steps(Scatter(p, G, o_ref, *rest))
+
+
+def gather_blocks(packed):
+    if lax.axis_size("dp") != 16:
+        return lax.all_gather(packed, "dp", axis=1, tiled=True)
+    out = pl.pallas_call(
+        gather_kernel,
+        out_shape=jax.ShapeDtypeStruct((NB, 4, 2, 2, 64, 128), jnp.bfloat16),
+        in_specs=[pl.BlockSpec(memory_space=pl.ANY)],
+        out_specs=pl.BlockSpec(memory_space=pl.ANY),
+        scratch_shapes=[
+            pltpu.VMEM((NB, 4, 2, 2, 64, 128), jnp.bfloat16),
+            pltpu.SemaphoreType.DMA((NB, 8)),
+            pltpu.SemaphoreType.DMA((NB, 8)),
+            pltpu.SemaphoreType.DMA((1,)),
+        ],
+        compiler_params=pltpu.CompilerParams(
+            collective_id=1, has_side_effects=True, vmem_limit_bytes=60 * 1024 * 1024
+        ),
+        name="gather_weights",
+    )(packed)
+    return out.reshape(NB, 1024, 128)
+
+
+def scatter_blocks(grads):
+    if lax.axis_size("dp") != 16:
+        return lax.psum_scatter(grads, "dp", scatter_dimension=1, tiled=True).astype(jnp.float32)
+    return pl.pallas_call(
+        scatter_kernel,
+        out_shape=jax.ShapeDtypeStruct((NB, 64, 128), jnp.float32),
+        in_specs=[pl.BlockSpec(memory_space=pl.ANY)],
+        out_specs=pl.BlockSpec(memory_space=pltpu.VMEM),
+        scratch_shapes=[
+            pltpu.VMEM((NB, 4, 2, 2, 64, 128), jnp.bfloat16),
+            pltpu.SemaphoreType.DMA((1,)),
+        ]
+        + Scatter.scratch(),
+        compiler_params=pltpu.CompilerParams(
+            collective_id=2, has_side_effects=True, vmem_limit_bytes=63 * 1024 * 1024
+        ),
+        name="scatter_grads",
+    )(grads.reshape(NB, 4, 2, 2, 64, 128))
+
+
+def to_blocks(x):
+    rows, cols = x.shape
+    return x.reshape(rows, cols // 128, 128).transpose(1, 0, 2)
+
+
+def from_blocks(x):
+    return x.transpose(1, 0, 2).reshape(x.shape[1], -1)
+
 
 HD = 64
 eps_norm = 1e-05
@@ -55,24 +336,25 @@
     scale = HD ** (-0.5)
     swap = [(0, 1), (1, 0)]
 
-    vec = jnp.stack([w_route, gain_attn, gain_mlp], 1)
-    vec = jnp.pad(vec, ((0, 0), (0, 125)))
-    packed = jnp.concatenate([w_query, w_key, w_value, w_up, w_out.T, w_down.T, vec], 1)
-    gathered = lax.all_gather(packed, "dp", axis=0, tiled=True)
-    b1, b2, b3 = cols, 2 * cols, 3 * cols
-    b4 = b3 + hidden_cols
-    b5 = b4 + w_out.shape[0]
-    b6 = b5 + w_down.shape[0]
-    fq = gathered[:, :b1]
-    fk = gathered[:, b1:b2]
-    fv = gathered[:, b2:b3]
-    fup = gathered[:, b3:b4]
-    foutT = gathered[:, b4:b5]
-    fdownT = gathered[:, b5:b6]
-    route = gathered[:, b6]
+    vec = jnp.stack([w_route, gain_attn, gain_mlp], 0)
+    vec = lax.all_gather(vec, "dp", axis=1, tiled=True)
+    route = vec[0]
     route_f32 = route.astype(jnp.float32)
-    gain1 = gathered[:, b6 + 1].astype(jnp.float32)
-    gain2 = gathered[:, b6 + 2].astype(jnp.float32)
+    gain1 = vec[1].astype(jnp.float32)
+    gain2 = vec[2].astype(jnp.float32)
+    mlp = jnp.concatenate(
+        [
+            to_blocks(w_up).reshape(8, 2, -1, 128),
+            to_blocks(w_down.T).reshape(8, 2, -1, 128),
+        ],
+        1,
+    ).reshape(32, -1, 128)
+    packed = jnp.concatenate([to_blocks(x) for x in (w_query, w_key, w_value, w_out.T)] + [mlp])
+    blocks = gather_blocks(packed)
+    fq, fk, fv, foutT = [from_blocks(blocks[4 * i : 4 * i + 4]) for i in range(4)]
+    mlp = blocks[16:].reshape(8, 2, 2, -1, 128)
+    fup = from_blocks(mlp[:, 0].reshape(16, -1, 128))
+    fdownT = from_blocks(mlp[:, 1].reshape(16, -1, 128))
 
     tok = tokens.reshape(batch, length, half_width)
     cot = cotangent.reshape(batch, length, half_width)
@@ -168,23 +450,28 @@
         grad_rows.reshape(batch, capacity, half_width), unique_indices=True
     )
 
-    g_vec = jnp.pad(jnp.stack([g_route, g_gain1, g_gain2], 1), ((0, 0), (0, 125)))
-    grads = jnp.concatenate(
-        [x.astype(jnp.bfloat16) for x in (g_q, g_k, g_v, g_up, g_outT, g_downT, g_vec)], 1
-    )
-    own = lax.psum_scatter(grads, "dp", scatter_dimension=0, tiled=True).astype(jnp.float32)
+    g_vec = lax.psum_scatter(
+        jnp.stack([g_route, g_gain1, g_gain2], 0), "dp", scatter_dimension=1, tiled=True
+    )
+    low = [to_blocks(x.astype(jnp.bfloat16)) for x in (g_q, g_k, g_v, g_outT, g_up, g_downT)]
+    mlp = jnp.concatenate([x.reshape(8, 2, -1, 128) for x in low[4:]], 1).reshape(32, -1, 128)
+    own = scatter_blocks(jnp.concatenate(low[:4] + [mlp]))
+    o_q, o_k, o_v, o_out = [from_blocks(own[4 * i : 4 * i + 4]) for i in range(4)]
+    mlp = own[16:].reshape(8, 2, 2, -1, 128)
+    o_up = from_blocks(mlp[:, 0].reshape(16, -1, 128))
+    o_down = from_blocks(mlp[:, 1].reshape(16, -1, 128))
     return (
         output.reshape(tokens.shape),
         input_grad.reshape(tokens.shape),
-        own[:, :b1],
-        own[:, b1:b2],
-        own[:, b2:b3],
-        own[:, b4:b5].T,
-        own[:, b3:b4],
-        own[:, b5:b6].T,
-        own[:, b6],
-        own[:, b6 + 1],
-        own[:, b6 + 2],
+        o_q,
+        o_k,
+        o_v,
+        o_out.T,
+        o_up,
+        o_down.T,
+        g_vec[0],
+        g_vec[1],
+        g_vec[2],
     )
 
 

time: 701 us -> 666 us (0.950)
  waiting for transfers between devices: 401 us -> 40 us
  Pallas kernels: 0 us -> 227 us
  local copies, waits for them, and re-layouts: 133 us -> 188 us
  blocking collectives: 0 us -> 42.4 us
  other arithmetic: 35.1 us -> 48.2 us
  matrix products: 106 us -> 98.5 us
    reduce_scatter x1 -> x0, waiting for transfers between devices: 230 us -> none  [shards(): lax.psum_scatter(grads, 'dp', scatter_dimension=0, tiled=True)]
    pallas_call x0 -> x2, Pallas kernels: none -> 227 us  [the longest x1 119 us: scatter_blocks(): pl.pallas_call(scatter_kernel, out_shape=jax.ShapeDtypeStruct((NB, 64, 12...]
    all_gather x1 -> x0, waiting for transfers between devices: 156 us -> none  [shards(): gathered = lax.all_gather(packed, 'dp', axis=0, tiled=True)]
    all_gather x0 -> x1, blocking collectives: none -> 42.4 us  [shards(): vec = lax.all_gather(vec, 'dp', axis=1, tiled=True)]
    unnamed x4, waiting for transfers between devices: 0.07 us -> 39.9 us
    slice x4 -> x12, local copies, waits for them, and re-layouts: 4.36 us -> 42 us  [the longest x2 12.6 us: shards(): fup = from_blocks(mlp[:, 0].reshape(16, -1, 128))]
    all_gather x1, waiting for transfers between devices: 11.9 us -> 0.02 us  [shards(): rows = lax.all_gather(rows_half, 'tensor', axis=1, tiled=True)]
    concatenate x2, local copies, waits for them, and re-layouts: 0.83 us -> 10.7 us  [the longest x1 10.7 us: shards(): own = scatter_blocks(jnp.concatenate(low[:4] + [mlp]))]
  transfers between devices with their start and end apart: 8 -> 7, of which waited for: 5 -> 1; matrix products, arithmetic and copies ran while one was open for 15% -> 22% of each run, Pallas kernels for 0% -> 34%
where the time goes in v2:
time: 666 us; the launch traced here: 659 us
  Pallas kernels  227 us (34%)
  local copies, waits for them, and re-layouts  188 us (28%)
  matrix products  98.5 us (15%)
  other arithmetic  48.2 us (7%)
  blocking collectives  42.4 us (6%)
  waiting for transfers between devices  40 us (6%)
  between operations  15 us (2%)
    pallas_call x1, Pallas kernels, scatter_blocks(): pl.pallas_call(scatter_kernel, out_shape=jax.ShapeDtypeStruct((NB, 64, 12...  119 us
    pallas_call x1, Pallas kernels, gather_blocks(): pl.pallas_call(gather_kernel, out_shape=jax.ShapeDtypeStruct((NB, 4, 2, 2...  108 us
    unnamed x146, local copies, waits for them, and re-layouts  64.6 us
    all_gather x1, blocking collectives, shards(): vec = lax.all_gather(vec, 'dp', axis=1, tiled=True)  42.4 us
    unnamed x4, waiting for transfers between devices  39.9 us
    dot_general x7, matrix products, dense(): return jnp.dot(left, right, preferred_element_type=jnp.float32)  32.2 us
    dot_general x6, matrix products, dense_t(): lax.dot_general(left, right, (((1,), (1,)), ((), ())), preferred_element_...  29.3 us
    dot_general x6, matrix products, dense_g(): lax.dot_general(left, right, (((0,), (0,)), ((), ())), preferred_element_...  19.7 us
  transfers between devices with their start and end apart: 7, of which 1 were waited for; matrix products, arithmetic and copies ran while one was open for 22% of the time, Pallas kernels for 34%

profile of v2, /device:TPU:0, one launch (start us, length us, event | category | flops | bytes accessed | tf_op | source)
XLA Modules:
  0.0 659.5 jit_solution(8469205852094636860)
XLA Ops:
  7.2 7.3 %copy.236 = bf16[4,1,2048,512]{3,2,1,0:T(8,128)(2,1)} copy(bf16[4,1,2048,512]{3,2,1,0:T(8,128)(2,1)} %param.14) | data formatting | bytes 16777216
  14.6 7.3 %copy.237 = bf16[4,1,2048,512]{3,2,1,0:T(8,128)(2,1)} copy(bf16[4,1,2048,512]{3,2,1,0:T(8,128)(2,1)} %param.25) | data formatting | bytes 16777216
  21.9 14.2 %gather_fusion = bf16[1024,512]{1,0:T(8,128)(2,1)S(1)} fusion(bf16[4,2048,512]{2,1,0:T(8,128)(2,1)} %bitcast.274, s32[1024]{0:T(1024)S(1)} %bitcast.272), kind=kCustom, calls=%fused_computation.clone | custom fusion | bytes 2105344 | tf_op jit(solution)/shard_map/jit(take_along_axis)/gather | solution.py:362
  36.9 14.2 %gather_fusion.1 = bf16[1024,512]{1,0:T(8,128)(2,1)S(1)} fusion(bf16[4,2048,512]{2,1,0:T(8,128)(2,1)} %bitcast.277, s32[1024]{0:T(1024)S(1)} %bitcast.273), kind=kCustom, calls=%fused_computation.1.clone | custom fusion | bytes 2105344 | tf_op jit(solution)/shard_map/jit(take_along_axis)/gather | solution.py:363
  55.1 42.4 %all-gather = bf16[16,64,3]{1,2,0:T(4,128)(2,1)S(1)} all-gather(bf16[1,64,3]{1,2,0:T(4,128)(2,1)S(1)} %maximum_bitcast_fusion), channel_id=1, replica_groups=mesh['dp'=16,'tensor'=2] {'dp'}, dimensions={0}, use_global_device_ids=true | all-gather | bytes 6528 | tf_op jit(solution)/shard_map/all_gather | solution.py:340
  99.1 107.7 %gather_weights.1 = bf16[48,4,2,2,64,128]{5,4,3,2,1,0:T(8,128)(2,1)} custom-call(bf16[48,64,128]{2,1,0:T(8,128)(2,1)} %copy-done.32), custom_call_target="tpu_custom_call" | custom-call | tf_op jit(solution)/shard_map/gather_weights/pallas_call | solution.py:239
  206.8 4.5 fusion.80
  219.5 4.1 convolution_convert_fusion.8
  226.8 2.8 convolution_convert_fusion.9
  232.8 4.2 convolution_convert_fusion.10
  239.3 3.1 reshape.277
  242.4 2.5 fusion.59
  248.1 2.5 copy-done.11
  251.8 2.7 convolution_convert_fusion.2
  255.8 10.6 %slice.84 = bf16[32,4,2,2,64,128]{5,4,3,2,1,0:T(8,128)(2,1)} slice(bf16[48,4,2,2,64,128]{5,4,3,2,1,0:T(8,128)(2,1)} %gather_weights.1), slice={[16:48], [0:4], [0:2], [0:2], [0:64], [0:128]} | slice | bytes 16777216 | tf_op jit(solution)/shard_map/slice | solution.py:355
  267.2 6.1 fusion.81
  273.3 6.5 copy.122
  279.8 6.5 copy.123
  286.9 2.4 convert_element_type.144
  289.8 3.9 multiply_reduce_fusion.3
  293.7 5.0 fusion.72
  298.7 3.3 copy-done.53
  302.0 6.0 convolution_convert_fusion.1
  308.0 13.5 %fusion.7 = bf16[1024,2048]{1,0:T(8,128)(2,1)S(1)} fusion(f32[1024,2048]{1,0:T(8,128)} %copy-done.53, bf16[1024,2048]{0,1:T(8,128)(2,1)} %bitcast.310, bf16[1024,1024]{0,1:T(8,128)(2,1)} %all-gather.6.cloned.1.call-done, f32[1024]{0:T(1024)S(1)} %add_divide_fusion), kind=kOutput, calls=%fused_computation.13 | convolution fusion | flops 4340056064 | bytes 18878464 | tf_op jit(solution)/shard_map/dot_general | solution.py:292
  321.6 5.8 convolution_convert_fusion
  327.9 5.0 convert_bitcast_fusion.1
  334.3 3.1 copy.147
  337.4 5.4 convert_bitcast_fusion
  344.3 3.0 copy.148
  347.3 7.4 %pad_maximum_fusion = bf16[8,4,1024,128]{3,2,1,0:T(8,128)(2,1)} fusion(bf16[8,2,1024,128]{3,2,1,0:T(8,128)(2,1)} %bitcast.285, bf16[8,2,1024,128]{3,2,1,0:T(8,128)(2,1)} %bitcast.284), kind=kLoop, calls=%fused_computation.14 | loop fusion | flops 4194304 | bytes 16777216 | tf_op jit(solution)/shard_map/concatenate | solution.py:457
  354.7 5.0 multiply_reduce_fusion.1
  360.0 9.3 %fusion.11 = (bf16[1024,1024]{0,1:T(8,128)(2,1)S(1)}, f32[1024,1024]{0,1:T(8,128)}, f32[1024]{0:T(1024)S(1)}, f32[1024,1024]{0,1:T(8,128)}) fusion(bf16[1024,1024]{0,1:T(8,128)(2,1)S(1)} %copy-done.24, f32[1024]{0:T(1024)S(1)} %add_divide_fusion, f32[1024]{0:T(1024)S(1)} %broadcast_multiply_fusion.1, f32[1024,1024]{0,1:T(8,128)S(1)} %copy-done.6, ...), kind=kLoop, calls=%fused_computation.31 | loop fusion | flops 22019072 | bytes 29384704 | tf_op jit(solution)/shard_map/convert_element_type | solution.py:421
  377.2 6.1 fusion.45
  383.3 4.8 multiply_reduce_fusion
  390.1 2.4 fusion.52
  397.8 2.3 convolution_convert_fusion.4
  404.7 3.3 fusion.86
  408.0 2.3 convolution_convert_fusion.5
  410.3 2.4 copy.144
  412.8 4.6 fusion.85
  421.3 6.8 %add_convert_fusion = bf16[1024,1024]{0,1:T(8,128)(2,1)} fusion(f32[1024,1024]{0,1:T(8,128)} %fusion.85, f32[1024,1024]{0,1:T(8,128)} %fusion.86, bf16[1024,512]{0,1:T(8,128)(2,1)} %bitcast.304, bf16[1024,512]{0,1:T(8,128)(2,1)} %bitcast.301), kind=kOutput, calls=%fused_computation.44 | convolution fusion | flops 1076887552 | bytes 12582912 | tf_op jit(solution)/shard_map/dot_general | solution.py:296
  432.9 10.7 %constant_dynamic-update-slice_fusion.1.g_ref = bf16[48,4,2,2,64,128]{5,4,3,2,1,0:T(8,128)(2,1)} fusion(bf16[48,4,2,2,64,128]{5,4,3,2,1,0:T(8,128)(2,1)} %constant_dynamic-update-slice_fusion.2, bf16[32,4,2,2,64,128]{5,4,3,2,1,0:T(8,128)(2,1)} %bitcast.280), kind=kLoop, calls=%fused_computation.125 | loop fusion | bytes 16777216 | tf_op jit(solution)/shard_map/concatenate | solution.py:458
  443.6 118.9 %scatter_grads.1 = f32[48,64,128]{2,1,0:T(8,128)} custom-call(bf16[48,4,2,2,64,128]{5,4,3,2,1,0:T(8,128)(2,1)} %constant_dynamic-update-slice_fusion.1.g_ref), custom_call_target="tpu_custom_call" | custom-call | tf_op jit(solution)/shard_map/scatter_grads/pallas_call | solution.py:261
  568.5 5.3 fusion.17
  574.9 5.9 fusion.27
  582.8 13.7 %scatter_fusion.1 = bf16[8192,512]{1,0:T(8,128)(2,1)} fusion(bf16[8192,512]{1,0:T(8,128)(2,1)} %bitcast.278, s32[1024]{0:T(1024)S(1)} %bitcast.356, bf16[1024,512]{1,0:T(8,128)(2,1)S(1)} %copy.142), kind=kCustom, calls=%fused_computation.3 | custom fusion | bytes 3149824
  596.5 13.6 %scatter_fusion = bf16[8192,512]{1,0:T(8,128)(2,1)} fusion(bf16[8192,512]{1,0:T(8,128)(2,1)} %bitcast.275, s32[1024]{0:T(1024)S(1)} %bitcast.357, bf16[1024,512]{1,0:T(8,128)(2,1)S(1)} %copy.124), kind=kCustom, calls=%fused_computation.2 | custom fusion | bytes 3149824
  610.2 39.9 %reduce-scatter.4.cloned.1.call-done = f32[64,3]{1,0:T(8,128)} async-done(((f32[1024,3]{1,0:T(8,128)}), f32[64,3]{1,0:T(8,128)}) %reduce-scatter.4.cloned.1.call-update) | async-done | bytes 784
  (220 shorter events, 74.0 us)
Async XLA Ops:
  7.2 90.8 %copy-start = (bf16[64,512]{1,0:T(8,128)(2,1)S(1)}, bf16[64,512]{1,0:T(8,128)(2,1)}, u32[]{:S(2)}) copy-start(bf16[64,512]{1,0:T(8,128)(2,1)} %param.16) | copy-start | bytes 196612
  7.2 209.6 %all-gather.4.cloned.1.call-start = ((), (), s32[]{:S(2)}) async-start(), calls=%async_computation.1 | async-start | bytes 3145728 | tf_op jit(solution)/shard_map/all_gather | solution.py:364
  14.6 7.3 %copy-start.47 = (s32[4,1,256]{2,1,0:T(1,128)S(1)}, s32[4,1,256]{2,1,0:T(1,128)}, u32[]{:S(2)}) copy-start(s32[4,1,256]{2,1,0:T(1,128)} %param.15) | copy-start | bytes 12292
  51.9 45.8 %copy-start.33 = (bf16[64,2048]{1,0:T(8,128)(2,1)S(1)}, bf16[64,2048]{1,0:T(8,128)(2,1)}, u32[]{:S(2)}) copy-start(bf16[64,2048]{1,0:T(8,128)(2,1)} %param.20) | copy-start | bytes 786436
  51.9 45.9 %copy-start.34 = (bf16[2048,64]{0,1:T(8,128)(2,1)S(1)}, bf16[2048,64]{0,1:T(8,128)(2,1)}, u32[]{:S(2)}) copy-start(bf16[2048,64]{0,1:T(8,128)(2,1)} %param.21) | copy-start | bytes 786436
  53.8 44.2 %copy-start.35 = (bf16[64,512]{1,0:T(8,128)(2,1)S(1)}, bf16[64,512]{1,0:T(8,128)(2,1)}, u32[]{:S(2)}) copy-start(bf16[64,512]{1,0:T(8,128)(2,1)} %param.17) | copy-start | bytes 196612
  53.8 44.2 %copy-start.36 = (bf16[64,512]{1,0:T(8,128)(2,1)S(1)}, bf16[64,512]{1,0:T(8,128)(2,1)}, u32[]{:S(2)}) copy-start(bf16[64,512]{1,0:T(8,128)(2,1)} %param.18) | copy-start | bytes 196612
  53.8 44.3 %copy-start.37 = (bf16[512,64]{0,1:T(8,128)(2,1)S(1)}, bf16[512,64]{0,1:T(8,128)(2,1)}, u32[]{:S(2)}) copy-start(bf16[512,64]{0,1:T(8,128)(2,1)} %param.19) | copy-start | bytes 196612
  55.0 253.0 %all-gather.6.cloned.1.call-start = ((), (), s32[]{:S(2)}) async-start(), calls=%async_computation.2 | async-start | bytes 3145728 | tf_op jit(solution)/shard_map/all_gather | solution.py:365
  214.0 5.4 copy-start.13
  216.8 16.1 %copy-start.44 = (f32[1,1024]{1,0:T(1,128)}, f32[1,1024]{1,0:T(1,128)S(1)}, u32[]{:S(2)}) copy-start(f32[1,1024]{1,0:T(1,128)S(1)} %get-tuple-element.67) | copy-start | bytes 12292
  219.5 13.4 %copy-start.38 = (f32[1024]{0:T(1024)}, f32[1024]{0:T(1024)S(1)}, u32[]{:S(2)}) copy-start(f32[1024]{0:T(1024)S(1)} %get-tuple-element.69) | copy-start | bytes 12292
  223.6 3.2 copy-start.2
  232.8 9.6 %copy-start.7 = (bf16[4,256,8,64]{1,0,3,2:T(4,128)(2,1)}, bf16[4,256,8,64]{1,0,3,2:T(4,128)(2,1)S(1)}, u32[]{:S(2)}) copy-start(bf16[4,256,8,64]{1,0,3,2:T(4,128)(2,1)S(1)} %reshape.279) | copy-start | bytes 3145732
  247.3 3.3 copy-start.11
  254.5 35.3 %collective-permute-start = (bf16[1024,1024]{0,1:T(8,128)(2,1)}, bf16[1024,1024]{0,1:T(8,128)(2,1)}, u32[]{:S(2)}, u32[]{:S(2)}) collective-permute-start(bf16[1024,1024]{0,1:T(8,128)(2,1)} %convolution_convert_fusion.2), channel_id=1, source_target_pairs={{0,1},{1,0},{2,3},{3,2},{4,5},{5,4},{6,7},{7,6},{8,9},{9,8},{10,11... | collective-permute-start | bytes 6291464 | tf_op jit(solution)/shard_map/ppermute | solution.py:397
  255.8 394.3 %reduce-scatter.4.cloned.1.call-start = ((), (), s32[]{:S(2)}) async-start(), calls=%async_computation.3 | async-start | bytes 557056
  255.8 10.6 %copy-start.52 = (s32[2]{0:T(128)S(1)}, s32[2]{0:T(128)}, u32[]{:S(2)}) copy-start(s32[2]{0:T(128)} %constant.58) | copy-start | bytes 28
  255.8 10.7 %copy-start.51 = (s32[2]{0:T(128)S(1)}, s32[2]{0:T(128)}, u32[]{:S(2)}) copy-start(s32[2]{0:T(128)} %constant.61) | copy-start | bytes 28
  289.8 3.9 copy-start.41
  289.8 3.9 copy-start.16
  293.7 5.0 copy-start.4
  293.7 8.3 %copy-start.18 = (bf16[8,1,2,1024,128]{3,4,2,0,1:T(8,128)(2,1)S(1)}, bf16[8,1,2,1024,128]{3,4,2,0,1:T(8,128)(2,1)}, u32[]{:S(2)}) copy-start(bf16[8,1,2,1024,128]{3,4,2,0,1:T(8,128)(2,1)} %copy.123) | copy-start | bytes 12582916
  298.7 3.3 copy-start.53
  308.0 13.5 %copy-start.17 = (bf16[8,1,2,1024,128]{3,4,2,0,1:T(8,128)(2,1)S(1)}, bf16[8,1,2,1024,128]{3,4,2,0,1:T(8,128)(2,1)}, u32[]{:S(2)}) copy-start(bf16[8,1,2,1024,128]{3,4,2,0,1:T(8,128)(2,1)} %copy.122) | copy-start | bytes 12582916
  321.5 6.3 copy-start.5
  321.5 15.9 %slice-start.2 = ((s8[8388608]{0:T(1024)(128)(4,1)}), s8[4194304]{0:T(1024)(128)(4,1)S(1)}, s32[]{:S(2)}) async-start(s8[8388608]{0:T(1024)(128)(4,1)} %bitcast.381), calls=%async_computation.6 | async-start | bytes 8388608
  327.4 10.1 %slice-start.3 = ((s8[8388608]{0:T(1024)(128)(4,1)}), s8[4194304]{0:T(1024)(128)(4,1)S(1)}, s32[]{:S(2)}) async-start(s8[8388608]{0:T(1024)(128)(4,1)} %bitcast.381), calls=%async_computation.7 | async-start | bytes 8388608
  327.4 27.3 %collective-permute-start.2 = (bf16[1024,1024]{0,1:T(8,128)(2,1)}, bf16[1024,1024]{0,1:T(8,128)(2,1)}, u32[]{:S(2)}, u32[]{:S(2)}) collective-permute-start(bf16[1024,1024]{0,1:T(8,128)(2,1)} %convolution_convert_fusion), channel_id=1, source_target_pairs={{0,1},{1,0},{2,3},{3,2},{4,5},{5,4},{6,7},{7,6},{8,9},{9,8},{10,11... | collective-permute-start | bytes 6291464 | tf_op jit(solution)/shard_map/ppermute | solution.py:397
  337.4 22.3 %collective-permute-start.1 = (bf16[1024,1024]{0,1:T(8,128)(2,1)}, bf16[1024,1024]{0,1:T(8,128)(2,1)}, u32[]{:S(2)}, u32[]{:S(2)}) collective-permute-start(bf16[1024,1024]{0,1:T(8,128)(2,1)} %convolution_convert_fusion.1), channel_id=1, source_target_pairs={{0,1},{1,0},{2,3},{3,2},{4,5},{5,4},{6,7},{7,6},{8,9},{9,8},{10,11... | collective-permute-start | bytes 6291464 | tf_op jit(solution)/shard_map/ppermute | solution.py:397
  354.7 5.0 copy-start.6
  354.7 5.3 copy-start.24
  360.0 9.3 %copy-start.29 = (bf16[64,8,4,256]{3,1,2,0:T(8,128)(2,1)S(1)}, bf16[64,8,4,256]{3,1,2,0:T(8,128)(2,1)}, u32[]{:S(2)}) copy-start(bf16[64,8,4,256]{3,1,2,0:T(8,128)(2,1)} %copy-done.28) | copy-start | bytes 3145732
  377.1 6.2 copy-start.27
  377.1 6.2 copy-start.31
  377.1 11.0 %slice-start = ((s8[8388608]{0:T(1024)(128)(4,1)}), s8[4194304]{0:T(1024)(128)(4,1)S(1)}, s32[]{:S(2)}) async-start(s8[8388608]{0:T(1024)(128)(4,1)} %bitcast.292), calls=%async_computation.4 | async-start | bytes 8388608
  383.3 4.8 slice-start.1
  393.2 4.6 copy-start.39
  393.2 4.6 copy-start.45
  421.3 8.4 %copy-start.21 = (bf16[1024,4,128]{2,0,1:T(8,128)(2,1)S(1)}, bf16[1024,4,128]{2,0,1:T(8,128)(2,1)}, u32[]{:S(2)}) copy-start(bf16[1024,4,128]{2,0,1:T(8,128)(2,1)} %copy.144) | copy-start | bytes 3145732
  428.2 3.7 copy-start.19
  428.2 140.3 %collective-permute-start.3 = (bf16[1024,1024]{0,1:T(8,128)(2,1)}, bf16[1024,1024]{0,1:T(8,128)(2,1)}, u32[]{:S(2)}, u32[]{:S(2)}) collective-permute-start(bf16[1024,1024]{0,1:T(8,128)(2,1)} %add_convert_fusion), channel_id=1, source_target_pairs={{0,1},{1,0},{2,3},{3,2},{4,5},{5,4},{6,7},{7,6},{8,9},{9,8},{10,11... | collective-permute-start | bytes 6291464 | tf_op jit(solution)/shard_map/ppermute | solution.py:397
  563.8 4.7 copy-start.3
  568.5 6.4 copy-start.9
  568.5 6.4 copy-start.10
  568.5 6.4 copy-start.43
  568.5 6.4 copy-start.46
  596.5 56.2 %copy-start.1 = (bf16[64,512]{1,0:T(8,128)(2,1)S(1)}, bf16[64,512]{1,0:T(8,128)(2,1)}, u32[]{:S(2)}) copy-start(bf16[64,512]{1,0:T(8,128)(2,1)} %param.16) | copy-start | bytes 196612
  (17 other events, 39.8 us)
Sparse Core Ops, SparseCore 0:
  55.2 13.2 all-gather.3
  255.9 9.7 all-gather.5
  575.0 75.0 reduce-scatter.3

commit v3 on v1

--- a/solution.py
+++ b/solution.py
@@ -1,6 +1,8 @@
 import jax
 import jax.numpy as jnp
 from jax import lax
+from jax.experimental import pallas as pl
+from jax.experimental.pallas import tpu as pltpu
 from jax.sharding import PartitionSpec as P
 
 HD = 64
@@ -30,7 +32,7 @@
     return inv * scaled - values * (inv * inv * inv) * dot, grad_gain
 
 
-def shards(
+def plain(
     tokens,
     routed,
     w_query,
@@ -186,6 +188,1195 @@
         own[:, b6 + 1],
         own[:, b6 + 2],
     )
+
+
+MESH = pl.DeviceIdType.MESH
+NB = 48
+PATTERN = "XYZX"
+PER = 4
+LAGS = (0, 3, 6, 9, 12, 15)
+
+
+class Place:
+    def __init__(self):
+        me = lax.axis_index("dp")
+        self.x = me % 2
+        self.y = (me // 2) % 2
+        self.z = me // 4
+        self.nx = me + 1 - 2 * self.x
+        self.ny = me + 2 - 4 * self.y
+        self.up = jnp.minimum(me + 4, 15)
+        self.dn = jnp.maximum(me - 4, 0)
+        self.t = lax.axis_index("tensor")
+
+
+def both(a, b):
+    return jnp.logical_and(a, b)
+
+
+def barrier(p, core):
+    bar = pltpu.get_barrier_semaphore()
+
+    def greet(dev):
+        pl.semaphore_signal(bar, inc=1, device_id=dev, device_id_type=MESH)
+
+    greet({"dp": p.nx})
+    greet({"dp": p.ny})
+    if core:
+        greet({"tensor": 1 - p.t})
+
+    @pl.when(p.z < 3)
+    def _():
+        greet({"dp": p.up})
+
+    @pl.when(p.z > 0)
+    def _():
+        greet({"dp": p.dn})
+
+    inner = both(p.z > 0, p.z < 3)
+    base = 4 if core else 3
+
+    @pl.when(inner)
+    def _():
+        pl.semaphore_wait(bar, base + 1)
+
+    @pl.when(jnp.logical_not(inner))
+    def _():
+        pl.semaphore_wait(bar, base)
+
+
+class Steps:
+    def step(self, s, pos, static=None, guard=False):
+        live = [j for j in (5, 4, 3, 2, 1, 0) if static is None or 0 <= static - LAGS[j] < NB]
+
+        def do(j, act):
+            b = s - LAGS[j]
+            if guard:
+                pl.when(b < NB)(lambda: act(b, (pos - LAGS[j]) % PER, j))
+            else:
+                act(b, (pos - LAGS[j]) % PER, j)
+
+        for j in live:
+            if j > 0:
+                do(j, lambda b, q, j: self.recv(b, q, j - 1))
+        for j in live:
+            if j < 5:
+                do(j, self.send)
+
+    def drain(self, nb=NB):
+        def body(r, _):
+            for pos in range(PER):
+                for j in range(5):
+                    self.send(r * PER + pos, pos, j, act=lambda d: d.wait_send())
+            return 0
+
+        lax.fori_loop(0, nb // PER, body, 0)
+
+
+class Gather(Steps):
+    def __init__(self, p, W, ss, rs):
+        self.p, self.W, self.ss, self.rs = p, W, ss, rs
+
+    def copy(self, ref, b, k, dev):
+        return pltpu.make_async_remote_copy(
+            ref, ref, self.ss.at[b, k], self.rs.at[b, k], device_id={"dp": dev}, device_id_type=MESH
+        )
+
+    def zref(self, b, c, zz):
+        zz = jnp.clip(zz, 0, 3)
+        return self.W.at[b, zz] if c == "Z" else self.W.at[b, zz, self.p.y, self.p.x]
+
+    def zsend(self, b, c, hop, act):
+        p = self.p
+
+        @pl.when(both(p.z - hop + 1 >= 0, p.z < 3))
+        def _():
+            act(self.copy(self.zref(b, c, p.z - hop + 1), b, hop - 1, p.up))
+
+        @pl.when(both(p.z + hop - 1 <= 3, p.z > 0))
+        def _():
+            act(self.copy(self.zref(b, c, p.z + hop - 1), b, 2 + hop, p.dn))
+
+    def zrecv(self, b, c, hop):
+        p = self.p
+
+        @pl.when(p.z - hop >= 0)
+        def _():
+            self.copy(self.zref(b, c, p.z - hop), b, hop - 1, p.nx).wait_recv()
+
+        @pl.when(p.z + hop <= 3)
+        def _():
+            self.copy(self.zref(b, c, p.z + hop), b, 2 + hop, p.nx).wait_recv()
+
+    def stage(self, b, c, j):
+        W = self.W
+        x, y, z = self.p.x, self.p.y, self.p.z
+        if c == "X":
+            line = (7, W.at[b, :, :, x], W.at[b, :, :, 1 - x])
+            return (1, 2, 3, (6, W.at[b, :, y, x], W.at[b, :, 1 - y, x]), line)[j]
+        if c == "Y":
+            line = (6, W.at[b, :, y], W.at[b, :, 1 - y])
+            return (1, 2, 3, (7, W.at[b, :, y, x], W.at[b, :, y, 1 - x]), line)[j]
+        line = (7, W.at[b, z, y, x], W.at[b, z, y, 1 - x])
+        return (line, (6, W.at[b, z, y], W.at[b, z, 1 - y]), 1, 2, 3)[j]
+
+    def send(self, b, pos, j, act=lambda d: d.start()):
+        c = PATTERN[pos]
+        st = self.stage(b, c, j)
+        if isinstance(st, int):
+            self.zsend(b, c, st, act)
+        else:
+            act(self.copy(st[1], b, st[0], self.p.ny if st[0] == 6 else self.p.nx))
+
+    def recv(self, b, pos, j):
+        c = PATTERN[pos]
+        st = self.stage(b, c, j)
+        if isinstance(st, int):
+            self.zrecv(b, c, st)
+        else:
+            self.copy(st[2], b, st[0], self.p.nx).wait_recv()
+
+
+class Scatter(Steps):
+    def __init__(self, p, G, out, L8, L4, LZ, P4, P2, P1, ss, rs):
+        self.p, self.G, self.out, self.ss, self.rs = p, G, out, ss, rs
+        self.L8, self.L4, self.LZ, self.P4, self.P2, self.P1 = L8, L4, LZ, P4, P2, P1
+
+    def slot(self, b, pos):
+        r = b // PER
+        return r if PATTERN[pos] == "Z" else r * 3 + {0: 0, 1: 1, 3: 2}[pos]
+
+    def copy(self, src, dst, b, k, dev):
+        return pltpu.make_async_remote_copy(
+            src, dst, self.ss.at[b, k], self.rs.at[b, k], device_id={"dp": dev}, device_id_type=MESH
+        )
+
+    def gz(self, b, c, t):
+        t = jnp.clip(t, 0, 3)
+        return self.G.at[b, t] if c == "Z" else self.G.at[b, t, self.p.y, self.p.x]
+
+    def lz(self, b, pos, k):
+        i = self.slot(b, pos)
+        return self.P4.at[i, k] if PATTERN[pos] == "Z" else self.LZ.at[i, k]
+
+    def add(self, ref, land):
+        ref[...] = (ref[...].astype(jnp.float32) + land[...].astype(jnp.float32)).astype(ref.dtype)
+
+    def zsend(self, b, pos, hop, act):
+        p, c = self.p, PATTERN[pos]
+
+        @pl.when(p.z + hop <= 3)
+        def _():
+            act(self.copy(self.gz(b, c, p.z + hop), self.lz(b, pos, hop - 1), b, hop - 1, p.up))
+
+        @pl.when(p.z - hop >= 0)
+        def _():
+            act(self.copy(self.gz(b, c, p.z - hop), self.lz(b, pos, 2 + hop), b, 2 + hop, p.dn))
+
+    def zrecv(self, b, pos, hop, final):
+        p, c = self.p, PATTERN[pos]
+
+        def take(k, t):
+            land = self.lz(b, pos, k)
+            self.copy(land, land, b, k, p.nx).wait_recv()
+            if not final:
+                self.add(self.gz(b, c, t), land)
+
+        if not final:
+
+            @pl.when(both(p.z >= 1, p.z - 1 + hop <= 3))
+            def _():
+                take(hop - 1, p.z - 1 + hop)
+
+            @pl.when(both(p.z <= 2, p.z + 1 - hop >= 0))
+            def _():
+                take(2 + hop, p.z + 1 - hop)
+
+            return
+        own = self.G.at[b, p.z, p.y, p.x]
+        below, above = self.lz(b, pos, 0), self.lz(b, pos, 3)
+        f32 = jnp.float32
+
+        @pl.when(p.z == 0)
+        def _():
+            take(3, p.z)
+            self.out[b] = own[...].astype(f32) + above[...].astype(f32)
+
+        @pl.when(p.z == 3)
+        def _():
+            take(0, p.z)
+            self.out[b] = own[...].astype(f32) + below[...].astype(f32)
+
+        @pl.when(both(p.z > 0, p.z < 3))
+        def _():
+            take(0, p.z)
+            take(3, p.z)
+            self.out[b] = own[...].astype(f32) + below[...].astype(f32) + above[...].astype(f32)
+
+    def stage(self, b, pos, j):
+        G = self.G
+        x, y, z = self.p.x, self.p.y, self.p.z
+        c, i = PATTERN[pos], self.slot(b, pos)
+        if c == "X":
+            first = (7, G.at[b, :, :, 1 - x], self.L8.at[i], G.at[b, :, :, x])
+            return (first, (6, G.at[b, :, 1 - y, x], self.L4.at[i], G.at[b, :, y, x]), 3, 2, 1)[j]
+        if c == "Y":
+            first = (6, G.at[b, :, 1 - y], self.L8.at[i], G.at[b, :, y])
+            return (first, (7, G.at[b, :, y, 1 - x], self.L4.at[i], G.at[b, :, y, x]), 3, 2, 1)[j]
+        last = (7, G.at[b, z, y, 1 - x], self.P1.at[i], G.at[b, z, y, x])
+        return (3, 2, 1, (6, G.at[b, z, 1 - y], self.P2.at[i], G.at[b, z, y]), last)[j]
+
+    def send(self, b, pos, j, act=lambda d: d.start()):
+        st = self.stage(b, pos, j)
+        if isinstance(st, int):
+            self.zsend(b, pos, st, act)
+        else:
+            act(self.copy(st[1], st[2], b, st[0], self.p.ny if st[0] == 6 else self.p.nx))
+
+    def recv(self, b, pos, j):
+        st = self.stage(b, pos, j)
+        if isinstance(st, int):
+            self.zrecv(b, pos, st, PATTERN[pos] != "Z" and j == 4)
+        else:
+            self.copy(st[2], st[2], b, st[0], self.p.nx).wait_recv()
+            if j == 4:
+                self.out[b] = st[3][...].astype(jnp.float32) + st[2][...].astype(jnp.float32)
+            else:
+                self.add(st[3], st[2])
+
+    @staticmethod
+    def landing(blocks, tail, dtype):
+        n, m = blocks // PER * 3, blocks // PER
+        return [
+            pltpu.VMEM(shape + tail, dtype)
+            for shape in ((n, 4, 2), (n, 4), (n, 6), (m, 6, 2, 2), (m, 2), (m,))
+        ] + [pltpu.SemaphoreType.DMA((blocks, 8))] * 2
+EPS = 1e-05
+SEQ = 4
+CAP = 256
+ROWS = SEQ * CAP
+HBM = pl.ANY
+
+
+def dot(a, b):
+    return jnp.dot(a, b, preferred_element_type=jnp.float32)
+
+
+def dot_nt(a, b):
+    return lax.dot_general(a, b, (((1,), (1,)), ((), ())), preferred_element_type=jnp.float32)
+
+
+def halves(ref, rs):
+    return jnp.concatenate([ref[0, rs, :], ref[1, rs, :]], 1).astype(jnp.float32)
+
+
+def wblocks(W, first, count):
+    return jnp.concatenate([W[first + i].reshape(1024, 128) for i in range(count)], 1)
+
+
+def seq_rows(i):
+    return pl.ds(i * CAP, CAP)
+
+
+def cut(i, n):
+    return pl.ds(pl.multiple_of(i * n, n), n)
+
+
+def head_masks():
+    lane = lax.broadcasted_iota(jnp.int32, (CAP, 128), 1)
+    one = jnp.where(lane < HD, 1.0, 0.0)
+    return [one.astype(jnp.bfloat16), (1.0 - one).astype(jnp.bfloat16)], lane < HD
+
+
+def causal_mask():
+    shape = (CAP, CAP)
+    return lax.broadcasted_iota(jnp.int32, shape, 0) >= lax.broadcasted_iota(jnp.int32, shape, 1)
+
+
+def softmax_rows(q, k, mask):
+    s = jnp.where(mask, dot_nt(q, k) * (HD**-0.5), -1e30)
+    e = jnp.exp(s - jnp.max(s, -1, keepdims=True))
+    return e * (1.0 / jnp.sum(e, -1, keepdims=True))
+
+
+def inv_rms(v):
+    return lax.rsqrt(jnp.mean(v * v, -1, keepdims=True) + EPS)
+
+
+def gate_of(rows_f, route):
+    return jax.nn.sigmoid(jnp.sum(rows_f * route, -1, keepdims=True))
+
+
+def own_slot(p, W, b):
+    return W.at[b, p.z, p.y, p.x]
+
+
+def forward_kernel(
+    idx_ref,
+    tile_ref,
+    tok_ref,
+    cot_ref,
+    wq,
+    wk,
+    wv,
+    wo,
+    wu,
+    wd,
+    o_rows,
+    o_cot,
+    o_nT,
+    o_qkv,
+    o_mix,
+    o_P,
+    o_R,
+    o_down,
+    o_back,
+    o_W,
+    o_G,
+    o_vec,
+    W,
+    VB,
+    vecs,
+    rows,
+    cot,
+    tokbuf,
+    onehot,
+    nrm,
+    nT,
+    dd,
+    ddT,
+    qkv,
+    mixed,
+    P,
+    R,
+    dacc,
+    nacc,
+    act,
+    dup,
+    u32,
+    d32,
+    Gst,
+    ss,
+    rs,
+    vss,
+    vrs,
+    hs,
+    hr,
+    asnd,
+    arcv,
+    first,
+    load,
+    outs,
+    gout,
+):
+    p = Place()
+    t = p.t
+    other = {"tensor": 1 - t}
+    f32, bf = jnp.float32, jnp.bfloat16
+
+    own = [pltpu.make_async_copy(tile_ref, own_slot(p, VB, 0), first.at[NB])]
+    for b in range(16):
+        src = (wq, wk, wv, wo)[b // 4]
+        own.append(
+            pltpu.make_async_copy(
+                src.at[:, pl.ds(b % 4 * 128, 128)], own_slot(p, W, b), first.at[b]
+            )
+        )
+    for b in range(32):
+        src = (wu, wd)[b % 4 // 2]
+        own.append(
+            pltpu.make_async_copy(
+                src.at[:, pl.ds((b // 4 * 2 + b % 2) * 128, 128)],
+                own_slot(p, W, 16 + b),
+                first.at[16 + b],
+            )
+        )
+    for c in own:
+        c.start()
+
+    units = [(a, i) for i in range(SEQ) for a in (0, 1)]
+
+    def loader(u):
+        a, i = units[u]
+        return pltpu.make_async_copy((tok_ref, cot_ref)[a].at[i], tokbuf.at[u % 2], load.at[u % 2])
+
+    loader(0).start()
+    loader(1).start()
+    barrier(p, True)
+    for c in own:
+        c.wait()
+    W_steps = Gather(p, W, ss, rs)
+    V_steps = Gather(p, VB, vss, vrs)
+
+    def tick(s, guard=False):
+        if isinstance(s, int):
+            W_steps.step(s, s % PER, static=s)
+            if s in LAGS:
+                j = LAGS.index(s)
+                if j > 0:
+                    V_steps.recv(0, 0, j - 1)
+                if j < 5:
+                    V_steps.send(0, 0, j)
+
+    def half_copy(u):
+        a, i = units[u]
+        ref = (rows, cot)[a].at[t, seq_rows(i)]
+        return pltpu.make_async_remote_copy(
+            ref, ref, hs.at[u], hr.at[u], device_id=other, device_id_type=MESH
+        )
+
+    def half_wait(u):
+        a, i = units[u]
+        ref = (rows, cot)[a].at[1 - t, seq_rows(i)]
+        pltpu.make_async_remote_copy(
+            ref, ref, hs.at[u], hr.at[u], device_id=other, device_id_type=MESH
+        ).wait_recv()
+
+    for u, (a, i) in enumerate(units):
+        tick(2 * u)
+        if a == 0:
+            spot = idx_ref[seq_rows(i), :]
+            hit = lax.broadcasted_iota(jnp.int32, (CAP, 2048), 1) == spot
+            onehot[...] = jnp.where(hit, 1.0, 0.0).astype(bf)
+        loader(u).wait()
+        (rows, cot)[a][t, seq_rows(i), :] = dot(onehot[...], tokbuf[u % 2]).astype(bf)
+        if u + 2 < 8:
+            loader(u + 2).start()
+        tick(2 * u + 1)
+        if u > 0:
+            half_copy(u - 1).start()
+    half_copy(7).start()
+
+    for z in range(4):
+        for y in range(2):
+            vecs[:, pl.ds((z * 2 + y) * 128, 128)] = VB[0, z, y, 0] + VB[0, z, y, 1]
+
+    def saver(k, src, dst):
+        return pltpu.make_async_copy(src, dst, outs.at[k])
+
+    saved = [saver(0, vecs, o_vec)]
+    saved[0].start()
+
+    dacc[...] = jnp.zeros_like(dacc)
+    nacc[...] = jnp.zeros_like(nacc)
+
+    for i in range(SEQ):
+        tick(16 + i)
+        half_wait(2 * i)
+        half_wait(2 * i + 1)
+
+        def norm_part(n, _):
+            rs_ = cut(i * 8 + n, 32)
+            r = halves(rows, rs_)
+            nrm[rs_, :] = (r * inv_rms(r) * vecs[1:2, :]).astype(bf)
+            dd[rs_, :] = (gate_of(r, vecs[0:1, :]) * halves(cot, rs_)).astype(bf)
+            return 0
+
+        lax.fori_loop(0, 8, norm_part, 0)
+        for c in range(4):
+            cs = pl.ds(c * 256, 256)
+            nT[cs, seq_rows(i)] = nrm[seq_rows(i), cs].T
+            ddT[cs, seq_rows(i)] = dd[seq_rows(i), cs].T
+    later = [saver(1, rows, o_rows), saver(2, cot, o_cot), saver(3, nT, o_nT)]
+    for c in later:
+        c.start()
+    saved += later[:2]
+    nT_saved = later[2]
+
+    def project(j):
+        y = dot(nrm[...], wblocks(W, 2 * j, 2)).astype(bf)
+        qkv[2 * j] = y[:, :128]
+        qkv[2 * j + 1] = y[:, 128:]
+
+    def project_part(n, _):
+        s = 20 + 4 * n
+        W_steps.step(s, 0)
+        W_steps.step(s + 1, 1)
+        project(3 * n)
+        W_steps.step(s + 2, 2)
+        project(3 * n + 1)
+        W_steps.step(s + 3, 3)
+        project(3 * n + 2)
+        return 0
+
+    lax.fori_loop(0, 2, project_part, 0)
+    saved.append(saver(4, qkv, o_qkv))
+    saved[-1].start()
+
+    masks, low_half = head_masks()
+    mask = causal_mask()
+
+    def attend(i, hp):
+        r_ = cut(i, CAP)
+        q, k, v = qkv[hp, r_, :], qkv[4 + hp, r_, :], qkv[8 + hp, r_, :]
+        mix = [dot(softmax_rows(q * masks[h], k, mask).astype(bf), v) for h in (0, 1)]
+        mixed[hp, r_, :] = jnp.where(low_half, mix[0], mix[1]).astype(bf)
+
+    def attend_part(n, _):
+        for q in range(4):
+            W_steps.step(28 + 4 * n + q, q)
+
+            def pair(e, _):
+                attend(2 * n + q // 2, q % 2 * 2 + e)
+                return 0
+
+            lax.fori_loop(0, 2, pair, 0)
+        return 0
+
+    lax.fori_loop(0, 2, attend_part, 0)
+    saved.append(saver(5, mixed, o_mix))
+    saved[-1].start()
+
+    def att_copy(i):
+        return pltpu.make_async_remote_copy(
+            P.at[seq_rows(i)],
+            R.at[seq_rows(i)],
+            asnd.at[i],
+            arcv.at[i],
+            device_id=other,
+            device_id_type=MESH,
+        )
+
+    for i in range(SEQ):
+        W_steps.step(36 + i, i)
+        mix = jnp.concatenate([mixed[h, seq_rows(i), :] for h in range(4)], 1)
+        P[seq_rows(i), :] = dot_nt(mix, wblocks(W, 12, 4)).astype(bf)
+        if i > 0:
+            att_copy(i - 1).start()
+    nT_saved.wait()
+    saved.append(saver(6, W.at[pl.ds(0, 16)], o_W))
+    saved[-1].start()
+    att_copy(3).start()
+    for i in range(SEQ):
+        att_copy(i).wait_recv()
+
+        def norm_part(n, _):
+            rs_ = cut(i * 8 + n, 32)
+            h = halves(rows, rs_) + (P[rs_, :].astype(f32) + R[rs_, :].astype(f32))
+            nrm[rs_, :] = (h * inv_rms(h) * vecs[2:3, :]).astype(bf)
+            return 0
+
+        lax.fori_loop(0, 8, norm_part, 0)
+        for c in range(4):
+            cs = pl.ds(c * 256, 256)
+            nT[cs, seq_rows(i)] = nrm[seq_rows(i), cs].T
+    later = [saver(7, P, o_P), saver(8, R, o_R)]
+    for c in later:
+        c.start()
+    saved += later
+
+    def g_copy(m):
+        slot = lax.rem(m, 2)
+        return pltpu.make_async_copy(Gst.at[slot], o_G.at[pl.ds(m * 4, 4)], gout.at[slot])
+
+    def mlp_part(m, _):
+        slot = lax.rem(m, 2)
+        s = 40 + 4 * m
+        up_w = wblocks(W, 16 + 4 * m, 2)
+        down_w = wblocks(W, 18 + 4 * m, 2)
+        for ht in range(2):
+            hs_ = pl.ds(ht * 512, 512)
+            W_steps.step(s + 2 * ht, 2 * ht, guard=True)
+            u32[...] = dot(nrm[hs_, :], up_w)
+            d32[...] = dot(dd[hs_, :], down_w)
+
+            def gelu_part(n, _):
+                rs_ = cut(n, 32)
+                out_ = pl.ds(pl.multiple_of(ht * 512 + n * 32, 32), 32)
+                u = u32[rs_, :]
+                c0 = 0.7978845608028654
+                u2 = u * u
+                th = jnp.tanh(c0 * (u + 0.044715 * (u * u2)))
+                cdf = 0.5 * (1.0 + th)
+                act[out_, :] = (u * cdf).astype(bf)
+                slope = cdf + 0.5 * u * (1.0 - th * th) * (c0 + (3 * 0.044715 * c0) * u2)
+                dup[out_, :] = (d32[rs_, :] * slope).astype(bf)
+                return 0
+
+            lax.fori_loop(0, 16, gelu_part, 0)
+            W_steps.step(s + 2 * ht + 1, 2 * ht + 1, guard=True)
+            dacc[hs_, :] += dot_nt(act[hs_, :], down_w)
+            nacc[hs_, :] += dot_nt(dup[hs_, :], up_w)
+
+        @pl.when(m >= 2)
+        def _():
+            g_copy(m - 2).wait()
+
+        for ht in range(2):
+            hs_ = pl.ds(ht * 512, 512)
+            gu = dot(nT[hs_, :], dup[...]).astype(bf)
+            Gst[slot, 0, hs_, :] = gu[:, :128]
+            Gst[slot, 1, hs_, :] = gu[:, 128:]
+            gd = dot(ddT[hs_, :], act[...]).astype(bf)
+            Gst[slot, 2, hs_, :] = gd[:, :128]
+            Gst[slot, 3, hs_, :] = gd[:, 128:]
+        g_copy(m).start()
+        return 0
+
+    lax.fori_loop(0, 8, mlp_part, 0)
+    for e in range(2):
+        for c in range(2):
+            tokbuf[e, pl.ds(c * 1024, 1024), :] = (dacc, nacc)[e][:, c * 512 : c * 512 + 512].astype(bf)
+            saved.append(
+                saver(9 + 2 * e + c, tokbuf.at[e, pl.ds(c * 1024, 1024)], (o_down, o_back)[e].at[c])
+            )
+            saved[-1].start()
+    for u in range(8):
+        half_copy(u).wait_send()
+    for i in range(SEQ):
+        att_copy(i).wait_send()
+    W_steps.drain()
+    for j in range(5):
+        V_steps.send(0, 0, j, act=lambda d: d.wait_send())
+    g_copy(6).wait()
+    g_copy(7).wait()
+    for c in saved:
+        c.wait()
+
+
+def forward_call(chosen, tile, tok, cotangent, weights):
+    bf, f32 = jnp.bfloat16, jnp.float32
+    S = jax.ShapeDtypeStruct
+    DMA = pltpu.SemaphoreType.DMA
+    any_ = pl.BlockSpec(memory_space=HBM)
+    vm = pltpu.VMEM
+    return pl.pallas_call(
+        forward_kernel,
+        out_shape=(
+            S((2, ROWS, 512), bf),
+            S((2, ROWS, 512), bf),
+            S((1024, ROWS), bf),
+            S((12, ROWS, 128), bf),
+            S((4, ROWS, 128), bf),
+            S((ROWS, 1024), bf),
+            S((ROWS, 1024), bf),
+            S((2, ROWS, 512), bf),
+            S((2, ROWS, 512), bf),
+            S((16, 4, 2, 2, 64, 128), bf),
+            S((32, 1024, 128), bf),
+            S((8, 1024), f32),
+        ),
+        in_specs=[pl.BlockSpec(memory_space=pltpu.VMEM)] + [any_] * 9,
+        out_specs=[any_] * 12,
+        scratch_shapes=[
+            vm((NB, 4, 2, 2, 64, 128), bf),
+            vm((1, 4, 2, 2, 8, 128), f32),
+            vm((8, 1024), f32),
+            vm((2, ROWS, 512), bf),
+            vm((2, ROWS, 512), bf),
+            vm((2, 2048, 512), bf),
+            vm((CAP, 2048), bf),
+            vm((ROWS, 1024), bf),
+            vm((1024, ROWS), bf),
+            vm((ROWS, 1024), bf),
+            vm((1024, ROWS), bf),
+            vm((12, ROWS, 128), bf),
+            vm((4, ROWS, 128), bf),
+            vm((ROWS, 1024), bf),
+            vm((ROWS, 1024), bf),
+            vm((ROWS, 1024), f32),
+            vm((ROWS, 1024), f32),
+            vm((ROWS, 256), bf),
+            vm((ROWS, 256), bf),
+            vm((512, 256), f32),
+            vm((512, 256), f32),
+            vm((2, 4, 1024, 128), bf),
+            DMA((NB, 8)),
+            DMA((NB, 8)),
+            DMA((1, 8)),
+            DMA((1, 8)),
+            DMA((8,)),
+            DMA((8,)),
+            DMA((4,)),
+            DMA((4,)),
+            DMA((NB + 1,)),
+            DMA((2,)),
+            DMA((13,)),
+            DMA((2,)),
+        ],
+        compiler_params=pltpu.CompilerParams(
+            collective_id=1, has_side_effects=True, vmem_limit_bytes=63 * 1024 * 1024
+        ),
+        name="forward",
+    )(chosen, tile, tok, cotangent, *weights)
+
+
+def backward_kernel(
+    spot_ref,
+    rows,
+    cot,
+    nT_in,
+    qkv_in,
+    mix_in,
+    P_in,
+    R_in,
+    down_in,
+    back_in,
+    W_in,
+    G_in,
+    vec_in,
+    tok_ref,
+    cot_ref,
+    o_tok,
+    o_cot,
+    o_sum,
+    o_vec,
+    G,
+    Wa,
+    qkv,
+    mixed,
+    nT,
+    vecs,
+    DR,
+    NR,
+    R1,
+    bufs,
+    buf2,
+    da,
+    daT,
+    dmix,
+    newr,
+    newg,
+    dhid,
+    dlog,
+    accs,
+    GV,
+    base,
+    gsem,
+    lsem,
+    psem,
+    prcv,
+    qsem,
+    qrcv,
+    tin,
+    tout,
+    *landing,
+):
+    p = Place()
+    t = p.t
+    other = {"tensor": 1 - t}
+    f32, bf = jnp.float32, jnp.bfloat16
+    wide, small = landing[:8], landing[8:]
+
+    g_loads = [
+        pltpu.make_async_copy(G_in.at[pl.ds(4 * c, 4)], G.at[pl.ds(4 * c, 4)], gsem.at[c])
+        for c in range(8)
+    ]
+    g_loads[0].start()
+
+    def stream(s, names):
+        q = s % 2
+        out = []
+        for k in names:
+            if k < 2:
+                src = (P_in, R_in)[k].at[seq_rows(s)]
+                dst = buf2.at[q, k]
+            else:
+                src = (rows, cot, down_in, back_in)[k - 2].at[:, seq_rows(s)]
+                dst = bufs.at[q, k - 2]
+            out.append(pltpu.make_async_copy(src, dst, lsem.at[q, k]))
+        return out
+
+    everything = (0, 1, 2, 3, 4, 5)
+    for c in stream(0, everything):
+        c.start()
+    fixed = [
+        pltpu.make_async_copy(a, b, base.at[i])
+        for i, (a, b) in enumerate(
+            ((vec_in, vecs), (W_in, Wa), (qkv_in, qkv), (mix_in, mixed), (nT_in, nT))
+        )
+    ]
+    for c in fixed[:1]:
+        c.start()
+    for c in g_loads[1:]:
+        c.start()
+    barrier(p, True)
+
+    def pair_copy(s, e):
+        return pltpu.make_async_remote_copy(
+            (down_in, back_in)[e].at[:, seq_rows(s)],
+            (DR, NR)[e].at[:, seq_rows(s)],
+            psem.at[s, e],
+            prcv.at[s, e],
+            device_id=other,
+            device_id_type=MESH,
+        )
+
+    for s in range(SEQ):
+        for e in range(2):
+            pair_copy(s, e).start()
+    for c in fixed[1:]:
+        c.start()
+    steps = Scatter(p, G, o_sum, *wide)
+    v_steps = Scatter(p, GV, o_vec, *small)
+
+    def tick(s):
+        if s < 32 and s % 4 == 0:
+            g_loads[s // 4].wait()
+        steps.step(s, s % PER, static=s)
+
+    accs[...] = jnp.zeros_like(accs)
+
+    def fold(v):
+        return jnp.sum(v.reshape(4, 8, 1024), 0)
+
+    def pick(v):
+        return jnp.where(t == 0, v[:, :512], v[:, 512:])
+
+    masks, low_half = head_masks()
+    seen = lax.broadcasted_iota(jnp.int32, (CAP, CAP), 0) <= lax.broadcasted_iota(
+        jnp.int32, (CAP, CAP), 1
+    )
+
+    for s in range(SEQ):
+        tick(4 * s)
+        q = s % 2
+        if s + 1 < SEQ:
+            for c in stream(s + 1, everything):
+                c.start()
+        if s == 0:
+            fixed[0].wait()
+        for c in stream(s, everything):
+            c.wait()
+        for e in range(2):
+            pair_copy(s, e).wait_recv()
+
+        def part(n, _):
+            rs_ = cut(n, 32)
+            as_ = pl.ds(pl.multiple_of(s * CAP + n * 32, 32), 32)
+
+            def mine(k):
+                return jnp.concatenate([bufs[q, k, 0, rs_, :], bufs[q, k, 1, rs_, :]], 1).astype(f32)
+
+            r, c = mine(0), mine(1)
+            att = buf2[q, 0, rs_, :].astype(f32) + buf2[q, 1, rs_, :].astype(f32)
+            h = r + att
+            branch = att + (mine(2) + halves(DR, as_))
+            dn = mine(3) + halves(NR, as_)
+            inv = inv_rms(h)
+            sc = dn * vecs[2:3, :]
+            dh = inv * sc - h * (inv * inv * inv * jnp.mean(sc * h, -1, keepdims=True))
+            gate = gate_of(r, vecs[0:1, :])
+            dl = jnp.sum(c * branch, -1, keepdims=True) * (gate * (1.0 - gate))
+            da[rs_, :] = (gate * c + dh).astype(bf)
+            accs[2] += fold(dn * (h * inv))
+            accs[0] += fold(r * dl)
+            newr[as_, :] = pick(r + gate * branch).astype(bf)
+            dhid[as_, :] = pick(dh)
+            dlog[as_, :] = jnp.broadcast_to(dl, (32, 128))
+            return 0
+
+        lax.fori_loop(0, 8, part, 0)
+        tick(4 * s + 1)
+        for c in range(4):
+            cs = pl.ds(c * 256, 256)
+            daT[cs, seq_rows(s)] = da[:, cs].T
+        if s == 0:
+            for c in fixed[1:]:
+                c.wait()
+        dm = dot(da[...], wblocks(Wa, 12, 4)).astype(bf)
+        for h in range(4):
+            dmix[h] = dm[:, h * 128 : h * 128 + 128]
+
+        def pair_back(hp):
+            r_ = seq_rows(s)
+            qh, kh, vh, dmh = qkv[hp, r_, :], qkv[4 + hp, r_, :], qkv[8 + hp, r_, :], dmix[hp]
+            outs = []
+            for h in (0, 1):
+                sc = jnp.where(seen, dot_nt(kh, qh * masks[h]) * (HD**-0.5), -1e30)
+                e = jnp.exp(sc - jnp.max(sc, 0, keepdims=True))
+                pr = e * (1.0 / jnp.sum(e, 0, keepdims=True))
+                dv = dot(pr.astype(bf), dmh)
+                dp = dot_nt(vh * masks[h], dmh)
+                ds = (pr * (dp - jnp.sum(dp * pr, 0, keepdims=True))).astype(bf)
+                outs.append((dot(ds.T, kh), dot(ds, qh), dv))
+            scale = HD**-0.5
+            for i, (a, b) in enumerate(zip(*outs)):
+                v = jnp.where(low_half, a, b)
+                qkv[4 * i + hp, r_, :] = (v if i == 2 else v * scale).astype(bf)
+
+        for half in range(2):
+            tick(4 * s + 2 + half)
+
+            def pair_part(e, _):
+                pair_back(2 * half + e)
+                return 0
+
+            lax.fori_loop(0, 2, pair_part, 0)
+
+    def grad_unit(leftT, a, b, first):
+        y = jnp.concatenate([a, b], 1)
+        for ht in range(2):
+            g = dot(leftT[pl.ds(ht * 512, 512), :], y).astype(bf)
+            for c in range(2):
+                G[first + c, pl.ds(ht * 2, 2)] = g[:, c * 128 : c * 128 + 128].reshape(
+                    2, 2, 2, 64, 128
+                )
+
+    def back_copy(s):
+        return pltpu.make_async_remote_copy(
+            DR.at[:, seq_rows(s)],
+            R1.at[:, seq_rows(s)],
+            qsem.at[s],
+            qrcv.at[s],
+            device_id=other,
+            device_id_type=MESH,
+        )
+
+    for c in stream(0, (2, 3)):
+        c.start()
+    for c in stream(1, (2, 3)):
+        c.start()
+    for s in range(SEQ):
+        tick(16 + s)
+        x = jnp.concatenate([qkv[i, seq_rows(s), :] for i in range(12)], 1)
+        y = dot_nt(x, wblocks(Wa, 0, 12)).astype(bf)
+        DR[0, seq_rows(s), :] = y[:, :512]
+        DR[1, seq_rows(s), :] = y[:, 512:]
+        if s > 0:
+            back_copy(s - 1).start()
+    tick(20)
+    back_copy(3).start()
+    grad_unit(daT, mixed[0], mixed[1], 32)
+    tick(21)
+    grad_unit(daT, mixed[2], mixed[3], 34)
+    for g_load in g_loads[6:]:
+        g_load.wait()
+
+    def grad_part(n, _):
+        for e in range(2):
+            sn = 22 + 4 * n + 2 * e
+            steps.step(sn, (2 + 2 * e) % 4)
+            steps.step(sn + 1, (3 + 2 * e) % 4)
+            j = 2 * n + e
+            grad_unit(nT, qkv[2 * j], qkv[2 * j + 1], 36 + 2 * j)
+        return 0
+
+    lax.fori_loop(0, 2, grad_part, 0)
+    for e in range(2):
+        grad_unit(nT, qkv[8 + 2 * e], qkv[9 + 2 * e], 44 + 2 * e)
+        steps.step(30 + e, 2 + e)
+
+    route_half = jnp.where(t == 0, vecs[0:1, :512], vecs[0:1, 512:])
+    for s in range(SEQ):
+        steps.step(32 + 2 * s, 2 * s % 4)
+        steps.step(33 + 2 * s, (2 * s + 1) % 4)
+        q = s % 2
+        for c in stream(s, (2, 3)):
+            c.wait()
+        back_copy(s).wait_recv()
+
+        def part(n, _):
+            rs_ = cut(n, 32)
+            as_ = pl.ds(pl.multiple_of(s * CAP + n * 32, 32), 32)
+            r = jnp.concatenate([bufs[q, 0, 0, rs_, :], bufs[q, 0, 1, rs_, :]], 1).astype(f32)
+            dn = halves(DR, as_) + halves(R1, as_)
+            inv = inv_rms(r)
+            sc = dn * vecs[1:2, :]
+            dr = inv * sc - r * (inv * inv * inv * jnp.mean(sc * r, -1, keepdims=True))
+            accs[1] += fold(dn * (r * inv))
+            dl = dlog[as_, :]
+            dl = jnp.concatenate([dl, dl, dl, dl], 1)
+            ch = bufs[q, 1, t, rs_, :].astype(f32)
+            newg[as_, :] = (ch + (dhid[as_, :] + pick(dr) + dl * route_half)).astype(bf)
+            return 0
+
+        lax.fori_loop(0, 8, part, 0)
+        if s + 2 < SEQ:
+            for c in stream(s + 2, (2, 3)):
+                c.start()
+
+    for z in range(4):
+        for y in range(2):
+            cs = pl.ds((z * 2 + y) * 128, 128)
+            tile = jnp.concatenate(
+                [jnp.sum(accs[k, :, cs], 0, keepdims=True) for k in range(3)]
+                + [jnp.zeros((5, 128), f32)],
+                0,
+            )
+            GV[0, z, y, 0] = tile
+            GV[0, z, y, 1] = tile
+    for s in range(SEQ):
+        back_copy(s).wait_send()
+
+    def tok_in(n, a):
+        return pltpu.make_async_copy(
+            (tok_ref, cot_ref)[a].at[n // 4, cut(n % 4, 512)],
+            NR.at[a, cut(n % 2, 512)],
+            tin.at[a, n % 2],
+        )
+
+    def tok_out(n, a):
+        return pltpu.make_async_copy(
+            DR.at[a, cut(n % 2, 512)],
+            (o_tok, o_cot)[a].at[n // 4, cut(n % 4, 512)],
+            tout.at[a, n % 2],
+        )
+
+    for n in range(2):
+        for a in range(2):
+            tok_in(n, a).start()
+    v_steps.send(0, 0, 0)
+    ones = jnp.ones((CAP, 128), bf)
+
+    def place_part(m, _):
+        for e in range(4):
+            n = 4 * m + e
+            steps.step(40 + n, e, guard=True)
+            place = lax.broadcasted_iota(jnp.int32, (512, CAP), 0) + e * 512
+            hit = jnp.where(place == spot_ref[m], 1.0, 0.0).astype(bf)
+            there = dot(hit, ones)
+            there = jnp.concatenate([there, there, there, there], 1) > 0.5
+            for a in range(2):
+                tok_in(n, a).wait()
+                new = dot(hit, (newr, newg)[a][cut(m, CAP), :])
+                slot = pl.ds(e % 2 * 512, 512)
+                old = NR[a, slot, :].astype(f32)
+                if e >= 2:
+                    tok_out(n - 2, a).wait()
+                else:
+                    pl.when(m > 0)(lambda: tok_out(n - 2, a).wait())
+                DR[a, slot, :] = jnp.where(there, new, old).astype(bf)
+                tok_out(n, a).start()
+                if e < 2:
+                    tok_in(n + 2, a).start()
+                else:
+                    pl.when(m < 3)(lambda: tok_in(n + 2, a).start())
+        return 0
+
+    lax.fori_loop(0, 4, place_part, 0)
+    for k, s in enumerate(range(56, 64)):
+        tick(s)
+        if k in (0, 2, 3, 5, 7):
+            j = (0, 2, 3, 5, 7).index(k) + 1
+            v_steps.recv(0, 0, j - 1)
+            if j < 5:
+                v_steps.send(0, 0, j)
+    for n in (14, 15):
+        for a in range(2):
+            tok_out(n, a).wait()
+    for s in range(SEQ):
+        for e in range(2):
+            pair_copy(s, e).wait_send()
+    for j in range(5):
+        v_steps.send(0, 0, j, act=lambda d: d.wait_send())
+    steps.drain()
+
+
+def backward_call(spot, kept, tok, cotangent):
+    bf, f32 = jnp.bfloat16, jnp.float32
+    S = jax.ShapeDtypeStruct
+    DMA = pltpu.SemaphoreType.DMA
+    any_ = pl.BlockSpec(memory_space=HBM)
+    vspec = pl.BlockSpec(memory_space=pltpu.VMEM)
+    vm = pltpu.VMEM
+    return pl.pallas_call(
+        backward_kernel,
+        out_shape=(
+            S((SEQ, 2048, 512), bf),
+            S((SEQ, 2048, 512), bf),
+            S((NB, 64, 128), f32),
+            S((1, 8, 128), f32),
+        ),
+        in_specs=[vspec] + [any_] * 14,
+        out_specs=[any_, any_, vspec, vspec],
+        scratch_shapes=[
+            vm((NB, 4, 2, 2, 64, 128), bf),
+            vm((16, 4, 2, 2, 64, 128), bf),
+            vm((12, ROWS, 128), bf),
+            vm((4, ROWS, 128), bf),
+            vm((1024, ROWS), bf),
+            vm((8, 1024), f32),
+            vm((2, ROWS, 512), bf),
+            vm((2, ROWS, 512), bf),
+            vm((2, ROWS, 512), bf),
+            vm((2, 4, 2, CAP, 512), bf),
+            vm((2, 2, CAP, 1024), bf),
+            vm((CAP, 1024), bf),
+            vm((1024, ROWS), bf),
+            vm((4, CAP, 128), bf),
+            vm((ROWS, 512), bf),
+            vm((ROWS, 512), bf),
+            vm((ROWS, 512), f32),
+            vm((ROWS, 128), f32),
+            vm((3, 8, 1024), f32),
+            vm((1, 4, 2, 2, 8, 128), f32),
+            DMA((5,)),
+            DMA((8,)),
+            DMA((2, 6)),
+            DMA((4, 2)),
+            DMA((4, 2)),
+            DMA((4,)),
+            DMA((4,)),
+            DMA((2, 2)),
+            DMA((2, 2)),
+        ]
+        + Scatter.landing(NB, (64, 128), bf)
+        + Scatter.landing(PER, (8, 128), f32),
+        compiler_params=pltpu.CompilerParams(
+            collective_id=2, has_side_effects=True, vmem_limit_bytes=63 * 1024 * 1024
+        ),
+        name="backward",
+    )(spot, *kept, tok, cotangent)
+
+
+def to_tile(w_route, gain_attn, gain_mlp):
+    v = jnp.stack([w_route, gain_attn, gain_mlp]).astype(jnp.float32)
+    v = jnp.pad(v, ((0, 5), (0, 0)))
+    z = jnp.zeros_like(v)
+    odd = lax.axis_index("dp") % 2
+    return jnp.where(odd == 0, jnp.concatenate([v, z], 1), jnp.concatenate([z, v], 1))
+
+
+def from_blocks(x):
+    return x.transpose(1, 0, 2).reshape(x.shape[1], -1)
+
+
+def fused(
+    tokens,
+    routed,
+    w_query,
+    w_key,
+    w_value,
+    w_out,
+    w_up,
+    w_down,
+    w_route,
+    gain_attn,
+    gain_mlp,
+    cotangent,
+):
+    tok = tokens.reshape(SEQ, 2048, 512)
+    cot = cotangent.reshape(SEQ, 2048, 512)
+    tile = to_tile(w_route, gain_attn, gain_mlp)
+    weights = (w_query, w_key, w_value, w_out.T, w_up, w_down.T)
+    kept = list(forward_call(routed.reshape(ROWS, 1), tile, tok, cot, weights))
+    kept[10] = kept[10].reshape(32, 4, 2, 2, 64, 128)
+    output, grad, own, vec = backward_call(routed.reshape(SEQ, 1, CAP), kept, tok, cot)
+    mlp = own[:32].reshape(8, 2, 2, 64, 128)
+    odd = lax.axis_index("dp") % 2
+    vec = jnp.where(odd == 0, vec[0, :3, :64], vec[0, :3, 64:])
+    return (
+        output.reshape(tokens.shape),
+        grad.reshape(tokens.shape),
+        from_blocks(own[36:40]),
+        from_blocks(own[40:44]),
+        from_blocks(own[44:48]),
+        from_blocks(own[32:36]).T,
+        from_blocks(mlp[:, 0].reshape(16, 64, 128)),
+        from_blocks(mlp[:, 1].reshape(16, 64, 128)).T,
+        vec[0],
+        vec[1],
+        vec[2],
+    )
+
+
+def shards(tokens, routed, *rest):
+    sizes = (lax.axis_size("dp"), lax.axis_size("tensor"))
+    here = tokens.shape == (4, 1, 2048, 512) and routed.shape == (4, 1, 256)
+    if sizes == (16, 2) and here:
+        return fused(tokens, routed, *rest)
+    return plain(tokens, routed, *rest)
 
 
 def solution(mesh):

time: 701 us -> 311 us (0.44)
  waiting for transfers between devices: 401 us -> 0 us
  Pallas kernels: 0 us -> 280 us
  local copies, waits for them, and re-layouts: 133 us -> 22.8 us
  matrix products: 106 us -> 0 us
  other arithmetic: 35.1 us -> 2.2 us
  between operations: 14.7 us -> 1.15 us
    pallas_call x0 -> x2, Pallas kernels: none -> 280 us  [the longest x1 144 us: forward_call(): pl.pallas_call(forward_kernel, out_shape=(S((2, ROWS, 512), bf), S((2, RO...]
    reduce_scatter x1 -> x0, waiting for transfers between devices: 230 us -> none  [shards(): lax.psum_scatter(grads, 'dp', scatter_dimension=0, tiled=True)]
    all_gather x3 -> x0, waiting for transfers between devices: 168 us -> none  [the longest x1 156 us: shards(): gathered = lax.all_gather(packed, 'dp', axis=0, tiled=True)]
    dot_general x25 -> x0, matrix products: 106 us -> none  [the longest x7 36.8 us: dense(): return jnp.dot(left, right, preferred_element_type=jnp.float32)]
    unnamed x102 -> x3, local copies, waits for them, and re-layouts: 63.8 us -> 15.8 us
    gather x4 -> x0, local copies, waits for them, and re-layouts: 35.9 us -> none  [the longest x2 20.9 us: shards(): jnp.take_along_axis(cot, chosen[:, :, None], axis=1)]
    convert_element_type x13 -> x0, local copies, waits for them, and re-layouts: 18.5 us -> none  [the longest x4 7.51 us: split(): x.astype(jnp.bfloat16).reshape(batch, capacity, heads, HD)]
    convert_element_type x6 -> x0, other arithmetic: 17.4 us -> none  [the longest x1 7.97 us: shards(): d_attended = (d_branch + d_hidden).astype(jnp.bfloat16)]
  transfers between devices with their start and end apart: 8 -> 0, of which waited for: 5 -> 0; matrix products, arithmetic and copies ran while one was open for 15% -> 0% of each run, Pallas kernels for 0% -> 0%
where the time goes in v3:
time: 311 us; the launch traced here: 306 us
  Pallas kernels  280 us (90%)
  local copies, waits for them, and re-layouts  22.8 us (7%)
    pallas_call x1, Pallas kernels, forward_call(): pl.pallas_call(forward_kernel, out_shape=(S((2, ROWS, 512), bf), S((2, RO...  144 us
    pallas_call x1, Pallas kernels, backward_call(): pl.pallas_call(backward_kernel, out_shape=(S((SEQ, 2048, 512), bf), S((SE...  136 us
    unnamed x3, local copies, waits for them, and re-layouts  15.8 us

profile of v3, /device:TPU:0, one launch (start us, length us, event | category | flops | bytes accessed | tf_op | source)
XLA Modules:
  0.0 306.3 jit_solution(1409976474959475428)
XLA Ops:
  0.7 0.7 fusion.5
  1.4 0.7 pad_select_fusion.tile_ref
  2.0 1.7 copy.27.idx_ref
  3.7 144.0 %forward.1 = (bf16[2,1024,512]{2,1,0:T(8,128)(2,1)}, bf16[2,1024,512]{2,1,0:T(8,128)(2,1)}, bf16[1024,1024]{1,0:T(8,128)(2,1)}, bf16[12,1024,128]{2,1,0:T(8,128)...) custom-call(s32[1024,1]{1,0:T(8,128)} %copy.27.idx_ref, ...), custom_call_target="tpu_custom_call" | custom-call | tf_op jit(solution)/shard_map/forward/pallas_call | solution.py:843
  147.7 136.2 %backward.1 = (bf16[4,2048,512]{2,1,0:T(8,128)(2,1)}, bf16[4,2048,512]{2,1,0:T(8,128)(2,1)}, f32[48,64,128]{2,1,0:T(8,128)}, f32[1,8,128]{2,1,0:T(8,128)}) custom-call(s32[4,1,256]{2,1,0:T(1,128)} %spot_ref.1, bf16[2,1024,512]{2,1,0:T(8,128)(2,1)} %get-tuple-element.27.rows, bf16[2,1024,512]{2,1,0:T(8,128)(2,1)} %get-tuple-element.28.cot, ...), custom_call_target="tpu_custom_call" | custom-call | tf_op jit(solution)/shard_map/backward/pallas_call | solution.py:1273
  283.9 0.8 slice_select_fusion
  284.7 0.5 slice_bitcast_fusion.4
  285.3 1.1 slice_bitcast_fusion
  286.4 1.3 slice.43
  287.7 0.7 bitcast_bitcast_fusion.1
  288.5 0.1 fusion.6
  288.6 0.3 copy.33
  288.9 0.3 copy.32
  289.2 1.3 bitcast_bitcast_fusion
  290.5 0.7 copy_bitcast_fusion.2
  291.2 7.3 %copy.50 = bf16[4,1,2048,512]{3,2,1,0:T(8,128)(2,1)} copy(bf16[4,1,2048,512]{3,2,1,0:T(8,128)(2,1)} %bitcast.61) | data formatting | bytes 16777216
  298.6 7.3 %copy.51 = bf16[4,1,2048,512]{3,2,1,0:T(8,128)(2,1)} copy(bf16[4,1,2048,512]{3,2,1,0:T(8,128)(2,1)} %bitcast.60) | data formatting | bytes 16777216

commit v4 on v3

--- a/solution.py
+++ b/solution.py
@@ -194,7 +194,17 @@
 NB = 48
 PATTERN = "XYZX"
 PER = 4
-LAGS = (0, 3, 6, 9, 12, 15)
+GATHER_LAGS = {
+    "X": (0, 3, 6, 9, 12, 18),
+    "Y": (0, 3, 6, 9, 13, 18),
+    "Z": (0, 3, 7, 11, 14, 17),
+}
+SCATTER_LAGS = {
+    "X": (0, 4, 7, 9, 13, 18),
+    "Y": (0, 5, 8, 10, 14, 17),
+    "Z": (0, 1, 6, 10, 13, 18),
+}
+VECTOR_STEPS = (0, 3, 6, 9, 12, 15)
 
 
 class Place:
@@ -247,21 +257,27 @@
 
 class Steps:
     def step(self, s, pos, static=None, guard=False):
-        live = [j for j in (5, 4, 3, 2, 1, 0) if static is None or 0 <= static - LAGS[j] < NB]
-
-        def do(j, act):
-            b = s - LAGS[j]
+        live = []
+        for c, lags in self.lags.items():
+            for j in range(6):
+                q = (pos - lags[j]) % PER
+                if PATTERN[q] == c and (static is None or 0 <= static - lags[j] < NB):
+                    live.append((j, lags[j], q))
+        live.sort(reverse=True)
+
+        def do(j, lag, q, act):
+            b = s - lag
             if guard:
-                pl.when(b < NB)(lambda: act(b, (pos - LAGS[j]) % PER, j))
+                pl.when(b < NB)(lambda: act(b, q, j))
             else:
-                act(b, (pos - LAGS[j]) % PER, j)
-
-        for j in live:
+                act(b, q, j)
+
+        for j, lag, q in live:
             if j > 0:
-                do(j, lambda b, q, j: self.recv(b, q, j - 1))
-        for j in live:
+                do(j, lag, q, lambda b, q, j: self.recv(b, q, j - 1))
+        for j, lag, q in live:
             if j < 5:
-                do(j, self.send)
+                do(j, lag, q, self.send)
 
     def drain(self, nb=NB):
         def body(r, _):
@@ -274,6 +290,8 @@
 
 
 class Gather(Steps):
+    lags = GATHER_LAGS
+
     def __init__(self, p, W, ss, rs):
         self.p, self.W, self.ss, self.rs = p, W, ss, rs
 
@@ -338,6 +356,8 @@
 
 
 class Scatter(Steps):
+    lags = SCATTER_LAGS
+
     def __init__(self, p, G, out, L8, L4, LZ, P4, P2, P1, ss, rs):
         self.p, self.G, self.out, self.ss, self.rs = p, G, out, ss, rs
         self.L8, self.L4, self.LZ, self.P4, self.P2, self.P1 = L8, L4, LZ, P4, P2, P1
@@ -553,8 +573,6 @@
     nacc,
     act,
     dup,
-    u32,
-    d32,
     Gst,
     ss,
     rs,
@@ -576,11 +594,9 @@
 
     own = [pltpu.make_async_copy(tile_ref, own_slot(p, VB, 0), first.at[NB])]
     for b in range(16):
-        src = (wq, wk, wv, wo)[b // 4]
+        src, col = ((wq, wk, wv)[b % 3], b // 3) if b < 12 else (wo, b - 12)
         own.append(
-            pltpu.make_async_copy(
-                src.at[:, pl.ds(b % 4 * 128, 128)], own_slot(p, W, b), first.at[b]
-            )
+            pltpu.make_async_copy(src.at[:, pl.ds(col * 128, 128)], own_slot(p, W, b), first.at[b])
         )
     for b in range(32):
         src = (wu, wd)[b % 4 // 2]
@@ -611,8 +627,8 @@
     def tick(s, guard=False):
         if isinstance(s, int):
             W_steps.step(s, s % PER, static=s)
-            if s in LAGS:
-                j = LAGS.index(s)
+            if s in VECTOR_STEPS:
+                j = VECTOR_STEPS.index(s)
                 if j > 0:
                     V_steps.recv(0, 0, j - 1)
                 if j < 5:
@@ -683,49 +699,29 @@
     saved += later[:2]
     nT_saved = later[2]
 
-    def project(j):
-        y = dot(nrm[...], wblocks(W, 2 * j, 2)).astype(bf)
-        qkv[2 * j] = y[:, :128]
-        qkv[2 * j + 1] = y[:, 128:]
-
-    def project_part(n, _):
-        s = 20 + 4 * n
-        W_steps.step(s, 0)
-        W_steps.step(s + 1, 1)
-        project(3 * n)
-        W_steps.step(s + 2, 2)
-        project(3 * n + 1)
-        W_steps.step(s + 3, 3)
-        project(3 * n + 2)
-        return 0
-
-    lax.fori_loop(0, 2, project_part, 0)
-    saved.append(saver(4, qkv, o_qkv))
-    saved[-1].start()
-
     masks, low_half = head_masks()
     mask = causal_mask()
 
     def attend(i, hp):
-        r_ = cut(i, CAP)
-        q, k, v = qkv[hp, r_, :], qkv[4 + hp, r_, :], qkv[8 + hp, r_, :]
+        r_ = seq_rows(i)
+        q, k, v = qkv[3 * hp, r_, :], qkv[3 * hp + 1, r_, :], qkv[3 * hp + 2, r_, :]
         mix = [dot(softmax_rows(q * masks[h], k, mask).astype(bf), v) for h in (0, 1)]
         mixed[hp, r_, :] = jnp.where(low_half, mix[0], mix[1]).astype(bf)
 
-    def attend_part(n, _):
-        for q in range(4):
-            W_steps.step(28 + 4 * n + q, q)
-
-            def pair(e, _):
-                attend(2 * n + q // 2, q % 2 * 2 + e)
-                return 0
-
-            lax.fori_loop(0, 2, pair, 0)
+    def pair_part(hp, _):
+        y = dot(nrm[...], wblocks(W, 3 * hp, 3)).astype(bf)
+        for c in range(3):
+            qkv[3 * hp + c] = y[:, c * 128 : c * 128 + 128]
+        for i in range(SEQ):
+            W_steps.step(20 + 4 * hp + i, i)
+            attend(i, hp)
         return 0
 
-    lax.fori_loop(0, 2, attend_part, 0)
-    saved.append(saver(5, mixed, o_mix))
-    saved[-1].start()
+    lax.fori_loop(0, 4, pair_part, 0)
+    later = [saver(4, qkv, o_qkv), saver(5, mixed, o_mix)]
+    for c in later:
+        c.start()
+    saved += later
 
     def att_copy(i):
         return pltpu.make_async_remote_copy(
@@ -737,17 +733,7 @@
             device_id_type=MESH,
         )
 
-    for i in range(SEQ):
-        W_steps.step(36 + i, i)
-        mix = jnp.concatenate([mixed[h, seq_rows(i), :] for h in range(4)], 1)
-        P[seq_rows(i), :] = dot_nt(mix, wblocks(W, 12, 4)).astype(bf)
-        if i > 0:
-            att_copy(i - 1).start()
-    nT_saved.wait()
-    saved.append(saver(6, W.at[pl.ds(0, 16)], o_W))
-    saved[-1].start()
-    att_copy(3).start()
-    for i in range(SEQ):
+    def norm_mlp(i):
         att_copy(i).wait_recv()
 
         def norm_part(n, _):
@@ -760,6 +746,32 @@
         for c in range(4):
             cs = pl.ds(c * 256, 256)
             nT[cs, seq_rows(i)] = nrm[seq_rows(i), cs].T
+
+    out_w = wblocks(W, 12, 4)
+
+    def project_out(i):
+        mix = jnp.concatenate([mixed[h, seq_rows(i), :] for h in range(4)], 1)
+        P[seq_rows(i), :] = dot_nt(mix, out_w).astype(bf)
+
+    W_steps.step(36, 0)
+    project_out(0)
+    project_out(1)
+    att_copy(0).start()
+    W_steps.step(37, 1)
+    project_out(2)
+    att_copy(1).start()
+    project_out(3)
+    att_copy(2).start()
+    nT_saved.wait()
+    W_steps.step(38, 2)
+    norm_mlp(0)
+    att_copy(3).start()
+    norm_mlp(1)
+    W_steps.step(39, 3)
+    norm_mlp(2)
+    norm_mlp(3)
+    saved.append(saver(6, W.at[pl.ds(0, 16)], o_W))
+    saved[-1].start()
     later = [saver(7, P, o_P), saver(8, R, o_R)]
     for c in later:
         c.start()
@@ -776,27 +788,22 @@
         down_w = wblocks(W, 18 + 4 * m, 2)
         for ht in range(2):
             hs_ = pl.ds(ht * 512, 512)
-            W_steps.step(s + 2 * ht, 2 * ht, guard=True)
-            u32[...] = dot(nrm[hs_, :], up_w)
-            d32[...] = dot(dd[hs_, :], down_w)
-
-            def gelu_part(n, _):
-                rs_ = cut(n, 32)
-                out_ = pl.ds(pl.multiple_of(ht * 512 + n * 32, 32), 32)
-                u = u32[rs_, :]
-                c0 = 0.7978845608028654
-                u2 = u * u
-                th = jnp.tanh(c0 * (u + 0.044715 * (u * u2)))
-                cdf = 0.5 * (1.0 + th)
-                act[out_, :] = (u * cdf).astype(bf)
-                slope = cdf + 0.5 * u * (1.0 - th * th) * (c0 + (3 * 0.044715 * c0) * u2)
-                dup[out_, :] = (d32[rs_, :] * slope).astype(bf)
-                return 0
-
-            lax.fori_loop(0, 16, gelu_part, 0)
-            W_steps.step(s + 2 * ht + 1, 2 * ht + 1, guard=True)
+            W_steps.step(s + ht, ht, guard=True)
+            u = dot(nrm[hs_, :], up_w)
+            d = dot(dd[hs_, :], down_w)
+            c0 = 0.7978845608028654
+            u2 = u * u
+            s1 = 1.0 + jnp.tanh(u * (c0 + (c0 * 0.044715) * u2))
+            h = 0.5 * u
+            act[hs_, :] = (h * s1).astype(bf)
+            slope = s1 * (0.5 + h * (2.0 - s1) * (c0 + (3 * 0.044715 * c0) * u2))
+            dup[hs_, :] = (d * slope).astype(bf)
+        W_steps.step(s + 2, 2, guard=True)
+        for ht in range(2):
+            hs_ = pl.ds(ht * 512, 512)
             dacc[hs_, :] += dot_nt(act[hs_, :], down_w)
             nacc[hs_, :] += dot_nt(dup[hs_, :], up_w)
+        W_steps.step(s + 3, 3, guard=True)
 
         @pl.when(m >= 2)
         def _():
@@ -878,8 +885,6 @@
             vm((ROWS, 1024), f32),
             vm((ROWS, 256), bf),
             vm((ROWS, 256), bf),
-            vm((512, 256), f32),
-            vm((512, 256), f32),
             vm((2, 4, 1024, 128), bf),
             DMA((NB, 8)),
             DMA((NB, 8)),
@@ -902,7 +907,6 @@
 
 
 def backward_kernel(
-    spot_ref,
     rows,
     cot,
     nT_in,
@@ -915,10 +919,8 @@
     W_in,
     G_in,
     vec_in,
-    tok_ref,
-    cot_ref,
-    o_tok,
-    o_cot,
+    o_newr,
+    o_newg,
     o_sum,
     o_vec,
     G,
@@ -948,7 +950,6 @@
     prcv,
     qsem,
     qrcv,
-    tin,
     tout,
     *landing,
 ):
@@ -1080,7 +1081,8 @@
 
         def pair_back(hp):
             r_ = seq_rows(s)
-            qh, kh, vh, dmh = qkv[hp, r_, :], qkv[4 + hp, r_, :], qkv[8 + hp, r_, :], dmix[hp]
+            qh, kh, vh = [qkv[3 * hp + c, r_, :] for c in range(3)]
+            dmh = dmix[hp]
             outs = []
             for h in (0, 1):
                 sc = jnp.where(seen, dot_nt(kh, qh * masks[h]) * (HD**-0.5), -1e30)
@@ -1093,7 +1095,7 @@
             scale = HD**-0.5
             for i, (a, b) in enumerate(zip(*outs)):
                 v = jnp.where(low_half, a, b)
-                qkv[4 * i + hp, r_, :] = (v if i == 2 else v * scale).astype(bf)
+                qkv[3 * hp + i, r_, :] = (v if i == 2 else v * scale).astype(bf)
 
         for half in range(2):
             tick(4 * s + 2 + half)
@@ -1103,6 +1105,9 @@
                 return 0
 
             lax.fori_loop(0, 2, pair_part, 0)
+
+    row_outs = [pltpu.make_async_copy(newr, o_newr, tout.at[0])]
+    row_outs[0].start()
 
     def grad_unit(leftT, a, b, first):
         y = jnp.concatenate([a, b], 1)
@@ -1198,63 +1203,25 @@
             GV[0, z, y, 1] = tile
     for s in range(SEQ):
         back_copy(s).wait_send()
-
-    def tok_in(n, a):
-        return pltpu.make_async_copy(
-            (tok_ref, cot_ref)[a].at[n // 4, cut(n % 4, 512)],
-            NR.at[a, cut(n % 2, 512)],
-            tin.at[a, n % 2],
-        )
-
-    def tok_out(n, a):
-        return pltpu.make_async_copy(
-            DR.at[a, cut(n % 2, 512)],
-            (o_tok, o_cot)[a].at[n // 4, cut(n % 4, 512)],
-            tout.at[a, n % 2],
-        )
-
-    for n in range(2):
-        for a in range(2):
-            tok_in(n, a).start()
+    row_outs.append(pltpu.make_async_copy(newg, o_newg, tout.at[1]))
+    row_outs[1].start()
     v_steps.send(0, 0, 0)
-    ones = jnp.ones((CAP, 128), bf)
-
-    def place_part(m, _):
+
+    def rest(m, _):
         for e in range(4):
-            n = 4 * m + e
-            steps.step(40 + n, e, guard=True)
-            place = lax.broadcasted_iota(jnp.int32, (512, CAP), 0) + e * 512
-            hit = jnp.where(place == spot_ref[m], 1.0, 0.0).astype(bf)
-            there = dot(hit, ones)
-            there = jnp.concatenate([there, there, there, there], 1) > 0.5
-            for a in range(2):
-                tok_in(n, a).wait()
-                new = dot(hit, (newr, newg)[a][cut(m, CAP), :])
-                slot = pl.ds(e % 2 * 512, 512)
-                old = NR[a, slot, :].astype(f32)
-                if e >= 2:
-                    tok_out(n - 2, a).wait()
-                else:
-                    pl.when(m > 0)(lambda: tok_out(n - 2, a).wait())
-                DR[a, slot, :] = jnp.where(there, new, old).astype(bf)
-                tok_out(n, a).start()
-                if e < 2:
-                    tok_in(n + 2, a).start()
-                else:
-                    pl.when(m < 3)(lambda: tok_in(n + 2, a).start())
+            steps.step(40 + 4 * m + e, e, guard=True)
         return 0
 
-    lax.fori_loop(0, 4, place_part, 0)
-    for k, s in enumerate(range(56, 64)):
+    lax.fori_loop(0, 4, rest, 0)
+    for k, s in enumerate(range(56, 67)):
         tick(s)
         if k in (0, 2, 3, 5, 7):
             j = (0, 2, 3, 5, 7).index(k) + 1
             v_steps.recv(0, 0, j - 1)
             if j < 5:
                 v_steps.send(0, 0, j)
-    for n in (14, 15):
-        for a in range(2):
-            tok_out(n, a).wait()
+    for c in row_outs:
+        c.wait()
     for s in range(SEQ):
         for e in range(2):
             pair_copy(s, e).wait_send()
@@ -1263,7 +1230,7 @@
     steps.drain()
 
 
-def backward_call(spot, kept, tok, cotangent):
+def backward_call(kept):
     bf, f32 = jnp.bfloat16, jnp.float32
     S = jax.ShapeDtypeStruct
     DMA = pltpu.SemaphoreType.DMA
@@ -1273,12 +1240,12 @@
     return pl.pallas_call(
         backward_kernel,
         out_shape=(
-            S((SEQ, 2048, 512), bf),
-            S((SEQ, 2048, 512), bf),
+            S((ROWS, 512), bf),
+            S((ROWS, 512), bf),
             S((NB, 64, 128), f32),
             S((1, 8, 128), f32),
         ),
-        in_specs=[vspec] + [any_] * 14,
+        in_specs=[any_] * 12,
         out_specs=[any_, any_, vspec, vspec],
         scratch_shapes=[
             vm((NB, 4, 2, 2, 64, 128), bf),
@@ -1308,8 +1275,7 @@
             DMA((4, 2)),
             DMA((4,)),
             DMA((4,)),
-            DMA((2, 2)),
-            DMA((2, 2)),
+            DMA((2,)),
         ]
         + Scatter.landing(NB, (64, 128), bf)
         + Scatter.landing(PER, (8, 128), f32),
@@ -1317,7 +1283,132 @@
             collective_id=2, has_side_effects=True, vmem_limit_bytes=63 * 1024 * 1024
         ),
         name="backward",
-    )(spot, *kept, tok, cotangent)
+    )(*kept)
+
+
+def place_kernel(
+    spot_ref,
+    own_ref,
+    newr,
+    newg,
+    tok,
+    cot,
+    o_tok,
+    o_cot,
+    g_q,
+    g_k,
+    g_v,
+    g_out,
+    g_up,
+    g_down,
+    old,
+    out,
+    new,
+    came,
+    went,
+    nsem,
+    gsem,
+):
+    bf = jnp.bfloat16
+
+    def piece(n):
+        return n // (2048 // SIZE), cut(n % (2048 // SIZE), SIZE)
+
+    def load(n, a):
+        i, rs = piece(n)
+        return pltpu.make_async_copy((tok, cot)[a].at[i, rs], old.at[a, n], came.at[a, n])
+
+    def store(n, a):
+        i, rs = piece(n)
+        return pltpu.make_async_copy(out.at[a, n], (o_tok, o_cot)[a].at[i, rs], went.at[a, n])
+
+    pieces = SEQ * 2048 // SIZE
+    news = [pltpu.make_async_copy((newr, newg)[a], new.at[a], nsem.at[a]) for a in range(2)]
+    for c in news:
+        c.start()
+
+    def start(n, _):
+        load(n, 0).start()
+        load(n, 1).start()
+        return 0
+
+    lax.fori_loop(0, pieces, start, 0)
+
+    moves = []
+    for b in range(NB):
+        if b < 32:
+            ref, k = (g_up, g_down)[b % 4 // 2], b // 4 * 2 + b % 2
+        else:
+            ref, k = (g_out, b - 32) if b < 36 else ((g_q, g_k, g_v)[b % 3], (b - 36) // 3)
+        moves.append(
+            pltpu.make_async_copy(own_ref.at[b], ref.at[:, pl.ds(k * 128, 128)], gsem.at[b])
+        )
+    for c in moves:
+        c.start()
+    for c in news:
+        c.wait()
+    ones = jnp.ones((CAP, 128), bf)
+
+    def place(n, _):
+        i, _rs = piece(n)
+        row = lax.broadcasted_iota(jnp.int32, (SIZE, CAP), 0) + n % (2048 // SIZE) * SIZE
+        hit = jnp.where(row == spot_ref[i], 1.0, 0.0).astype(bf)
+        kept = 1.0 - dot(hit, ones)
+        kept = jnp.concatenate([kept, kept, kept, kept], 1).astype(bf)
+        for a in range(2):
+            moved = dot(hit, new[a, cut(i, CAP), :]).astype(bf)
+            load(n, a).wait()
+            out[a, n] = old[a, n] * kept + moved
+            store(n, a).start()
+        return 0
+
+    lax.fori_loop(0, pieces, place, 0)
+
+    def finish(n, _):
+        store(n, 0).wait()
+        store(n, 1).wait()
+        return 0
+
+    lax.fori_loop(0, pieces, finish, 0)
+    for c in moves:
+        c.wait()
+
+
+SIZE = 1024
+
+
+def place_call(spot, own, newr, newg, tok, cotangent):
+    bf, f32 = jnp.bfloat16, jnp.float32
+    S = jax.ShapeDtypeStruct
+    DMA = pltpu.SemaphoreType.DMA
+    any_ = pl.BlockSpec(memory_space=HBM)
+    pieces = SEQ * 2048 // SIZE
+    return pl.pallas_call(
+        place_kernel,
+        out_shape=(
+            S((SEQ, 2048, 512), bf),
+            S((SEQ, 2048, 512), bf),
+            S((64, 512), f32),
+            S((64, 512), f32),
+            S((64, 512), f32),
+            S((64, 512), f32),
+            S((64, 2048), f32),
+            S((64, 2048), f32),
+        ),
+        in_specs=[pl.BlockSpec(memory_space=pltpu.VMEM), any_, any_, any_, any_, any_],
+        out_specs=[any_] * 8,
+        scratch_shapes=[
+            pltpu.VMEM((2, pieces, SIZE, 512), bf),
+            pltpu.VMEM((2, pieces, SIZE, 512), bf),
+            pltpu.VMEM((2, ROWS, 512), bf),
+            DMA((2, pieces)),
+            DMA((2, pieces)),
+            DMA((2,)),
+            DMA((NB,)),
+        ],
+        compiler_params=pltpu.CompilerParams(vmem_limit_bytes=48 * 1024 * 1024),
+        name="place_rows",
+    )(spot, own, newr, newg, tok, cotangent)
 
 
 def to_tile(w_route, gain_attn, gain_mlp):
@@ -1326,10 +1417,6 @@
     z = jnp.zeros_like(v)
     odd = lax.axis_index("dp") % 2
     return jnp.where(odd == 0, jnp.concatenate([v, z], 1), jnp.concatenate([z, v], 1))
-
-
-def from_blocks(x):
-    return x.transpose(1, 0, 2).reshape(x.shape[1], -1)
 
 
 def fused(
@@ -1352,19 +1439,21 @@
     weights = (w_query, w_key, w_value, w_out.T, w_up, w_down.T)
     kept = list(forward_call(routed.reshape(ROWS, 1), tile, tok, cot, weights))
     kept[10] = kept[10].reshape(32, 4, 2, 2, 64, 128)
-    output, grad, own, vec = backward_call(routed.reshape(SEQ, 1, CAP), kept, tok, cot)
-    mlp = own[:32].reshape(8, 2, 2, 64, 128)
+    newr, newg, own, vec = backward_call(kept)
     odd = lax.axis_index("dp") % 2
     vec = jnp.where(odd == 0, vec[0, :3, :64], vec[0, :3, 64:])
+    output, grad, g_q, g_k, g_v, g_out, g_up, g_down = place_call(
+        routed.reshape(SEQ, 1, CAP), own, newr, newg, tok, cot
+    )
     return (
         output.reshape(tokens.shape),
         grad.reshape(tokens.shape),
-        from_blocks(own[36:40]),
-        from_blocks(own[40:44]),
-        from_blocks(own[44:48]),
-        from_blocks(own[32:36]).T,
-        from_blocks(mlp[:, 0].reshape(16, 64, 128)),
-        from_blocks(mlp[:, 1].reshape(16, 64, 128)).T,
+        g_q,
+        g_k,
+        g_v,
+        g_out.T,
+        g_up,
+        g_down.T,
         vec[0],
         vec[1],
         vec[2],

time: 311 us -> 278 us (0.89)
  local copies, waits for them, and re-layouts: 22.8 us -> 6.09 us
  Pallas kernels: 280 us -> 265 us
    pallas_call x1, Pallas kernels: 144 us -> 126 us  [forward_call(): pl.pallas_call(forward_kernel, out_shape=(S((2, ROWS, 512), bf), S((2, RO...]
    unnamed x3 -> x8, local copies, waits for them, and re-layouts: 15.8 us -> 3.86 us
    pallas_call x1 -> x2, Pallas kernels: 136 us -> 139 us  [the longest x1 124 us: backward_call(): pl.pallas_call(backward_kernel, out_shape=(S((ROWS, 512), bf), S((ROWS, 5...]
where the time goes in v4:
time: 278 us; the launch traced here: 274 us
  Pallas kernels  265 us (95%)
  local copies, waits for them, and re-layouts  6.09 us (2%)
    pallas_call x1, Pallas kernels, forward_call(): pl.pallas_call(forward_kernel, out_shape=(S((2, ROWS, 512), bf), S((2, RO...  126 us
    pallas_call x1, Pallas kernels, backward_call(): pl.pallas_call(backward_kernel, out_shape=(S((ROWS, 512), bf), S((ROWS, 5...  124 us
    pallas_call x1, Pallas kernels, place_call(): pl.pallas_call(place_kernel, out_shape=(S((SEQ, 2048, 512), bf), S((SEQ,...  14.3 us

profile of v4, /device:TPU:0, one launch (start us, length us, event | category | flops | bytes accessed | tf_op | source)
XLA Modules:
  0.0 274.0 jit_solution(15006194170680845113)
XLA Ops:
  0.7 0.7 fusion.5
  1.4 0.7 pad_select_fusion.tile_ref
  2.0 1.7 copy.25.idx_ref
  3.7 126.0 %forward.1 = (bf16[2,1024,512]{2,1,0:T(8,128)(2,1)}, bf16[2,1024,512]{2,1,0:T(8,128)(2,1)}, bf16[1024,1024]{1,0:T(8,128)(2,1)}, bf16[12,1024,128]{2,1,0:T(8,128)...) custom-call(s32[1024,1]{1,0:T(8,128)} %copy.25.idx_ref, ...), custom_call_target="tpu_custom_call" | custom-call | tf_op jit(solution)/shard_map/forward/pallas_call | solution.py:850
  129.8 0.0 copy-start.3
  129.8 124.5 %backward.1 = (bf16[1024,512]{1,0:T(8,128)(2,1)}, bf16[1024,512]{1,0:T(8,128)(2,1)}, f32[48,64,128]{2,1,0:T(8,128)}, f32[1,8,128]{2,1,0:T(8,128)}) custom-call(bf16[2,1024,512]{2,1,0:T(8,128)(2,1)} %get-tuple-element.35.rows, bf16[2,1024,512]{2,1,0:T(8,128)(2,1)} %get-tuple-element.36.cot, bf16[1024,1024]{1,0:T(8,128)(2,1)} %get-tuple-element.37.nT_in, ...), custom_call_target="tpu_custom_call" | custom-call | tf_op jit(solution)/shard_map/backward/pallas_call | solution.py:1240
  254.3 0.8 slice_select_fusion
  255.1 0.5 slice_bitcast_fusion
  255.6 0.0 copy-done.3
  255.6 0.0 copy-start
  255.6 1.4 copy-done
  257.0 0.0 copy-start.1
  257.0 1.2 copy-done.1
  258.3 0.0 copy-start.2
  258.3 1.2 copy-done.2
  259.5 14.3 %place_rows.1 = (bf16[4,2048,512]{2,1,0:T(8,128)(2,1)}, bf16[4,2048,512]{2,1,0:T(8,128)(2,1)}, f32[64,512]{1,0:T(8,128)}, f32[64,512]{1,0:T(8,128)}, f32[64,512]...) custom-call(s32[4,1,256]{2,1,0:T(1,128)S(1)} %copy-done.3, f32[48,64,128]{2,1,0:T(8,128)S(1)} %copy-done, ...), custom_call_target="tpu_custom_call" | custom-call | tf_op jit(solution)/shard_map/place_rows/pallas_call | solution.py:1386
Async XLA Ops:
  129.8 125.9 %copy-start.3 = (s32[4,1,256]{2,1,0:T(1,128)S(1)}, s32[4,1,256]{2,1,0:T(1,128)}, u32[]{:S(2)}) copy-start(s32[4,1,256]{2,1,0:T(1,128)} %spot_ref.1) | copy-start | bytes 12292
  255.6 1.4 copy-start
  257.0 1.2 copy-start.1
  258.3 1.2 copy-start.2

commit v5 on v4

--- a/solution.py
+++ b/solution.py
@@ -195,14 +195,14 @@
 PATTERN = "XYZX"
 PER = 4
 GATHER_LAGS = {
-    "X": (0, 3, 6, 9, 12, 18),
-    "Y": (0, 3, 6, 9, 13, 18),
-    "Z": (0, 3, 7, 11, 14, 17),
+    "X": (0, 3, 6, 9, 12, 19),
+    "Y": (0, 3, 7, 9, 13, 17),
+    "Z": (0, 3, 8, 11, 14, 17),
 }
 SCATTER_LAGS = {
-    "X": (0, 4, 7, 9, 13, 18),
-    "Y": (0, 5, 8, 10, 14, 17),
-    "Z": (0, 1, 6, 10, 13, 18),
+    "X": (0, 4, 8, 9, 13, 18),
+    "Y": (0, 5, 8, 9, 13, 18),
+    "Z": (0, 2, 5, 9, 13, 18),
 }
 VECTOR_STEPS = (0, 3, 6, 9, 12, 15)
 
@@ -256,7 +256,7 @@
 
 
 class Steps:
-    def step(self, s, pos, static=None, guard=False):
+    def step(self, s, pos, static=None, low=False, high=False):
         live = []
         for c, lags in self.lags.items():
             for j in range(6):
@@ -267,7 +267,9 @@
 
         def do(j, lag, q, act):
             b = s - lag
-            if guard:
+            if low:
+                pl.when(b >= 0)(lambda: act(b, q, j))
+            elif high:
                 pl.when(b < NB)(lambda: act(b, q, j))
             else:
                 act(b, q, j)
@@ -279,14 +281,14 @@
             if j < 5:
                 do(j, lag, q, self.send)
 
-    def drain(self, nb=NB):
+    def drain(self, first, last):
         def body(r, _):
             for pos in range(PER):
                 for j in range(5):
                     self.send(r * PER + pos, pos, j, act=lambda d: d.wait_send())
             return 0
 
-        lax.fori_loop(0, nb // PER, body, 0)
+        lax.fori_loop(first, last, body, 0)
 
 
 class Gather(Steps):
@@ -532,7 +534,7 @@
 
 
 def forward_kernel(
-    idx_ref,
+    spot_ref,
     tile_ref,
     tok_ref,
     cot_ref,
@@ -610,58 +612,60 @@
     for c in own:
         c.start()
 
-    units = [(a, i) for i in range(SEQ) for a in (0, 1)]
-
-    def loader(u):
-        a, i = units[u]
-        return pltpu.make_async_copy((tok_ref, cot_ref)[a].at[i], tokbuf.at[u % 2], load.at[u % 2])
-
-    loader(0).start()
-    loader(1).start()
+    def loader(i, a):
+        return pltpu.make_async_copy((tok_ref, cot_ref)[a].at[i], tokbuf.at[a], load.at[a])
+
+    loader(0, 0).start()
+    loader(0, 1).start()
     barrier(p, True)
     for c in own:
         c.wait()
     W_steps = Gather(p, W, ss, rs)
     V_steps = Gather(p, VB, vss, vrs)
 
-    def tick(s, guard=False):
-        if isinstance(s, int):
-            W_steps.step(s, s % PER, static=s)
-            if s in VECTOR_STEPS:
-                j = VECTOR_STEPS.index(s)
-                if j > 0:
-                    V_steps.recv(0, 0, j - 1)
-                if j < 5:
-                    V_steps.send(0, 0, j)
-
-    def half_copy(u):
-        a, i = units[u]
-        ref = (rows, cot)[a].at[t, seq_rows(i)]
+    def half_copy(i, a):
+        ref = (rows, cot)[a].at[t, cut(i, CAP)]
         return pltpu.make_async_remote_copy(
-            ref, ref, hs.at[u], hr.at[u], device_id=other, device_id_type=MESH
+            ref, ref, hs.at[i, a], hr.at[i, a], device_id=other, device_id_type=MESH
         )
 
-    def half_wait(u):
-        a, i = units[u]
+    def half_wait(i, a):
         ref = (rows, cot)[a].at[1 - t, seq_rows(i)]
         pltpu.make_async_remote_copy(
-            ref, ref, hs.at[u], hr.at[u], device_id=other, device_id_type=MESH
+            ref, ref, hs.at[i, a], hr.at[i, a], device_id=other, device_id_type=MESH
         ).wait_recv()
 
-    for u, (a, i) in enumerate(units):
-        tick(2 * u)
-        if a == 0:
-            spot = idx_ref[seq_rows(i), :]
-            hit = lax.broadcasted_iota(jnp.int32, (CAP, 2048), 1) == spot
-            onehot[...] = jnp.where(hit, 1.0, 0.0).astype(bf)
-        loader(u).wait()
-        (rows, cot)[a][t, seq_rows(i), :] = dot(onehot[...], tokbuf[u % 2]).astype(bf)
-        if u + 2 < 8:
-            loader(u + 2).start()
-        tick(2 * u + 1)
-        if u > 0:
-            half_copy(u - 1).start()
-    half_copy(7).start()
+    def gather_part(i, _):
+        def tick(q):
+            W_steps.step(4 * i + q, q, low=True)
+            for j, s in enumerate(VECTOR_STEPS):
+                if s % 4 == q:
+
+                    @pl.when(i == s // 4)
+                    def _():
+                        if j > 0:
+                            V_steps.recv(0, 0, j - 1)
+                        if j < 5:
+                            V_steps.send(0, 0, j)
+
+        for a in range(2):
+            tick(2 * a)
+            if a == 0:
+                spot = jnp.broadcast_to(spot_ref[i], (128, CAP)).T[:, :1]
+                hit = lax.broadcasted_iota(jnp.int32, (CAP, 2048), 1) == spot
+                onehot[...] = jnp.where(hit, 1.0, 0.0).astype(bf)
+            loader(i, a).wait()
+            (rows, cot)[a][t, cut(i, CAP), :] = dot(onehot[...], tokbuf[a]).astype(bf)
+            pl.when(i < 3)(lambda: loader(i + 1, a).start())
+            tick(2 * a + 1)
+            if a == 0:
+                pl.when(i > 0)(lambda: half_copy(i - 1, 1).start())
+            else:
+                half_copy(i, 0).start()
+        return 0
+
+    lax.fori_loop(0, 4, gather_part, 0)
+    half_copy(3, 1).start()
 
     for z in range(4):
         for y in range(2):
@@ -677,9 +681,9 @@
     nacc[...] = jnp.zeros_like(nacc)
 
     for i in range(SEQ):
-        tick(16 + i)
-        half_wait(2 * i)
-        half_wait(2 * i + 1)
+        W_steps.step(16 + i, i, static=16 + i)
+        half_wait(i, 0)
+        half_wait(i, 1)
 
         def norm_part(n, _):
             rs_ = cut(i * 8 + n, 32)
@@ -788,7 +792,7 @@
         down_w = wblocks(W, 18 + 4 * m, 2)
         for ht in range(2):
             hs_ = pl.ds(ht * 512, 512)
-            W_steps.step(s + ht, ht, guard=True)
+            W_steps.step(s + ht, ht, high=True)
             u = dot(nrm[hs_, :], up_w)
             d = dot(dd[hs_, :], down_w)
             c0 = 0.7978845608028654
@@ -798,12 +802,13 @@
             act[hs_, :] = (h * s1).astype(bf)
             slope = s1 * (0.5 + h * (2.0 - s1) * (c0 + (3 * 0.044715 * c0) * u2))
             dup[hs_, :] = (d * slope).astype(bf)
-        W_steps.step(s + 2, 2, guard=True)
+        W_steps.step(s + 2, 2, high=True)
         for ht in range(2):
             hs_ = pl.ds(ht * 512, 512)
             dacc[hs_, :] += dot_nt(act[hs_, :], down_w)
             nacc[hs_, :] += dot_nt(dup[hs_, :], up_w)
-        W_steps.step(s + 3, 3, guard=True)
+        W_steps.step(s + 3, 3, high=True)
+        W_steps.drain(m, m + 1)
 
         @pl.when(m >= 2)
         def _():
@@ -828,11 +833,12 @@
                 saver(9 + 2 * e + c, tokbuf.at[e, pl.ds(c * 1024, 1024)], (o_down, o_back)[e].at[c])
             )
             saved[-1].start()
-    for u in range(8):
-        half_copy(u).wait_send()
+    for i in range(SEQ):
+        half_copy(i, 0).wait_send()
+        half_copy(i, 1).wait_send()
     for i in range(SEQ):
         att_copy(i).wait_send()
-    W_steps.drain()
+    W_steps.drain(8, NB // PER)
     for j in range(5):
         V_steps.send(0, 0, j, act=lambda d: d.wait_send())
     g_copy(6).wait()
@@ -890,8 +896,8 @@
             DMA((NB, 8)),
             DMA((1, 8)),
             DMA((1, 8)),
-            DMA((8,)),
-            DMA((8,)),
+            DMA((4, 2)),
+            DMA((4, 2)),
             DMA((4,)),
             DMA((4,)),
             DMA((NB + 1,)),
@@ -959,21 +965,21 @@
     f32, bf = jnp.float32, jnp.bfloat16
     wide, small = landing[:8], landing[8:]
 
-    g_loads = [
-        pltpu.make_async_copy(G_in.at[pl.ds(4 * c, 4)], G.at[pl.ds(4 * c, 4)], gsem.at[c])
-        for c in range(8)
-    ]
-    g_loads[0].start()
+    def g_load(c):
+        return pltpu.make_async_copy(G_in.at[pl.ds(4 * c, 4)], G.at[pl.ds(4 * c, 4)], gsem.at[c])
+
+    g_load(0).start()
+    g_load(1).start()
 
     def stream(s, names):
-        q = s % 2
+        q = lax.rem(s, 2)
         out = []
         for k in names:
             if k < 2:
-                src = (P_in, R_in)[k].at[seq_rows(s)]
+                src = (P_in, R_in)[k].at[cut(s, CAP)]
                 dst = buf2.at[q, k]
             else:
-                src = (rows, cot, down_in, back_in)[k - 2].at[:, seq_rows(s)]
+                src = (rows, cot, down_in, back_in)[k - 2].at[:, cut(s, CAP)]
                 dst = bufs.at[q, k - 2]
             out.append(pltpu.make_async_copy(src, dst, lsem.at[q, k]))
         return out
@@ -987,34 +993,24 @@
             ((vec_in, vecs), (W_in, Wa), (qkv_in, qkv), (mix_in, mixed), (nT_in, nT))
         )
     ]
-    for c in fixed[:1]:
-        c.start()
-    for c in g_loads[1:]:
+    for c in fixed[:3]:
         c.start()
     barrier(p, True)
 
     def pair_copy(s, e):
         return pltpu.make_async_remote_copy(
-            (down_in, back_in)[e].at[:, seq_rows(s)],
-            (DR, NR)[e].at[:, seq_rows(s)],
+            (down_in, back_in)[e].at[:, cut(s, CAP)],
+            (DR, NR)[e].at[:, cut(s, CAP)],
             psem.at[s, e],
             prcv.at[s, e],
             device_id=other,
             device_id_type=MESH,
         )
 
-    for s in range(SEQ):
-        for e in range(2):
-            pair_copy(s, e).start()
-    for c in fixed[1:]:
-        c.start()
+    pair_copy(0, 0).start()
+    pair_copy(0, 1).start()
     steps = Scatter(p, G, o_sum, *wide)
     v_steps = Scatter(p, GV, o_vec, *small)
-
-    def tick(s):
-        if s < 32 and s % 4 == 0:
-            g_loads[s // 4].wait()
-        steps.step(s, s % PER, static=s)
 
     accs[...] = jnp.zeros_like(accs)
 
@@ -1029,14 +1025,28 @@
         jnp.int32, (CAP, CAP), 1
     )
 
-    for s in range(SEQ):
-        tick(4 * s)
-        q = s % 2
-        if s + 1 < SEQ:
+    def seq_part(s, _):
+        def tick(q):
+            if q % 4 == 0:
+                g_load(2 * s + q // 4).wait()
+
+                @pl.when(s < 3)
+                def _():
+                    g_load(2 * s + q // 4 + 2).start()
+
+            steps.step(8 * s + q, q % 4, low=True)
+
+        tick(0)
+        q = lax.rem(s, 2)
+
+        @pl.when(s + 1 < SEQ)
+        def _():
             for c in stream(s + 1, everything):
                 c.start()
-        if s == 0:
-            fixed[0].wait()
+            pair_copy(s + 1, 0).start()
+            pair_copy(s + 1, 1).start()
+
+        pl.when(s == 0)(lambda: fixed[0].wait())
         for c in stream(s, everything):
             c.wait()
         for e in range(2):
@@ -1067,20 +1077,28 @@
             dlog[as_, :] = jnp.broadcast_to(dl, (32, 128))
             return 0
 
-        lax.fori_loop(0, 8, part, 0)
-        tick(4 * s + 1)
+        lax.fori_loop(0, 4, part, 0)
+        tick(1)
+        lax.fori_loop(4, 8, part, 0)
+        tick(2)
         for c in range(4):
             cs = pl.ds(c * 256, 256)
-            daT[cs, seq_rows(s)] = da[:, cs].T
-        if s == 0:
-            for c in fixed[1:]:
+            daT[cs, cut(s, CAP)] = da[:, cs].T
+
+        @pl.when(s == 0)
+        def _():
+            for c in fixed[1:3]:
                 c.wait()
+            for c in fixed[3:]:
+                c.start()
+
+        tick(3)
         dm = dot(da[...], wblocks(Wa, 12, 4)).astype(bf)
         for h in range(4):
             dmix[h] = dm[:, h * 128 : h * 128 + 128]
 
         def pair_back(hp):
-            r_ = seq_rows(s)
+            r_ = cut(s, CAP)
             qh, kh, vh = [qkv[3 * hp + c, r_, :] for c in range(3)]
             dmh = dmix[hp]
             outs = []
@@ -1097,15 +1115,12 @@
                 v = jnp.where(low_half, a, b)
                 qkv[3 * hp + i, r_, :] = (v if i == 2 else v * scale).astype(bf)
 
-        for half in range(2):
-            tick(4 * s + 2 + half)
-
-            def pair_part(e, _):
-                pair_back(2 * half + e)
-                return 0
-
-            lax.fori_loop(0, 2, pair_part, 0)
-
+        for hp in range(4):
+            tick(4 + hp)
+            pair_back(hp)
+        return 0
+
+    lax.fori_loop(0, SEQ, seq_part, 0)
     row_outs = [pltpu.make_async_copy(newr, o_newr, tout.at[0])]
     row_outs[0].start()
 
@@ -1128,44 +1143,41 @@
             device_id_type=MESH,
         )
 
-    for c in stream(0, (2, 3)):
-        c.start()
-    for c in stream(1, (2, 3)):
-        c.start()
+    for s in range(2):
+        for c in stream(s, (2, 3)):
+            c.start()
+    for c in fixed[3:]:
+        c.wait()
+    grad_unit(daT, mixed[0], mixed[1], 32)
+    grad_unit(daT, mixed[2], mixed[3], 34)
+
+    def grad_part(n, _):
+        for e in range(2):
+            steps.step(32 + 4 * n + 2 * e, 2 * e)
+            steps.step(33 + 4 * n + 2 * e, 2 * e + 1)
+            j = 2 * n + e
+            grad_unit(nT, qkv[2 * j], qkv[2 * j + 1], 36 + 2 * j)
+        return 0
+
+    lax.fori_loop(0, 3, grad_part, 0)
     for s in range(SEQ):
-        tick(16 + s)
-        x = jnp.concatenate([qkv[i, seq_rows(s), :] for i in range(12)], 1)
-        y = dot_nt(x, wblocks(Wa, 0, 12)).astype(bf)
+        steps.step(44 + s, s)
+        y = 0.0
+        for g in range(3):
+            x = jnp.concatenate([qkv[4 * g + i, seq_rows(s), :] for i in range(4)], 1)
+            y = y + dot_nt(x, wblocks(Wa, 4 * g, 4))
+        y = y.astype(bf)
         DR[0, seq_rows(s), :] = y[:, :512]
         DR[1, seq_rows(s), :] = y[:, 512:]
         if s > 0:
             back_copy(s - 1).start()
-    tick(20)
+    steps.step(48, 0, high=True)
     back_copy(3).start()
-    grad_unit(daT, mixed[0], mixed[1], 32)
-    tick(21)
-    grad_unit(daT, mixed[2], mixed[3], 34)
-    for g_load in g_loads[6:]:
-        g_load.wait()
-
-    def grad_part(n, _):
-        for e in range(2):
-            sn = 22 + 4 * n + 2 * e
-            steps.step(sn, (2 + 2 * e) % 4)
-            steps.step(sn + 1, (3 + 2 * e) % 4)
-            j = 2 * n + e
-            grad_unit(nT, qkv[2 * j], qkv[2 * j + 1], 36 + 2 * j)
-        return 0
-
-    lax.fori_loop(0, 2, grad_part, 0)
-    for e in range(2):
-        grad_unit(nT, qkv[8 + 2 * e], qkv[9 + 2 * e], 44 + 2 * e)
-        steps.step(30 + e, 2 + e)
 
     route_half = jnp.where(t == 0, vecs[0:1, :512], vecs[0:1, 512:])
     for s in range(SEQ):
-        steps.step(32 + 2 * s, 2 * s % 4)
-        steps.step(33 + 2 * s, (2 * s + 1) % 4)
+        steps.step(49 + s, (1 + s) % 4, high=True)
+        steps.drain(2 * s, 2 * s + 2)
         q = s % 2
         for c in stream(s, (2, 3)):
             c.wait()
@@ -1207,14 +1219,8 @@
     row_outs[1].start()
     v_steps.send(0, 0, 0)
 
-    def rest(m, _):
-        for e in range(4):
-            steps.step(40 + 4 * m + e, e, guard=True)
-        return 0
-
-    lax.fori_loop(0, 4, rest, 0)
-    for k, s in enumerate(range(56, 67)):
-        tick(s)
+    for k, s in enumerate(range(53, 67)):
+        steps.step(s, s % PER, static=s)
         if k in (0, 2, 3, 5, 7):
             j = (0, 2, 3, 5, 7).index(k) + 1
             v_steps.recv(0, 0, j - 1)
@@ -1227,7 +1233,7 @@
             pair_copy(s, e).wait_send()
     for j in range(5):
         v_steps.send(0, 0, j, act=lambda d: d.wait_send())
-    steps.drain()
+    steps.drain(8, NB // PER)
 
 
 def backward_call(kept):
@@ -1306,6 +1312,7 @@
     new,
     came,
     went,
+    own,
     nsem,
     gsem,
 ):
@@ -1324,7 +1331,8 @@
 
     pieces = SEQ * 2048 // SIZE
     news = [pltpu.make_async_copy((newr, newg)[a], new.at[a], nsem.at[a]) for a in range(2)]
-    for c in news:
+    sums = pltpu.make_async_copy(own_ref, own, nsem.at[2])
+    for c in news + [sums]:
         c.start()
 
     def start(n, _):
@@ -1341,16 +1349,21 @@
         else:
             ref, k = (g_out, b - 32) if b < 36 else ((g_q, g_k, g_v)[b % 3], (b - 36) // 3)
         moves.append(
-            pltpu.make_async_copy(own_ref.at[b], ref.at[:, pl.ds(k * 128, 128)], gsem.at[b])
+            pltpu.make_async_copy(own.at[b], ref.at[:, pl.ds(k * 128, 128)], gsem.at[b])
         )
-    for c in moves:
-        c.start()
     for c in news:
         c.wait()
     ones = jnp.ones((CAP, 128), bf)
 
     def place(n, _):
         i, _rs = piece(n)
+
+        @pl.when(n == 2)
+        def _():
+            sums.wait()
+            for c in moves:
+                c.start()
+
         row = lax.broadcasted_iota(jnp.int32, (SIZE, CAP), 0) + n % (2048 // SIZE) * SIZE
         hit = jnp.where(row == spot_ref[i], 1.0, 0.0).astype(bf)
         kept = 1.0 - dot(hit, ones)
@@ -1381,7 +1394,7 @@
     bf, f32 = jnp.bfloat16, jnp.float32
     S = jax.ShapeDtypeStruct
     DMA = pltpu.SemaphoreType.DMA
-    any_ = pl.BlockSpec(memory_space=HBM)
+    any_ = pl.BlockSpec(memory_space=pltpu.MemorySpace.HBM)
     pieces = SEQ * 2048 // SIZE
     return pl.pallas_call(
         place_kernel,
@@ -1395,7 +1408,7 @@
             S((64, 2048), f32),
             S((64, 2048), f32),
         ),
-        in_specs=[pl.BlockSpec(memory_space=pltpu.VMEM), any_, any_, any_, any_, any_],
+        in_specs=[pl.BlockSpec(memory_space=pltpu.VMEM)] + [any_] * 5,
         out_specs=[any_] * 8,
         scratch_shapes=[
             pltpu.VMEM((2, pieces, SIZE, 512), bf),
@@ -1403,10 +1416,11 @@
             pltpu.VMEM((2, ROWS, 512), bf),
             DMA((2, pieces)),
             DMA((2, pieces)),
-            DMA((2,)),
+            pltpu.VMEM((NB, 64, 128), f32),
+            DMA((3,)),
             DMA((NB,)),
         ],
-        compiler_params=pltpu.CompilerParams(vmem_limit_bytes=48 * 1024 * 1024),
+        compiler_params=pltpu.CompilerParams(vmem_limit_bytes=63 * 1024 * 1024),
         name="place_rows",
     )(spot, own, newr, newg, tok, cotangent)
 
@@ -1435,15 +1449,16 @@
 ):
     tok = tokens.reshape(SEQ, 2048, 512)
     cot = cotangent.reshape(SEQ, 2048, 512)
+    spot = routed.reshape(SEQ, 1, CAP)
     tile = to_tile(w_route, gain_attn, gain_mlp)
     weights = (w_query, w_key, w_value, w_out.T, w_up, w_down.T)
-    kept = list(forward_call(routed.reshape(ROWS, 1), tile, tok, cot, weights))
+    kept = list(forward_call(spot, tile, tok, cot, weights))
     kept[10] = kept[10].reshape(32, 4, 2, 2, 64, 128)
     newr, newg, own, vec = backward_call(kept)
     odd = lax.axis_index("dp") % 2
     vec = jnp.where(odd == 0, vec[0, :3, :64], vec[0, :3, 64:])
     output, grad, g_q, g_k, g_v, g_out, g_up, g_down = place_call(
-        routed.reshape(SEQ, 1, CAP), own, newr, newg, tok, cot
+        spot, own, newr, newg, tok, cot
     )
     return (
         output.reshape(tokens.shape),

time: 278 us -> 263 us (0.946); the launches traced: 274 us -> 262 us
  Pallas kernels: 265 us -> 259 us
  local copies, waits for them, and re-layouts: 6.09 us -> 0.52 us
    pallas_call x1, Pallas kernels: 124 us -> 117 us  [backward_call(): pl.pallas_call(backward_kernel, out_shape=(S((ROWS, 512), bf), S((ROWS, 5...]
    unnamed x8 -> x0, local copies, waits for them, and re-layouts: 3.86 us -> none
where the time goes in v5:
time: 263 us; the launch traced here: 262 us
  Pallas kernels  259 us (98%)
    pallas_call x1, Pallas kernels, forward_call(): pl.pallas_call(forward_kernel, out_shape=(S((2, ROWS, 512), bf), S((2, RO...  126 us
    pallas_call x1, Pallas kernels, backward_call(): pl.pallas_call(backward_kernel, out_shape=(S((ROWS, 512), bf), S((ROWS, 5...  117 us
    pallas_call x1, Pallas kernels, place_call(): pl.pallas_call(place_kernel, out_shape=(S((SEQ, 2048, 512), bf), S((SEQ,...  15.6 us

profile of v5, /device:TPU:0, one launch (start us, length us, event | category | flops | bytes accessed | tf_op | source)
XLA Modules:
  0.0 262.5 jit_solution(15172244746708010815)
XLA Ops:
  0.7 0.7 fusion.5
  1.4 0.7 pad_select_fusion.tile_ref
  2.0 126.3 %forward.1 = (bf16[2,1024,512]{2,1,0:T(8,128)(2,1)}, bf16[2,1024,512]{2,1,0:T(8,128)(2,1)}, bf16[1024,1024]{1,0:T(8,128)(2,1)}, bf16[12,1024,128]{2,1,0:T(8,128)...) custom-call(s32[4,1,256]{2,1,0:T(1,128)} %spot_ref.3, ...), custom_call_target="tpu_custom_call" | custom-call | tf_op jit(solution)/shard_map/forward/pallas_call | solution.py:856
  128.3 117.0 %backward.1 = (bf16[1024,512]{1,0:T(8,128)(2,1)}, bf16[1024,512]{1,0:T(8,128)(2,1)}, f32[48,64,128]{2,1,0:T(8,128)}, f32[1,8,128]{2,1,0:T(8,128)}) custom-call(bf16[2,1024,512]{2,1,0:T(8,128)(2,1)} %get-tuple-element.35.rows, bf16[2,1024,512]{2,1,0:T(8,128)(2,1)} %get-tuple-element.36.cot, bf16[1024,1024]{1,0:T(8,128)(2,1)} %get-tuple-element.37.nT_in, ...), custom_call_target="tpu_custom_call" | custom-call | tf_op jit(solution)/shard_map/backward/pallas_call | solution.py:1246
  245.3 0.8 slice_select_fusion
  246.1 0.5 slice_bitcast_fusion
  246.7 15.6 %place_rows.1 = (bf16[4,2048,512]{2,1,0:T(8,128)(2,1)}, bf16[4,2048,512]{2,1,0:T(8,128)(2,1)}, f32[64,512]{1,0:T(8,128)}, f32[64,512]{1,0:T(8,128)}, f32[64,512]...) custom-call(s32[4,1,256]{2,1,0:T(1,128)} %spot_ref.3, ...), custom_call_target="tpu_custom_call" | custom-call | tf_op jit(solution)/shard_map/place_rows/pallas_call | solution.py:1399

commit v6 on v5

--- a/solution.py
+++ b/solution.py
@@ -196,13 +196,13 @@
 PER = 4
 GATHER_LAGS = {
     "X": (0, 3, 6, 9, 12, 19),
-    "Y": (0, 3, 7, 9, 13, 17),
-    "Z": (0, 3, 8, 11, 14, 17),
+    "Y": (0, 4, 7, 9, 13, 19),
+    "Z": (0, 5, 9, 12, 15, 19),
 }
 SCATTER_LAGS = {
-    "X": (0, 4, 8, 9, 13, 18),
-    "Y": (0, 5, 8, 9, 13, 18),
-    "Z": (0, 2, 5, 9, 13, 18),
+    "X": (0, 4, 7, 9, 13, 18),
+    "Y": (0, 4, 8, 10, 12, 17),
+    "Z": (0, 2, 5, 9, 14, 19),
 }
 VECTOR_STEPS = (0, 3, 6, 9, 12, 15)
 
@@ -224,7 +224,7 @@
     return jnp.logical_and(a, b)
 
 
-def barrier(p, core):
+def greet_all(p):
     bar = pltpu.get_barrier_semaphore()
 
     def greet(dev):
@@ -232,8 +232,7 @@
 
     greet({"dp": p.nx})
     greet({"dp": p.ny})
-    if core:
-        greet({"tensor": 1 - p.t})
+    greet({"tensor": 1 - p.t})
 
     @pl.when(p.z < 3)
     def _():
@@ -243,16 +242,18 @@
     def _():
         greet({"dp": p.dn})
 
+
+def await_all(p):
+    bar = pltpu.get_barrier_semaphore()
     inner = both(p.z > 0, p.z < 3)
-    base = 4 if core else 3
 
     @pl.when(inner)
     def _():
-        pl.semaphore_wait(bar, base + 1)
+        pl.semaphore_wait(bar, 5)
 
     @pl.when(jnp.logical_not(inner))
     def _():
-        pl.semaphore_wait(bar, base)
+        pl.semaphore_wait(bar, 4)
 
 
 class Steps:
@@ -594,6 +595,8 @@
     other = {"tensor": 1 - t}
     f32, bf = jnp.float32, jnp.bfloat16
 
+    greet_all(p)
+
     own = [pltpu.make_async_copy(tile_ref, own_slot(p, VB, 0), first.at[NB])]
     for b in range(16):
         src, col = ((wq, wk, wv)[b % 3], b // 3) if b < 12 else (wo, b - 12)
@@ -617,7 +620,7 @@
 
     loader(0, 0).start()
     loader(0, 1).start()
-    barrier(p, True)
+    await_all(p)
     for c in own:
         c.wait()
     W_steps = Gather(p, W, ss, rs)
@@ -669,7 +672,9 @@
 
     for z in range(4):
         for y in range(2):
-            vecs[:, pl.ds((z * 2 + y) * 128, 128)] = VB[0, z, y, 0] + VB[0, z, y, 1]
+            vecs[:, pl.ds((z * 2 + y) * 128, 128)] = VB[0, z, y, 0] + pltpu.roll(
+                VB[0, z, y, 1], 64, 1
+            )
 
     def saver(k, src, dst):
         return pltpu.make_async_copy(src, dst, outs.at[k])
@@ -713,12 +718,15 @@
         mixed[hp, r_, :] = jnp.where(low_half, mix[0], mix[1]).astype(bf)
 
     def pair_part(hp, _):
+        W_steps.step(20 + 4 * hp, 0)
+        W_steps.step(21 + 4 * hp, 1)
         y = dot(nrm[...], wblocks(W, 3 * hp, 3)).astype(bf)
         for c in range(3):
             qkv[3 * hp + c] = y[:, c * 128 : c * 128 + 128]
         for i in range(SEQ):
-            W_steps.step(20 + 4 * hp + i, i)
             attend(i, hp)
+            if i in (0, 2):
+                W_steps.step(22 + 4 * hp + i // 2, 2 + i // 2)
         return 0
 
     lax.fori_loop(0, 4, pair_part, 0)
@@ -784,6 +792,11 @@
     def g_copy(m):
         slot = lax.rem(m, 2)
         return pltpu.make_async_copy(Gst.at[slot], o_G.at[pl.ds(m * 4, 4)], gout.at[slot])
+
+    partials = [
+        saver(9 + n, tokbuf.at[n // 2, pl.ds(n % 2 * 1024, 1024)], (o_down, o_back)[n // 2].at[n % 2])
+        for n in range(4)
+    ]
 
     def mlp_part(m, _):
         slot = lax.rem(m, 2)
@@ -810,6 +823,13 @@
         W_steps.step(s + 3, 3, high=True)
         W_steps.drain(m, m + 1)
 
+        @pl.when(m == 7)
+        def _():
+            for n, c in enumerate(partials):
+                piece = (dacc, nacc)[n // 2][:, n % 2 * 512 : n % 2 * 512 + 512]
+                tokbuf[n // 2, pl.ds(n % 2 * 1024, 1024), :] = piece.astype(bf)
+                c.start()
+
         @pl.when(m >= 2)
         def _():
             g_copy(m - 2).wait()
@@ -826,13 +846,7 @@
         return 0
 
     lax.fori_loop(0, 8, mlp_part, 0)
-    for e in range(2):
-        for c in range(2):
-            tokbuf[e, pl.ds(c * 1024, 1024), :] = (dacc, nacc)[e][:, c * 512 : c * 512 + 512].astype(bf)
-            saved.append(
-                saver(9 + 2 * e + c, tokbuf.at[e, pl.ds(c * 1024, 1024)], (o_down, o_back)[e].at[c])
-            )
-            saved[-1].start()
+    saved += partials
     for i in range(SEQ):
         half_copy(i, 0).wait_send()
         half_copy(i, 1).wait_send()
@@ -927,8 +941,9 @@
     vec_in,
     o_newr,
     o_newg,
+    sum_out,
+    o_vec,
     o_sum,
-    o_vec,
     G,
     Wa,
     qkv,
@@ -964,6 +979,7 @@
     other = {"tensor": 1 - t}
     f32, bf = jnp.float32, jnp.bfloat16
     wide, small = landing[:8], landing[8:]
+    greet_all(p)
 
     def g_load(c):
         return pltpu.make_async_copy(G_in.at[pl.ds(4 * c, 4)], G.at[pl.ds(4 * c, 4)], gsem.at[c])
@@ -995,7 +1011,7 @@
     ]
     for c in fixed[:3]:
         c.start()
-    barrier(p, True)
+    await_all(p)
 
     def pair_copy(s, e):
         return pltpu.make_async_remote_copy(
@@ -1212,20 +1228,27 @@
                 0,
             )
             GV[0, z, y, 0] = tile
-            GV[0, z, y, 1] = tile
+            GV[0, z, y, 1] = pltpu.roll(tile, 64, 1)
     for s in range(SEQ):
         back_copy(s).wait_send()
     row_outs.append(pltpu.make_async_copy(newg, o_newg, tout.at[1]))
     row_outs[1].start()
     v_steps.send(0, 0, 0)
 
+    def sum_copy(e):
+        part = pl.ds(32, 16) if e else pl.ds(0, 32)
+        return pltpu.make_async_copy(o_sum.at[part], sum_out.at[part], tout.at[2 + e])
+
     for k, s in enumerate(range(53, 67)):
         steps.step(s, s % PER, static=s)
+        if s == 53:
+            sum_copy(0).start()
         if k in (0, 2, 3, 5, 7):
             j = (0, 2, 3, 5, 7).index(k) + 1
             v_steps.recv(0, 0, j - 1)
             if j < 5:
                 v_steps.send(0, 0, j)
+    sum_copy(1).start()
     for c in row_outs:
         c.wait()
     for s in range(SEQ):
@@ -1234,6 +1257,8 @@
     for j in range(5):
         v_steps.send(0, 0, j, act=lambda d: d.wait_send())
     steps.drain(8, NB // PER)
+    sum_copy(0).wait()
+    sum_copy(1).wait()
 
 
 def backward_call(kept):
@@ -1252,8 +1277,9 @@
             S((1, 8, 128), f32),
         ),
         in_specs=[any_] * 12,
-        out_specs=[any_, any_, vspec, vspec],
+        out_specs=[any_, any_, any_, vspec],
         scratch_shapes=[
+            vm((NB, 64, 128), f32),
             vm((NB, 4, 2, 2, 64, 128), bf),
             vm((16, 4, 2, 2, 64, 128), bf),
             vm((12, ROWS, 128), bf),
@@ -1281,7 +1307,7 @@
             DMA((4, 2)),
             DMA((4,)),
             DMA((4,)),
-            DMA((2,)),
+            DMA((4,)),
         ]
         + Scatter.landing(NB, (64, 128), bf)
         + Scatter.landing(PER, (8, 128), f32),
@@ -1427,10 +1453,7 @@
 
 def to_tile(w_route, gain_attn, gain_mlp):
     v = jnp.stack([w_route, gain_attn, gain_mlp]).astype(jnp.float32)
-    v = jnp.pad(v, ((0, 5), (0, 0)))
-    z = jnp.zeros_like(v)
-    odd = lax.axis_index("dp") % 2
-    return jnp.where(odd == 0, jnp.concatenate([v, z], 1), jnp.concatenate([z, v], 1))
+    return jnp.pad(v, ((0, 5), (0, 64)))
 
 
 def fused(
@@ -1455,8 +1478,7 @@
     kept = list(forward_call(spot, tile, tok, cot, weights))
     kept[10] = kept[10].reshape(32, 4, 2, 2, 64, 128)
     newr, newg, own, vec = backward_call(kept)
-    odd = lax.axis_index("dp") % 2
-    vec = jnp.where(odd == 0, vec[0, :3, :64], vec[0, :3, 64:])
+    vec = vec[0, :3, :64]
     output, grad, g_q, g_k, g_v, g_out, g_up, g_down = place_call(
         spot, own, newr, newg, tok, cot
     )

time: 263 us -> 260 us (0.989)
  Pallas kernels: 259 us -> 256 us
where the time goes in v6:
time: 260 us
  Pallas kernels  256 us (98%)
    pallas_call x1, Pallas kernels, forward_call(): pl.pallas_call(forward_kernel, out_shape=(S((2, ROWS, 512), bf), S((2, RO...  124 us
    pallas_call x1, Pallas kernels, backward_call(): pl.pallas_call(backward_kernel, out_shape=(S((ROWS, 512), bf), S((ROWS, 5...  117 us
    pallas_call x1, Pallas kernels, place_call(): pl.pallas_call(place_kernel, out_shape=(S((SEQ, 2048, 512), bf), S((SEQ,...  15.6 us

profile of v6, /device:TPU:0, one launch (start us, length us, event | category | flops | bytes accessed | tf_op | source)
XLA Modules:
  0.0 259.7 jit_solution(17448631214192241296)
XLA Ops:
  0.6 1.3 fusion.9.tile_ref
  1.9 123.9 %forward.1 = (bf16[2,1024,512]{2,1,0:T(8,128)(2,1)}, bf16[2,1024,512]{2,1,0:T(8,128)(2,1)}, bf16[1024,1024]{1,0:T(8,128)(2,1)}, bf16[12,1024,128]{2,1,0:T(8,128)...) custom-call(s32[4,1,256]{2,1,0:T(1,128)} %spot_ref.3, ...), custom_call_target="tpu_custom_call" | custom-call | tf_op jit(solution)/shard_map/forward/pallas_call | solution.py:870
  125.8 116.7 %backward.1 = (bf16[1024,512]{1,0:T(8,128)(2,1)}, bf16[1024,512]{1,0:T(8,128)(2,1)}, f32[48,64,128]{2,1,0:T(8,128)}, f32[1,8,128]{2,1,0:T(8,128)}) custom-call(bf16[2,1024,512]{2,1,0:T(8,128)(2,1)} %get-tuple-element.35.rows, bf16[2,1024,512]{2,1,0:T(8,128)(2,1)} %get-tuple-element.36.cot, bf16[1024,1024]{1,0:T(8,128)(2,1)} %get-tuple-element.37.nT_in, ...), custom_call_target="tpu_custom_call" | custom-call | tf_op jit(solution)/shard_map/backward/pallas_call | solution.py:1271
  242.5 1.3 slice_bitcast_fusion
  243.9 15.6 %place_rows.1 = (bf16[4,2048,512]{2,1,0:T(8,128)(2,1)}, bf16[4,2048,512]{2,1,0:T(8,128)(2,1)}, f32[64,512]{1,0:T(8,128)}, f32[64,512]{1,0:T(8,128)}, f32[64,512]...) custom-call(s32[4,1,256]{2,1,0:T(1,128)} %spot_ref.3, ...), custom_call_target="tpu_custom_call" | custom-call | tf_op jit(solution)/shard_map/place_rows/pallas_call | solution.py:1425

commit v7 on v6

--- a/solution.py
+++ b/solution.py
@@ -276,10 +276,15 @@
                 act(b, q, j)
 
         for j, lag, q in live:
+            if j == 0:
+                do(j, lag, q, self.send)
+        for j, lag, q in live:
             if j > 0:
                 do(j, lag, q, lambda b, q, j: self.recv(b, q, j - 1))
+            if self.relay and 0 < j < 5:
+                do(j, lag, q, self.send)
         for j, lag, q in live:
-            if j < 5:
+            if not self.relay and 0 < j < 5:
                 do(j, lag, q, self.send)
 
     def drain(self, first, last):
@@ -294,6 +299,7 @@
 
 class Gather(Steps):
     lags = GATHER_LAGS
+    relay = True
 
     def __init__(self, p, W, ss, rs):
         self.p, self.W, self.ss, self.rs = p, W, ss, rs
@@ -360,6 +366,7 @@
 
 class Scatter(Steps):
     lags = SCATTER_LAGS
+    relay = False
 
     def __init__(self, p, G, out, L8, L4, LZ, P4, P2, P1, ss, rs):
         self.p, self.G, self.out, self.ss, self.rs = p, G, out, ss, rs
@@ -1413,7 +1420,7 @@
         c.wait()
 
 
-SIZE = 1024
+SIZE = 2048
 
 
 def place_call(spot, own, newr, newg, tok, cotangent):

time: 260 us -> 259 us (level)
  no operation moved by 1% of the time
where the time goes in v7:
time: 259 us
  Pallas kernels  255 us (98%)
    pallas_call x1, Pallas kernels, forward_call(): pl.pallas_call(forward_kernel, out_shape=(S((2, ROWS, 512), bf), S((2, RO...  124 us
    pallas_call x1, Pallas kernels, backward_call(): pl.pallas_call(backward_kernel, out_shape=(S((ROWS, 512), bf), S((ROWS, 5...  116 us
    pallas_call x1, Pallas kernels, place_call(): pl.pallas_call(place_kernel, out_shape=(S((SEQ, 2048, 512), bf), S((SEQ,...  15 us

profile of v7, /device:TPU:0, one launch (start us, length us, event | category | flops | bytes accessed | tf_op | source)
XLA Modules:
  0.0 258.7 jit_solution(10348780731210567046)
XLA Ops:
  0.6 1.3 fusion.9.tile_ref
  1.9 124.0 %forward.1 = (bf16[2,1024,512]{2,1,0:T(8,128)(2,1)}, bf16[2,1024,512]{2,1,0:T(8,128)(2,1)}, bf16[1024,1024]{1,0:T(8,128)(2,1)}, bf16[12,1024,128]{2,1,0:T(8,128)...) custom-call(s32[4,1,256]{2,1,0:T(1,128)} %spot_ref.3, ...), custom_call_target="tpu_custom_call" | custom-call | tf_op jit(solution)/shard_map/forward/pallas_call | solution.py:877
  125.9 116.2 %backward.1 = (bf16[1024,512]{1,0:T(8,128)(2,1)}, bf16[1024,512]{1,0:T(8,128)(2,1)}, f32[48,64,128]{2,1,0:T(8,128)}, f32[1,8,128]{2,1,0:T(8,128)}) custom-call(bf16[2,1024,512]{2,1,0:T(8,128)(2,1)} %get-tuple-element.35.rows, bf16[2,1024,512]{2,1,0:T(8,128)(2,1)} %get-tuple-element.36.cot, bf16[1024,1024]{1,0:T(8,128)(2,1)} %get-tuple-element.37.nT_in, ...), custom_call_target="tpu_custom_call" | custom-call | tf_op jit(solution)/shard_map/backward/pallas_call | solution.py:1278
  242.2 1.3 slice_bitcast_fusion
  243.5 15.0 %place_rows.1 = (bf16[4,2048,512]{2,1,0:T(8,128)(2,1)}, bf16[4,2048,512]{2,1,0:T(8,128)(2,1)}, f32[64,512]{1,0:T(8,128)}, f32[64,512]{1,0:T(8,128)}, f32[64,512]...) custom-call(s32[4,1,256]{2,1,0:T(1,128)} %spot_ref.3, ...), custom_call_target="tpu_custom_call" | custom-call | tf_op jit(solution)/shard_map/place_rows/pallas_call | solution.py:1432

commit v8 on v7

--- a/solution.py
+++ b/solution.py
@@ -1327,6 +1327,7 @@
 
 def place_kernel(
     spot_ref,
+    vec_ref,
     own_ref,
     newr,
     newg,
@@ -1340,6 +1341,9 @@
     g_out,
     g_up,
     g_down,
+    g_route,
+    g_attn,
+    g_mlp,
     old,
     out,
     new,
@@ -1350,6 +1354,8 @@
     gsem,
 ):
     bf = jnp.bfloat16
+    for k, ref in enumerate((g_route, g_attn, g_mlp)):
+        ref[...] = vec_ref[0, k, :64]
 
     def piece(n):
         return n // (2048 // SIZE), cut(n % (2048 // SIZE), SIZE)
@@ -1423,11 +1429,12 @@
 SIZE = 2048
 
 
-def place_call(spot, own, newr, newg, tok, cotangent):
+def place_call(spot, vec, own, newr, newg, tok, cotangent):
     bf, f32 = jnp.bfloat16, jnp.float32
     S = jax.ShapeDtypeStruct
     DMA = pltpu.SemaphoreType.DMA
     any_ = pl.BlockSpec(memory_space=pltpu.MemorySpace.HBM)
+    vspec = pl.BlockSpec(memory_space=pltpu.VMEM)
     pieces = SEQ * 2048 // SIZE
     return pl.pallas_call(
         place_kernel,
@@ -1440,9 +1447,12 @@
             S((64, 512), f32),
             S((64, 2048), f32),
             S((64, 2048), f32),
+            S((64,), f32),
+            S((64,), f32),
+            S((64,), f32),
         ),
-        in_specs=[pl.BlockSpec(memory_space=pltpu.VMEM)] + [any_] * 5,
-        out_specs=[any_] * 8,
+        in_specs=[vspec, vspec] + [any_] * 5,
+        out_specs=[any_] * 8 + [vspec] * 3,
         scratch_shapes=[
             pltpu.VMEM((2, pieces, SIZE, 512), bf),
             pltpu.VMEM((2, pieces, SIZE, 512), bf),
@@ -1455,7 +1465,7 @@
         ],
         compiler_params=pltpu.CompilerParams(vmem_limit_bytes=63 * 1024 * 1024),
         name="place_rows",
-    )(spot, own, newr, newg, tok, cotangent)
+    )(spot, vec, own, newr, newg, tok, cotangent)
 
 
 def to_tile(w_route, gain_attn, gain_mlp):
@@ -1485,9 +1495,8 @@
     kept = list(forward_call(spot, tile, tok, cot, weights))
     kept[10] = kept[10].reshape(32, 4, 2, 2, 64, 128)
     newr, newg, own, vec = backward_call(kept)
-    vec = vec[0, :3, :64]
-    output, grad, g_q, g_k, g_v, g_out, g_up, g_down = place_call(
-        spot, own, newr, newg, tok, cot
+    output, grad, g_q, g_k, g_v, g_out, g_up, g_down, *g_vec = place_call(
+        spot, vec, own, newr, newg, tok, cot
     )
     return (
         output.reshape(tokens.shape),
@@ -1498,9 +1507,7 @@
         g_out.T,
         g_up,
         g_down.T,
-        vec[0],
-        vec[1],
-        vec[2],
+        *g_vec,
     )
 
 

time: 259 us -> 258 us (level)
  no operation moved by 1% of the time
where the time goes in v8:
time: 258 us
  Pallas kernels  256 us (99%)
    pallas_call x1, Pallas kernels, forward_call(): pl.pallas_call(forward_kernel, out_shape=(S((2, ROWS, 512), bf), S((2, RO...  124 us
    pallas_call x1, Pallas kernels, backward_call(): pl.pallas_call(backward_kernel, out_shape=(S((ROWS, 512), bf), S((ROWS, 5...  116 us
    pallas_call x1, Pallas kernels, place_call(): pl.pallas_call(place_kernel, out_shape=(S((SEQ, 2048, 512), bf), S((SEQ,...  15.6 us

profile of v8, /device:TPU:0, one launch (start us, length us, event | category | flops | bytes accessed | tf_op | source)
XLA Modules:
  0.0 258.0 jit_solution(844547008246236622)
XLA Ops:
  0.6 1.3 fusion.9.tile_ref
  1.9 124.0 %forward.1 = (bf16[2,1024,512]{2,1,0:T(8,128)(2,1)}, bf16[2,1024,512]{2,1,0:T(8,128)(2,1)}, bf16[1024,1024]{1,0:T(8,128)(2,1)}, bf16[12,1024,128]{2,1,0:T(8,128)...) custom-call(s32[4,1,256]{2,1,0:T(1,128)} %spot_ref.3, ...), custom_call_target="tpu_custom_call" | custom-call | tf_op jit(solution)/shard_map/forward/pallas_call | solution.py:877
  125.9 116.2 %backward.1 = (bf16[1024,512]{1,0:T(8,128)(2,1)}, bf16[1024,512]{1,0:T(8,128)(2,1)}, f32[48,64,128]{2,1,0:T(8,128)}, f32[1,8,128]{2,1,0:T(8,128)}) custom-call(bf16[2,1024,512]{2,1,0:T(8,128)(2,1)} %get-tuple-element.38.rows, bf16[2,1024,512]{2,1,0:T(8,128)(2,1)} %get-tuple-element.39.cot, bf16[1024,1024]{1,0:T(8,128)(2,1)} %get-tuple-element.40.nT_in, ...), custom_call_target="tpu_custom_call" | custom-call | tf_op jit(solution)/shard_map/backward/pallas_call | solution.py:1278
  242.2 15.6 %place_rows.1 = (bf16[4,2048,512]{2,1,0:T(8,128)(2,1)}, bf16[4,2048,512]{2,1,0:T(8,128)(2,1)}, f32[64,512]{1,0:T(8,128)}, f32[64,512]{1,0:T(8,128)}, f32[64,512]...) custom-call(s32[4,1,256]{2,1,0:T(1,128)} %spot_ref.3, ...), custom_call_target="tpu_custom_call" | custom-call | tf_op jit(solution)/shard_map/place_rows/pallas_call | solution.py:1439
